TPU v7x, 128 devices: a whole 4x4x4 slice. The times are simulated.
128 devices in a mesh: corpus: 32 (over y, z, core), query: 4 (over x).
Axes of the slice: x: 4, y: 4, z: 4, core: 2. Of those that a mesh axis runs over, the one named last changes fastest.
Arguments:
- queries: bfloat16 [32768, 768], P(('corpus', 'query')), may hold values from -8 to 8
- probes: int32 [32768, 4], P(('corpus', 'query')), may hold values from 0 to 1023, as said below
- targets: int32 [32768, 8], P(('corpus', 'query')), may hold values from 0 to 4095, all different within a row
- passage_codes: int32 [1024, 96, 1024], P('corpus'), may hold values from 0 to 15
- codebook: float32 [16, 768], replicated, may hold values from -6 to 6
Outputs:
- grad_queries: bfloat16 [32768, 768], P(('corpus', 'query'))
- codebook_step: float32 [16, 768], replicated
Inputs may be any that keep to these rules, and one draw needn't show every extreme that they name: `probes`: each row names 4 different lists; list l belongs to index l // 32 of corpus. In every aligned block of 256 rows (the rows of one device) no list is named more than 2 times, and one list, the same one in every block, is named exactly 2 times. `targets`: each row names 8 different candidates; column r holds the candidate of rank r.
All inputs are finite; a program needn't handle non-finite values.
Results may differ from a plain program's by a relative error of at most 0.01.
The roundings to bfloat16 on the way count: a program that leaves them out, or rounds other values in their place, can miss the bound.
Values may be sent and summed in bfloat16 or wider, within the bound.
No kernel may reach another device: no remote copies, remote signals or barrier semaphores. Data moves between devices by JAX's collectives and lax.ppermute only.
A program may use at most 192 MiB of HBM per device.

v0:
```python
import jax
import jax.numpy as jnp
from jax import lax
from jax.sharding import PartitionSpec as P

D = 768
SUBSPACES = 96
CENTROIDS = 16
SUBDIM = 8
PASSAGES = 1024
PROBES = 4
TARGETS = 8


NEGATIVE = -1e30
EPSILON = 1e-06


def rank_weights():
    levels = jnp.arange(TARGETS, dtype=jnp.int32).astype(jnp.float32)
    return 2.0 * (TARGETS - levels) / (TARGETS * (TARGETS + 1.0))


def rank_slots(list_keys, key_count, keep):
    key_ids = jnp.arange(key_count, dtype=jnp.int32)
    marked = ((list_keys[:, None] == key_ids[None, :]) & keep[:, None]).astype(jnp.int32)
    running = jnp.cumsum(marked, axis=0)
    return jnp.sum(marked * running, axis=1) - 1


def note_block(probes, targets):
    row_count = probes.shape[0]
    probe_cols = jnp.arange(PROBES, dtype=jnp.int32)
    inside = targets[:, None, :] // PASSAGES == probe_cols[None, :, None]
    target_spot = jnp.where(inside, targets[:, None, :] % PASSAGES, -1)
    query_ids = jnp.broadcast_to(
        jnp.arange(row_count, dtype=jnp.int32)[:, None, None], (row_count, PROBES, 1)
    )
    return jnp.concatenate([query_ids, target_spot], axis=2).reshape(
        row_count * PROBES, TARGETS + 1
    )


def lookup_rows(rows_block, codebook):
    lead_shape = rows_block.shape[:-1]
    split_rows = rows_block.astype(jnp.float32).reshape(lead_shape + (SUBSPACES, SUBDIM))
    centroids = codebook.reshape(CENTROIDS, SUBSPACES, SUBDIM)
    lut_rows = jnp.einsum(
        "...me,kme->...mk", split_rows, centroids, precision=lax.Precision.HIGHEST
    )
    return lut_rows.reshape(lead_shape + (SUBSPACES * CENTROIDS,)).astype(jnp.bfloat16)


def code_one_hot(code_block):
    levels = jnp.arange(CENTROIDS, dtype=jnp.int32)
    marked = code_block[:, :, None, :] == levels[None, None, :, None]
    return marked.astype(jnp.bfloat16).reshape(
        code_block.shape[0], SUBSPACES * CENTROIDS, code_block.shape[2]
    )


def group_size(lists_dev, slot_rows):
    group_width = 1
    while (
        group_width * 2 <= lists_dev
        and lists_dev % (group_width * 2) == 0
        and (group_width * slot_rows < 512)
    ):
        group_width = group_width * 2
    return group_width


def first_pass(got_rows, passage_codes, codebook, group_width):
    lists_dev, slot_rows = (got_rows.shape[0], got_rows.shape[1])
    groups = lists_dev // group_width

    def score_piece(pieces):
        row_group, code_group = pieces
        lut_rows = lookup_rows(row_group, codebook)
        one_hot = code_one_hot(code_group)
        scores = jnp.einsum("grk,gkl->grl", lut_rows, one_hot, preferred_element_type=jnp.float32)
        top_score = jnp.max(scores, axis=2)
        exp_total = jnp.sum(jnp.exp(scores - top_score[:, :, None]), axis=2)
        return (scores, top_score, exp_total)

    scores, top_score, exp_total = lax.map(
        score_piece,
        (
            got_rows.reshape(groups, group_width, slot_rows, D),
            passage_codes.reshape(groups, group_width, SUBSPACES, PASSAGES),
        ),
    )
    return (
        scores.reshape(lists_dev, slot_rows, PASSAGES),
        top_score.reshape(lists_dev, slot_rows),
        exp_total.reshape(lists_dev, slot_rows),
    )


def second_pass(
    got_rows, got_notes, passage_codes, codebook, scores, query_top, query_total, group_width
):
    lists_dev, slot_rows = (got_rows.shape[0], got_rows.shape[1])
    groups = lists_dev // group_width
    weights = rank_weights()
    places = jnp.arange(PASSAGES, dtype=jnp.int32)
    centroids = codebook.reshape(CENTROIDS, SUBSPACES, SUBDIM)
    highest = lax.Precision.HIGHEST

    def grad_piece(pieces):
        row_group, note_group, code_group, score_group, top_group, total_group = pieces
        one_hot = code_one_hot(code_group)
        target_spot = note_group[:, :, 1:]
        teacher = jnp.sum(
            jnp.where(target_spot[:, :, :, None] == places, weights[:, None], 0.0), axis=2
        )
        student = jnp.exp(score_group - top_group[:, :, None]) / total_group[:, :, None]
        is_valid = note_group[:, :, 0] >= 0
        grad_scores = jnp.where(is_valid[:, :, None], student - teacher, 0.0).astype(jnp.bfloat16)
        histogram = jnp.einsum(
            "grl,gkl->grk", grad_scores, one_hot, preferred_element_type=jnp.float32
        )
        histogram = histogram.reshape(group_width, slot_rows, SUBSPACES, CENTROIDS)
        partial_value = jnp.einsum("grmk,kme->grme", histogram, centroids, precision=highest)
        split_rows = row_group.astype(jnp.float32).reshape(
            group_width, slot_rows, SUBSPACES, SUBDIM
        )
        book_part = jnp.einsum("grmk,grme->kme", histogram, split_rows, precision=highest)
        return (partial_value.reshape(group_width, slot_rows, D), book_part)

    partial_value, book_part = lax.map(
        grad_piece,
        (
            got_rows.reshape(groups, group_width, slot_rows, D),
            got_notes.reshape(groups, group_width, slot_rows, TARGETS + 1),
            passage_codes.reshape(groups, group_width, SUBSPACES, PASSAGES),
            scores.reshape(groups, group_width, slot_rows, PASSAGES),
            query_top.reshape(groups, group_width, slot_rows),
            query_total.reshape(groups, group_width, slot_rows),
        ),
    )
    return (
        partial_value.reshape(lists_dev, slot_rows, D),
        jnp.sum(book_part, axis=0).reshape(CENTROIDS, D),
    )


def shards(queries, probes, targets, passage_codes, codebook):
    corpus_size = lax.axis_size("corpus")
    query_rows = queries.shape[0]
    lists_dev = passage_codes.shape[0]
    list_total = lists_dev * corpus_size
    capacity = min(query_rows, max(2, 2 * PROBES * query_rows // list_total))
    slot_rows = corpus_size * capacity
    slot_count = lists_dev * slot_rows
    group_width = group_size(lists_dev, slot_rows)
    flat_probes = probes.reshape(-1)
    local_list = flat_probes % lists_dev
    owner_ids = flat_probes // lists_dev
    slot_rank = rank_slots(flat_probes, list_total, jnp.ones(flat_probes.shape, jnp.bool_))
    note_rows = note_block(probes, targets)
    placed = (local_list * corpus_size + owner_ids) * capacity + slot_rank
    sending = (
        jnp.zeros((slot_count, D), jnp.bfloat16).at[placed].set(jnp.repeat(queries, PROBES, axis=0))
    )
    note_buffer = jnp.full((slot_count, TARGETS + 1), -1, jnp.int32).at[placed].set(note_rows)
    got_rows, got_notes = (
        lax.all_to_all(
            sending.reshape(lists_dev, corpus_size, capacity, D),
            "corpus",
            split_axis=1,
            concat_axis=1,
            tiled=True,
        ),
        lax.all_to_all(
            note_buffer.reshape(lists_dev, corpus_size, capacity, TARGETS + 1),
            "corpus",
            split_axis=1,
            concat_axis=1,
            tiled=True,
        ),
    )
    got_rows = got_rows.reshape(lists_dev, slot_rows, D)
    got_notes = got_notes.reshape(lists_dev, slot_rows, TARGETS + 1)
    is_valid = got_notes[:, :, 0] >= 0
    scores, top_score, exp_total = first_pass(got_rows, passage_codes, codebook, group_width)
    top_score = jnp.where(is_valid, top_score, NEGATIVE)
    exp_total = jnp.where(is_valid, exp_total, 0.0)
    back_top, back_total = (
        lax.all_to_all(
            top_score.reshape(lists_dev, corpus_size, capacity),
            "corpus",
            split_axis=1,
            concat_axis=1,
            tiled=True,
        ),
        lax.all_to_all(
            exp_total.reshape(lists_dev, corpus_size, capacity),
            "corpus",
            split_axis=1,
            concat_axis=1,
            tiled=True,
        ),
    )
    entry_top = back_top.reshape(-1)[placed].reshape(query_rows, PROBES)
    entry_total = back_total.reshape(-1)[placed].reshape(query_rows, PROBES)
    own_top = jnp.max(entry_top, axis=1)
    own_total = jnp.sum(entry_total * jnp.exp(entry_top - own_top[:, None]), axis=1)
    slot_top = jnp.zeros((slot_count,), jnp.float32).at[placed].set(jnp.repeat(own_top, PROBES))
    slot_total = jnp.ones((slot_count,), jnp.float32).at[placed].set(jnp.repeat(own_total, PROBES))
    query_top, query_total = (
        lax.all_to_all(
            slot_top.reshape(lists_dev, corpus_size, capacity),
            "corpus",
            split_axis=1,
            concat_axis=1,
            tiled=True,
        ),
        lax.all_to_all(
            slot_total.reshape(lists_dev, corpus_size, capacity),
            "corpus",
            split_axis=1,
            concat_axis=1,
            tiled=True,
        ),
    )
    query_top = query_top.reshape(lists_dev, slot_rows)
    query_total = query_total.reshape(lists_dev, slot_rows)
    query_top = jnp.where(is_valid, query_top, 0.0)
    query_total = jnp.where(is_valid, query_total, 1.0)
    partial_value, book_part = second_pass(
        got_rows, got_notes, passage_codes, codebook, scores, query_top, query_total, group_width
    )
    returned = lax.all_to_all(
        partial_value.reshape(lists_dev, corpus_size, capacity, D),
        "corpus",
        split_axis=1,
        concat_axis=1,
        tiled=True,
    )
    per_probe = returned.reshape(slot_count, D)[placed].reshape(query_rows, PROBES, D)
    grad_queries = jnp.sum(per_probe, axis=1)
    book_sum = lax.psum(book_part, ("corpus", "query"))
    normed = book_sum * lax.rsqrt(jnp.mean(book_sum * book_sum) + EPSILON)
    return (grad_queries.astype(jnp.bfloat16), normed)


def solution(mesh):
    placed = (
        P(("corpus", "query"), None),
        P(("corpus", "query"), None),
        P(("corpus", "query"), None),
        P("corpus", None, None),
        P(),
    )
    return jax.shard_map(
        shards,
        mesh=mesh,
        in_specs=placed,
        out_specs=(P(("corpus", "query"), None), P()),
        check_vma=False,
    )
```

profile of v0, /device:TPU:1, one launch (start us, length us, event | category | flops | bytes accessed | tf_op | source)
XLA Modules:
  0.0 697.2 jit_solution(16750538512104853884)
XLA Ops:
  16.7 9.6 %all-to-all-start = ((s32[32,1,576]{2,1,0:T(1,128)}), s32[32,1,576]{2,1,0:T(1,128)S(1)}, u32[]{:S(2)}, u32[]{:S(2)}) async-start(s32[32,1,576]{2,1,0:T(1,128)} %reshape.393), calls=%async_computation | async-start | bytes 163840 | tf_op jit(solution)/shard_map/all_to_all | solution.py:175
  28.1 7.1 %scatter_custom_fusion.1 = bf16[2048,768]{1,0:T(8,128)(2,1)S(1)} fusion(s32[1024]{0:T(1024)S(1)} %bitcast.179, bf16[1024,768]{1,0:T(8,128)(2,1)} %reshape.360, bf16[]{:T(256)} %constant.118.clone.1), kind=kCustom, calls=%fused_computation.62 | custom fusion | bytes 3146240 | tf_op jit(solution)/shard_map/scatter | solution.py:164
  37.9 6.8 copy.136
  44.7 7.4 %all-to-all-start.1 = ((bf16[32,32,2,768]{3,2,0,1:T(2,128)(2,1)}), bf16[32,32,2,768]{3,2,0,1:T(2,128)(2,1)S(1)}, u32[]{:S(2)}, u32[]{:S(2)}) async-start(bf16[32,32,2,768]{3,2,0,1:T(2,128)(2,1)} %copy.136), calls=%async_computation.1 | async-start | bytes 6291456 | tf_op jit(solution)/shard_map/all_to_all | solution.py:168
  60.2 31.6 %all-to-all-done.1 = bf16[32,32,2,768]{3,2,0,1:T(2,128)(2,1)S(1)} async-done(((bf16[32,32,2,768]{3,2,0,1:T(2,128)(2,1)}), bf16[32,32,2,768]{3,2,0,1:T(2,128)(2,1)S(1)}, u32[]{:S(2)}, u32[]{:S(2)}) %all-to-all-start.1) | async-done | bytes 3145760 | tf_op jit(solution)/shard_map/all_to_all | solution.py:168
  94.2 7.3 %copy.138 = bf16[4,8,64,768]{2,3,1,0:T(8,128)(2,1)} copy(bf16[4,8,64,768]{3,1,0,2:T(8,128)(2,1)} %bitcast.169) | data formatting | bytes 6291456 | tf_op jit(solution)/shard_map/while | solution.py:86
  102.7 129.6 %while.27 = (s32[]{:T(128)}, f32[4,8,64,1024]{3,2,1,0:T(8,128)}, f32[4,8,64]{2,1,0:T(8,128)}, f32[4,8,64]{2,1,0:T(8,128)}, bf16[4,8,64,768]{2,3,1,0:T(8,128)(2,1...) while((s32[]{:T(128)}, f32[4,8,64,1024]{3,2,1,0:T(8,128)}, ...), condition=%wide.region_8.9_spmd, body=%wide.region_5.8_spmd.sunk | while | flops 1701051392 | bytes 57241216 | solution.py:86
  112.8 9.4 %bitcast_compare_fusion.4 = pred[8,1536,1024]{2,1,0:T(32,128)(4,1)} fusion(s32[1536]{0:T(1024)S(1)} %eq.177, s32[8,96,1024]{2,1,0:T(8,128)S(1)} %dynamic-slice_bitcast_fusion.14), kind=kLoop, calls=%fused_computation.9.clone.1 | loop fusion | flops 12582912 | bytes 15734784 | tf_op jit(solution)/shard_map/while/body/eval_jaxpr/eq | solution.py:56
  122.1 11.7 %bitcast_dynamic-update-slice_fusion.5 = (f32[4,8,64,1024]{3,2,1,0:T(8,128)}, f32[8,64,1024]{2,1,0:T(8,128)S(1)}) fusion(f32[4,8,64,1024]{3,2,1,0:T(8,128)} %get-tuple-element.387, s32[]{:T(128)} %get-tuple-element.386, bf16[8,64,1536]{1,2,0:T(8,128)(2,1)S(1)} %bitcast.165, pred[8,1536,1024]{2,1,0:T(32,128)(4,1)} %bitcast_compare_fusion.4), kind=kOutput, calls=%fused_computation.12.clone.1 | convolution fusion | flops 1610612736 | bytes 18350592 | tf_op jit(solution)/shard_map/while/body/eval_jaxpr/grk,gkl->grl/dot_general | solution.py:81
  145.2 9.4 %bitcast_compare_fusion.4 = pred[8,1536,1024]{2,1,0:T(32,128)(4,1)} fusion(s32[1536]{0:T(1024)S(1)} %eq.177, s32[8,96,1024]{2,1,0:T(8,128)S(1)} %dynamic-slice_bitcast_fusion.14), kind=kLoop, calls=%fused_computation.9.clone.1 | loop fusion | flops 12582912 | bytes 15734784 | tf_op jit(solution)/shard_map/while/body/eval_jaxpr/eq | solution.py:56
  154.5 11.7 %bitcast_dynamic-update-slice_fusion.5 = (f32[4,8,64,1024]{3,2,1,0:T(8,128)}, f32[8,64,1024]{2,1,0:T(8,128)S(1)}) fusion(f32[4,8,64,1024]{3,2,1,0:T(8,128)} %get-tuple-element.387, s32[]{:T(128)} %get-tuple-element.386, bf16[8,64,1536]{1,2,0:T(8,128)(2,1)S(1)} %bitcast.165, pred[8,1536,1024]{2,1,0:T(32,128)(4,1)} %bitcast_compare_fusion.4), kind=kOutput, calls=%fused_computation.12.clone.1 | convolution fusion | flops 1610612736 | bytes 18350592 | tf_op jit(solution)/shard_map/while/body/eval_jaxpr/grk,gkl->grl/dot_general | solution.py:81
  177.6 9.4 %bitcast_compare_fusion.4 = pred[8,1536,1024]{2,1,0:T(32,128)(4,1)} fusion(s32[1536]{0:T(1024)S(1)} %eq.177, s32[8,96,1024]{2,1,0:T(8,128)S(1)} %dynamic-slice_bitcast_fusion.14), kind=kLoop, calls=%fused_computation.9.clone.1 | loop fusion | flops 12582912 | bytes 15734784 | tf_op jit(solution)/shard_map/while/body/eval_jaxpr/eq | solution.py:56
  186.9 11.7 %bitcast_dynamic-update-slice_fusion.5 = (f32[4,8,64,1024]{3,2,1,0:T(8,128)}, f32[8,64,1024]{2,1,0:T(8,128)S(1)}) fusion(f32[4,8,64,1024]{3,2,1,0:T(8,128)} %get-tuple-element.387, s32[]{:T(128)} %get-tuple-element.386, bf16[8,64,1536]{1,2,0:T(8,128)(2,1)S(1)} %bitcast.165, pred[8,1536,1024]{2,1,0:T(32,128)(4,1)} %bitcast_compare_fusion.4), kind=kOutput, calls=%fused_computation.12.clone.1 | convolution fusion | flops 1610612736 | bytes 18350592 | tf_op jit(solution)/shard_map/while/body/eval_jaxpr/grk,gkl->grl/dot_general | solution.py:81
  210.0 9.4 %bitcast_compare_fusion.4 = pred[8,1536,1024]{2,1,0:T(32,128)(4,1)} fusion(s32[1536]{0:T(1024)S(1)} %eq.177, s32[8,96,1024]{2,1,0:T(8,128)S(1)} %dynamic-slice_bitcast_fusion.14), kind=kLoop, calls=%fused_computation.9.clone.1 | loop fusion | flops 12582912 | bytes 15734784 | tf_op jit(solution)/shard_map/while/body/eval_jaxpr/eq | solution.py:56
  219.4 11.7 %bitcast_dynamic-update-slice_fusion.5 = (f32[4,8,64,1024]{3,2,1,0:T(8,128)}, f32[8,64,1024]{2,1,0:T(8,128)S(1)}) fusion(f32[4,8,64,1024]{3,2,1,0:T(8,128)} %get-tuple-element.387, s32[]{:T(128)} %get-tuple-element.386, bf16[8,64,1536]{1,2,0:T(8,128)(2,1)S(1)} %bitcast.165, pred[8,1536,1024]{2,1,0:T(32,128)(4,1)} %bitcast_compare_fusion.4), kind=kOutput, calls=%fused_computation.12.clone.1 | convolution fusion | flops 1610612736 | bytes 18350592 | tf_op jit(solution)/shard_map/while/body/eval_jaxpr/grk,gkl->grl/dot_general | solution.py:81
  235.6 11.5 %all_to_all.35 = f32[32,32,2]{0,2,1:T(2,128)S(1)} all-to-all(f32[32,32,2]{0,2,1:T(2,128)S(1)} %get-tuple-element.256), channel_id=1, replica_groups=mesh['corpus'=32,'query'=4] {'corpus'}, dimensions={1} | all-to-all | bytes 16384 | tf_op jit(solution)/shard_map/all_to_all | solution.py:190
  253.0 6.2 gather_fusion
  260.2 6.2 gather_fusion.1
  266.9 4.5 scatter_custom_fusion.3
  272.8 7.5 %all-to-all-start.5 = ((f32[32,32,2]{0,2,1:T(2,128)}), f32[32,32,2]{0,2,1:T(2,128)S(1)}, u32[]{:S(2)}, u32[]{:S(2)}) async-start(f32[32,32,2]{0,2,1:T(2,128)} %copy.148), calls=%async_computation.5 | async-start | bytes 65536 | tf_op jit(solution)/shard_map/all_to_all | solution.py:219
  287.6 6.2 all-to-all-start.3
  295.2 5.9 all-to-all-done.3
  301.3 212.7 %while.28 = (s32[]{:T(128)}, f32[4,8,64,768]{3,1,0,2:T(8,128)}, f32[4,16,96,8]{1,3,2,0:T(8,128)}, s32[4,8,64,9]{2,1,3,0:T(8,128)S(1)}, f32[4,8,64,1024]{3,2,1,0:...) while((s32[]{:T(128)}, f32[4,8,64,768]{3,1,0,2:T(8,128)}, ...), condition=%wide.region_15.16_spmd.clone, body=%wide.region_13.15_spmd.clone.sunk | while | flops 1788871168 | bytes 67385192 | solution.py:131
  302.3 7.1 %select_reduce_fusion.2 = f32[8,64,1024]{2,1,0:T(8,128)} fusion(f32[8]{0:T(128)S(1)} %subtract_multiply_fusion.2, s32[8,64,8]{2,1,0:T(8,128)S(1)} %copy.183), kind=kLoop, calls=%fused_computation.21.clone.1 | loop fusion | flops 12058624 | bytes 2113568 | tf_op jit(solution)/shard_map/while/body/eval_jaxpr/reduce_sum | solution.py:114
  313.6 9.3 %bitcast_compare_fusion.5 = pred[8,1536,1024]{2,1,0:T(32,128)(4,1)} fusion(s32[1536]{0:T(1024)S(1)} %eq.184, s32[8,96,1024]{2,1,0:T(8,128)S(1)} %dynamic-slice_bitcast_fusion.15), kind=kLoop, calls=%fused_computation.19.clone.1 | loop fusion | flops 12582912 | bytes 15734784 | tf_op jit(solution)/shard_map/while/body/eval_jaxpr/eq | solution.py:56
  322.9 12.8 %fusion.84 = f32[8,64,1536]{1,2,0:T(8,128)} fusion(pred[8,1536,1024]{2,1,0:T(32,128)(4,1)} %bitcast_compare_fusion.5, f32[8,64,1024]{2,1,0:T(8,128)} %select_reduce_fusion.2, f32[4,8,64,1024]{3,2,1,0:T(8,128)} %get-tuple-element.430, s32[]{:T(128)} %get-tuple-element.415, f32[8,64]{1,0:T(8,128)S(1)} %get-tuple-element.375, ...), kind=kOutput, calls=%fused_computation.38.clone.1 | convolution fusion | flops 1613234176 | bytes 19928576 | tf_op jit(solution)/shard_map/while/body/eval_jaxpr/grl,gkl->grk/dot_general | solution.py:120
  335.8 5.5 fusion.85
  346.3 8.3 %fusion.86 = f32[4,16,96,8]{1,3,2,0:T(8,128)} fusion(f32[4,16,96,8]{1,3,2,0:T(8,128)} %get-tuple-element.417, s32[]{:T(128)} %get-tuple-element.415, f32[8,64,96,16]{1,3,2,0:T(8,128)} %bitcast.164, bf16[4,8,64,768]{2,3,1,0:T(8,128)(2,1)} %get-tuple-element.435), kind=kOutput, calls=%fused_computation.37.clone.1 | convolution fusion | flops 75497472 | bytes 8258560 | tf_op jit(solution)/shard_map/while/body/eval_jaxpr/grmk,grme->kme/dot_general | solution.py:128
  355.4 7.1 %select_reduce_fusion.2 = f32[8,64,1024]{2,1,0:T(8,128)} fusion(f32[8]{0:T(128)S(1)} %subtract_multiply_fusion.2, s32[8,64,8]{2,1,0:T(8,128)S(1)} %copy.183), kind=kLoop, calls=%fused_computation.21.clone.1 | loop fusion | flops 12058624 | bytes 2113568 | tf_op jit(solution)/shard_map/while/body/eval_jaxpr/reduce_sum | solution.py:114
  366.7 9.3 %bitcast_compare_fusion.5 = pred[8,1536,1024]{2,1,0:T(32,128)(4,1)} fusion(s32[1536]{0:T(1024)S(1)} %eq.184, s32[8,96,1024]{2,1,0:T(8,128)S(1)} %dynamic-slice_bitcast_fusion.15), kind=kLoop, calls=%fused_computation.19.clone.1 | loop fusion | flops 12582912 | bytes 15734784 | tf_op jit(solution)/shard_map/while/body/eval_jaxpr/eq | solution.py:56
  376.0 12.8 %fusion.84 = f32[8,64,1536]{1,2,0:T(8,128)} fusion(pred[8,1536,1024]{2,1,0:T(32,128)(4,1)} %bitcast_compare_fusion.5, f32[8,64,1024]{2,1,0:T(8,128)} %select_reduce_fusion.2, f32[4,8,64,1024]{3,2,1,0:T(8,128)} %get-tuple-element.430, s32[]{:T(128)} %get-tuple-element.415, f32[8,64]{1,0:T(8,128)S(1)} %get-tuple-element.375, ...), kind=kOutput, calls=%fused_computation.38.clone.1 | convolution fusion | flops 1613234176 | bytes 19928576 | tf_op jit(solution)/shard_map/while/body/eval_jaxpr/grl,gkl->grk/dot_general | solution.py:120
  388.9 5.5 fusion.85
  399.4 8.2 %fusion.86 = f32[4,16,96,8]{1,3,2,0:T(8,128)} fusion(f32[4,16,96,8]{1,3,2,0:T(8,128)} %get-tuple-element.417, s32[]{:T(128)} %get-tuple-element.415, f32[8,64,96,16]{1,3,2,0:T(8,128)} %bitcast.164, bf16[4,8,64,768]{2,3,1,0:T(8,128)(2,1)} %get-tuple-element.435), kind=kOutput, calls=%fused_computation.37.clone.1 | convolution fusion | flops 75497472 | bytes 8258560 | tf_op jit(solution)/shard_map/while/body/eval_jaxpr/grmk,grme->kme/dot_general | solution.py:128
  408.4 7.1 %select_reduce_fusion.2 = f32[8,64,1024]{2,1,0:T(8,128)} fusion(f32[8]{0:T(128)S(1)} %subtract_multiply_fusion.2, s32[8,64,8]{2,1,0:T(8,128)S(1)} %copy.183), kind=kLoop, calls=%fused_computation.21.clone.1 | loop fusion | flops 12058624 | bytes 2113568 | tf_op jit(solution)/shard_map/while/body/eval_jaxpr/reduce_sum | solution.py:114
  419.8 9.3 %bitcast_compare_fusion.5 = pred[8,1536,1024]{2,1,0:T(32,128)(4,1)} fusion(s32[1536]{0:T(1024)S(1)} %eq.184, s32[8,96,1024]{2,1,0:T(8,128)S(1)} %dynamic-slice_bitcast_fusion.15), kind=kLoop, calls=%fused_computation.19.clone.1 | loop fusion | flops 12582912 | bytes 15734784 | tf_op jit(solution)/shard_map/while/body/eval_jaxpr/eq | solution.py:56
  429.1 12.8 %fusion.84 = f32[8,64,1536]{1,2,0:T(8,128)} fusion(pred[8,1536,1024]{2,1,0:T(32,128)(4,1)} %bitcast_compare_fusion.5, f32[8,64,1024]{2,1,0:T(8,128)} %select_reduce_fusion.2, f32[4,8,64,1024]{3,2,1,0:T(8,128)} %get-tuple-element.430, s32[]{:T(128)} %get-tuple-element.415, f32[8,64]{1,0:T(8,128)S(1)} %get-tuple-element.375, ...), kind=kOutput, calls=%fused_computation.38.clone.1 | convolution fusion | flops 1613234176 | bytes 19928576 | tf_op jit(solution)/shard_map/while/body/eval_jaxpr/grl,gkl->grk/dot_general | solution.py:120
  441.9 5.5 fusion.85
  452.5 8.2 %fusion.86 = f32[4,16,96,8]{1,3,2,0:T(8,128)} fusion(f32[4,16,96,8]{1,3,2,0:T(8,128)} %get-tuple-element.417, s32[]{:T(128)} %get-tuple-element.415, f32[8,64,96,16]{1,3,2,0:T(8,128)} %bitcast.164, bf16[4,8,64,768]{2,3,1,0:T(8,128)(2,1)} %get-tuple-element.435), kind=kOutput, calls=%fused_computation.37.clone.1 | convolution fusion | flops 75497472 | bytes 8258560 | tf_op jit(solution)/shard_map/while/body/eval_jaxpr/grmk,grme->kme/dot_general | solution.py:128
  461.5 7.1 %select_reduce_fusion.2 = f32[8,64,1024]{2,1,0:T(8,128)} fusion(f32[8]{0:T(128)S(1)} %subtract_multiply_fusion.2, s32[8,64,8]{2,1,0:T(8,128)S(1)} %copy.183), kind=kLoop, calls=%fused_computation.21.clone.1 | loop fusion | flops 12058624 | bytes 2113568 | tf_op jit(solution)/shard_map/while/body/eval_jaxpr/reduce_sum | solution.py:114
  472.8 9.3 %bitcast_compare_fusion.5 = pred[8,1536,1024]{2,1,0:T(32,128)(4,1)} fusion(s32[1536]{0:T(1024)S(1)} %eq.184, s32[8,96,1024]{2,1,0:T(8,128)S(1)} %dynamic-slice_bitcast_fusion.15), kind=kLoop, calls=%fused_computation.19.clone.1 | loop fusion | flops 12582912 | bytes 15734784 | tf_op jit(solution)/shard_map/while/body/eval_jaxpr/eq | solution.py:56
  482.2 12.8 %fusion.84 = f32[8,64,1536]{1,2,0:T(8,128)} fusion(pred[8,1536,1024]{2,1,0:T(32,128)(4,1)} %bitcast_compare_fusion.5, f32[8,64,1024]{2,1,0:T(8,128)} %select_reduce_fusion.2, f32[4,8,64,1024]{3,2,1,0:T(8,128)} %get-tuple-element.430, s32[]{:T(128)} %get-tuple-element.415, f32[8,64]{1,0:T(8,128)S(1)} %get-tuple-element.375, ...), kind=kOutput, calls=%fused_computation.38.clone.1 | convolution fusion | flops 1613234176 | bytes 19928576 | tf_op jit(solution)/shard_map/while/body/eval_jaxpr/grl,gkl->grk/dot_general | solution.py:120
  495.0 5.5 fusion.85
  505.6 8.2 %fusion.86 = f32[4,16,96,8]{1,3,2,0:T(8,128)} fusion(f32[4,16,96,8]{1,3,2,0:T(8,128)} %get-tuple-element.417, s32[]{:T(128)} %get-tuple-element.415, f32[8,64,96,16]{1,3,2,0:T(8,128)} %bitcast.164, bf16[4,8,64,768]{2,3,1,0:T(8,128)(2,1)} %get-tuple-element.435), kind=kOutput, calls=%fused_computation.37.clone.1 | convolution fusion | flops 75497472 | bytes 8258560 | tf_op jit(solution)/shard_map/while/body/eval_jaxpr/grmk,grme->kme/dot_general | solution.py:128
  514.1 5.0 all-to-all-start.6
  519.2 141.8 %psum.7 = f32[16,768]{0,1:T(8,128)S(1)} all-reduce(f32[16,768]{0,1:T(8,128)S(1)} %bitcast.174), channel_id=1, replica_groups=mesh['corpus'=32,'query'=4] {'corpus','query'}, use_global_device_ids=true, to_apply=%region_18.19 | all-reduce | flops 12288 | bytes 98304 | tf_op jit(solution)/shard_map/psum | solution.py:243
  663.2 10.3 %copy.154 = f32[32,32,2,768]{3,2,1,0:T(2,128)} copy(f32[32,32,2,768]{3,0,2,1:T(8,128)} %all-to-all-done.6) | data formatting | bytes 12582912 | tf_op jit(solution)/shard_map/all_to_all | solution.py:234
  673.5 8.5 %reshape.321 = f32[2048,768]{1,0:T(8,128)} reshape(f32[32,32,2,768]{3,2,1,0:T(2,128)} %copy.154) | data formatting | bytes 12582912 | tf_op jit(solution)/shard_map/reshape | solution.py:241
  682.1 8.7 %gather_fusion.2 = f32[1024,768]{1,0:T(8,128)} fusion(f32[2048,768]{1,0:T(8,128)} %reshape.321, s32[1024]{0:T(1024)S(1)} %copy-done.14), kind=kCustom, calls=%fused_computation.2 | custom fusion | bytes 6295552 | tf_op jit(solution)/shard_map/gather | solution.py:241
  (241 shorter events, 145.7 us)
Async XLA Ops:
  2.4 1.9 copy-start.1
  9.5 0.8 copy-start.16
  10.2 16.1 %copy-start.7 = (bf16[256,768]{1,0:T(8,128)(2,1)S(1)}, bf16[256,768]{1,0:T(8,128)(2,1)}, u32[]{:S(2)}) copy-start(bf16[256,768]{1,0:T(8,128)(2,1)} %param.9) | copy-start | bytes 1179652
  10.9 17.1 %copy-start.15 = (s32[1024,1]{0,1:T(1,128)}, s32[1024,1]{0,1:T(1,128)S(1)}, u32[]{:S(2)}) copy-start(s32[1024,1]{0,1:T(1,128)S(1)} %compare_select_fusion.1) | copy-start | bytes 12292
  16.7 28.0 %all-to-all-start = ((s32[32,1,576]{2,1,0:T(1,128)}), s32[32,1,576]{2,1,0:T(1,128)S(1)}, u32[]{:S(2)}, u32[]{:S(2)}) async-start(s32[32,1,576]{2,1,0:T(1,128)} %reshape.393), calls=%async_computation | async-start | bytes 163840 | tf_op jit(solution)/shard_map/all_to_all | solution.py:175
  44.7 7.4 %copy-start.8 = (s32[32,1,576]{2,1,0:T(1,128)}, s32[32,1,576]{2,1,0:T(1,128)S(1)}, u32[]{:S(2)}) copy-start(s32[32,1,576]{2,1,0:T(1,128)S(1)} %all-to-all-done) | copy-start | bytes 221188
  44.7 47.1 %all-to-all-start.1 = ((bf16[32,32,2,768]{3,2,0,1:T(2,128)(2,1)}), bf16[32,32,2,768]{3,2,0,1:T(2,128)(2,1)S(1)}, u32[]{:S(2)}, u32[]{:S(2)}) async-start(bf16[32,32,2,768]{3,2,0,1:T(2,128)(2,1)} %copy.136), calls=%async_computation.1 | async-start | bytes 6291456 | tf_op jit(solution)/shard_map/all_to_all | solution.py:168
  58.8 0.7 copy-start.3
  112.8 9.4 %copy-start = (bf16[8,64,96,16]{1,3,2,0:T(8,128)(2,1)S(1)}, bf16[8,64,96,16]{1,3,2,0:T(8,128)(2,1)}, u32[]{:S(2)}) copy-start(bf16[8,64,96,16]{1,3,2,0:T(8,128)(2,1)} %copy.181) | copy-start | bytes 4718596 | tf_op jit(solution)/shard_map/while
  145.2 9.4 %copy-start = (bf16[8,64,96,16]{1,3,2,0:T(8,128)(2,1)S(1)}, bf16[8,64,96,16]{1,3,2,0:T(8,128)(2,1)}, u32[]{:S(2)}) copy-start(bf16[8,64,96,16]{1,3,2,0:T(8,128)(2,1)} %copy.181) | copy-start | bytes 4718596 | tf_op jit(solution)/shard_map/while
  177.6 9.4 %copy-start = (bf16[8,64,96,16]{1,3,2,0:T(8,128)(2,1)S(1)}, bf16[8,64,96,16]{1,3,2,0:T(8,128)(2,1)}, u32[]{:S(2)}) copy-start(bf16[8,64,96,16]{1,3,2,0:T(8,128)(2,1)} %copy.181) | copy-start | bytes 4718596 | tf_op jit(solution)/shard_map/while
  210.0 9.4 %copy-start = (bf16[8,64,96,16]{1,3,2,0:T(8,128)(2,1)S(1)}, bf16[8,64,96,16]{1,3,2,0:T(8,128)(2,1)}, u32[]{:S(2)}) copy-start(bf16[8,64,96,16]{1,3,2,0:T(8,128)(2,1)} %copy.181) | copy-start | bytes 4718596 | tf_op jit(solution)/shard_map/while
  247.1 12.3 %all-to-all-start.4 = ((f32[32,32,2]{0,2,1:T(2,128)}), f32[32,32,2]{0,2,1:T(2,128)S(1)}, u32[]{:S(2)}, u32[]{:S(2)}) async-start(f32[32,32,2]{0,2,1:T(2,128)} %get-tuple-element.255), calls=%async_computation.4 | async-start | bytes 65536 | tf_op jit(solution)/shard_map/all_to_all | solution.py:197
  252.2 14.2 %copy-start.13 = (s32[1024]{0:T(1024)}, s32[1024]{0:T(1024)S(1)}, u32[]{:S(2)}) copy-start(s32[1024]{0:T(1024)S(1)} %broadcast_clamp_fusion) | copy-start | bytes 12292
  259.4 34.5 %copy-start.4 = (s32[32,32,2,9]{0,2,1,3:T(2,128)S(1)}, s32[32,32,2,9]{0,2,1,3:T(2,128)}, u32[]{:S(2)}) copy-start(s32[32,32,2,9]{0,2,1,3:T(2,128)} %copy-done.3) | copy-start | bytes 221188
  272.8 14.8 %all-to-all-start.5 = ((f32[32,32,2]{0,2,1:T(2,128)}), f32[32,32,2]{0,2,1:T(2,128)S(1)}, u32[]{:S(2)}, u32[]{:S(2)}) async-start(f32[32,32,2]{0,2,1:T(2,128)} %copy.148), calls=%async_computation.5 | async-start | bytes 65536 | tf_op jit(solution)/shard_map/all_to_all | solution.py:219
  287.6 13.5 %all-to-all-start.3 = ((f32[32,32,2]{0,2,1:T(2,128)}), f32[32,32,2]{0,2,1:T(2,128)S(1)}, u32[]{:S(2)}, u32[]{:S(2)}) async-start(f32[32,32,2]{0,2,1:T(2,128)} %copy.144), calls=%async_computation.3 | async-start | bytes 65536 | tf_op jit(solution)/shard_map/all_to_all | solution.py:212
  301.5 0.6 copy-start.9
  301.5 0.6 copy-start.11
  301.5 8.5 %copy-start.5 = (s32[4,8,64,9]{2,1,3,0:T(8,128)}, s32[4,8,64,9]{2,1,3,0:T(8,128)S(1)}, u32[]{:S(2)}) copy-start(s32[4,8,64,9]{2,1,3,0:T(8,128)S(1)} %get-tuple-element.429) | copy-start | bytes 221188 | tf_op jit(solution)/shard_map/while
  346.3 8.3 %copy-start.6 = (s32[4,8,64,9]{2,1,3,0:T(8,128)S(1)}, s32[4,8,64,9]{2,1,3,0:T(8,128)}, u32[]{:S(2)}) copy-start(s32[4,8,64,9]{2,1,3,0:T(8,128)} %copy-done.5) | copy-start | bytes 221188 | tf_op jit(solution)/shard_map/while
  346.3 8.3 %copy-start.10 = (f32[4,8,64]{2,1,0:T(8,128)S(1)}, f32[4,8,64]{2,1,0:T(8,128)}, u32[]{:S(2)}) copy-start(f32[4,8,64]{2,1,0:T(8,128)} %copy-done.9) | copy-start | bytes 24580 | tf_op jit(solution)/shard_map/while
  346.3 8.3 %copy-start.12 = (f32[4,8,64]{2,1,0:T(8,128)S(1)}, f32[4,8,64]{2,1,0:T(8,128)}, u32[]{:S(2)}) copy-start(f32[4,8,64]{2,1,0:T(8,128)} %copy-done.11) | copy-start | bytes 24580 | tf_op jit(solution)/shard_map/while
  354.6 0.6 copy-start.9
  354.6 0.6 copy-start.11
  354.6 8.5 %copy-start.5 = (s32[4,8,64,9]{2,1,3,0:T(8,128)}, s32[4,8,64,9]{2,1,3,0:T(8,128)S(1)}, u32[]{:S(2)}) copy-start(s32[4,8,64,9]{2,1,3,0:T(8,128)S(1)} %get-tuple-element.429) | copy-start | bytes 221188 | tf_op jit(solution)/shard_map/while
  399.4 8.2 %copy-start.6 = (s32[4,8,64,9]{2,1,3,0:T(8,128)S(1)}, s32[4,8,64,9]{2,1,3,0:T(8,128)}, u32[]{:S(2)}) copy-start(s32[4,8,64,9]{2,1,3,0:T(8,128)} %copy-done.5) | copy-start | bytes 221188 | tf_op jit(solution)/shard_map/while
  399.4 8.2 %copy-start.10 = (f32[4,8,64]{2,1,0:T(8,128)S(1)}, f32[4,8,64]{2,1,0:T(8,128)}, u32[]{:S(2)}) copy-start(f32[4,8,64]{2,1,0:T(8,128)} %copy-done.9) | copy-start | bytes 24580 | tf_op jit(solution)/shard_map/while
  399.4 8.2 %copy-start.12 = (f32[4,8,64]{2,1,0:T(8,128)S(1)}, f32[4,8,64]{2,1,0:T(8,128)}, u32[]{:S(2)}) copy-start(f32[4,8,64]{2,1,0:T(8,128)} %copy-done.11) | copy-start | bytes 24580 | tf_op jit(solution)/shard_map/while
  407.7 0.6 copy-start.9
  407.7 0.6 copy-start.11
  407.7 8.5 %copy-start.5 = (s32[4,8,64,9]{2,1,3,0:T(8,128)}, s32[4,8,64,9]{2,1,3,0:T(8,128)S(1)}, u32[]{:S(2)}) copy-start(s32[4,8,64,9]{2,1,3,0:T(8,128)S(1)} %get-tuple-element.429) | copy-start | bytes 221188 | tf_op jit(solution)/shard_map/while
  452.5 8.3 %copy-start.6 = (s32[4,8,64,9]{2,1,3,0:T(8,128)S(1)}, s32[4,8,64,9]{2,1,3,0:T(8,128)}, u32[]{:S(2)}) copy-start(s32[4,8,64,9]{2,1,3,0:T(8,128)} %copy-done.5) | copy-start | bytes 221188 | tf_op jit(solution)/shard_map/while
  452.5 8.3 %copy-start.10 = (f32[4,8,64]{2,1,0:T(8,128)S(1)}, f32[4,8,64]{2,1,0:T(8,128)}, u32[]{:S(2)}) copy-start(f32[4,8,64]{2,1,0:T(8,128)} %copy-done.9) | copy-start | bytes 24580 | tf_op jit(solution)/shard_map/while
  452.5 8.3 %copy-start.12 = (f32[4,8,64]{2,1,0:T(8,128)S(1)}, f32[4,8,64]{2,1,0:T(8,128)}, u32[]{:S(2)}) copy-start(f32[4,8,64]{2,1,0:T(8,128)} %copy-done.11) | copy-start | bytes 24580 | tf_op jit(solution)/shard_map/while
  460.7 0.6 copy-start.9
  460.8 0.6 copy-start.11
  460.8 8.5 %copy-start.5 = (s32[4,8,64,9]{2,1,3,0:T(8,128)}, s32[4,8,64,9]{2,1,3,0:T(8,128)S(1)}, u32[]{:S(2)}) copy-start(s32[4,8,64,9]{2,1,3,0:T(8,128)S(1)} %get-tuple-element.429) | copy-start | bytes 221188 | tf_op jit(solution)/shard_map/while
  505.6 8.2 %copy-start.6 = (s32[4,8,64,9]{2,1,3,0:T(8,128)S(1)}, s32[4,8,64,9]{2,1,3,0:T(8,128)}, u32[]{:S(2)}) copy-start(s32[4,8,64,9]{2,1,3,0:T(8,128)} %copy-done.5) | copy-start | bytes 221188 | tf_op jit(solution)/shard_map/while
  505.6 8.2 %copy-start.10 = (f32[4,8,64]{2,1,0:T(8,128)S(1)}, f32[4,8,64]{2,1,0:T(8,128)}, u32[]{:S(2)}) copy-start(f32[4,8,64]{2,1,0:T(8,128)} %copy-done.9) | copy-start | bytes 24580 | tf_op jit(solution)/shard_map/while
  505.6 8.2 %copy-start.12 = (f32[4,8,64]{2,1,0:T(8,128)S(1)}, f32[4,8,64]{2,1,0:T(8,128)}, u32[]{:S(2)}) copy-start(f32[4,8,64]{2,1,0:T(8,128)} %copy-done.11) | copy-start | bytes 24580 | tf_op jit(solution)/shard_map/while
  514.0 5.0 copy-start.2
  514.1 149.2 %all-to-all-start.6 = ((f32[32,32,2,768]{3,0,2,1:T(8,128)}), f32[32,32,2,768]{3,0,2,1:T(8,128)}, u32[]{:S(2)}, u32[]{:S(2)}) async-start(f32[32,32,2,768]{3,0,2,1:T(8,128)} %bitcast.170), calls=%async_computation.6 | async-start | bytes 12582912 | tf_op jit(solution)/shard_map/all_to_all | solution.py:234
  673.5 8.5 %copy-start.14 = (s32[1024]{0:T(1024)S(1)}, s32[1024]{0:T(1024)}, u32[]{:S(2)}) copy-start(s32[1024]{0:T(1024)} %copy-done.13) | copy-start | bytes 12292
where the time goes:
time: 708 us; the launch traced here: 697 us
  matrix products  170 us (24%)
  local copies, waits for them, and re-layouts  168 us (24%)
  blocking collectives  153 us (22%)
  other arithmetic  125 us (18%)
  starting transfers between devices  40.1 us (6%)
  waiting for transfers between devices  38.7 us (5%)
    psum x1, blocking collectives, shards(): book_sum = lax.psum(book_part, ('corpus', 'query'))  142 us
    eq x8, other arithmetic, code_one_hot(): marked = code_block[:, :, None, :] == levels[None, None, :, None]  74.8 us
    dot_general x4, matrix products, grad_piece(): jnp.einsum('grl,gkl->grk', grad_scores, one_hot, preferred_element_type=j...  51.3 us
    dot_general x4, matrix products, score_piece(): jnp.einsum('grk,gkl->grl', lut_rows, one_hot, preferred_element_type=jnp....  46.8 us
    dot_general x4, matrix products, grad_piece(): jnp.einsum('grmk,grme->kme', histogram, split_rows, precision=highest)  33 us
    all_to_all x1, waiting for transfers between devices, shards(): lax.all_to_all(sending.reshape(lists_dev, corpus_size, capacity, D), 'cor...  31.6 us
    eq x24, local copies, waits for them, and re-layouts, code_one_hot(): marked = code_block[:, :, None, :] == levels[None, None, :, None]  28.9 us
    reduce_sum x4, other arithmetic, grad_piece(): jnp.sum(jnp.where(target_spot[:, :, :, None] == places, weights[:, None],...  28.5 us
  transfers between devices with their start and end apart: 6, of which 3 were waited for; matrix products, arithmetic and copies ran while one was open for 6% of the time, Pallas kernels for 0%

commit v1 on v0

v1 whole, which is shorter than its diff:
```python
import functools

import jax
import jax.numpy as jnp
from jax import lax
from jax.experimental import pallas as pl
from jax.experimental.pallas import tpu as pltpu
from jax.sharding import PartitionSpec as P

D = 768
SUBSPACES = 96
CENTROIDS = 16
SUBDIM = 8
PASSAGES = 1024
PROBES = 4
TARGETS = 8
CAP = 2
EPSILON = 1e-06

BOTH = ("corpus", "query")
CHUNKS = 6
FEATS = 128
ENTRIES = 256
WIDTH = SUBSPACES * CENTROIDS
F32 = jnp.float32
BF16 = jnp.bfloat16


def dot(a, b, dims=((1,), (0,))):
    return lax.dot_general(a, b, (dims, ((), ())), preferred_element_type=F32)


def iota(shape, axis):
    return lax.broadcasted_iota(jnp.int32, shape, axis)


def ones_where(mask):
    return jnp.where(mask, 1.0, 0.0).astype(BF16)


def split_two(value):
    high = value.astype(BF16)
    return high, (value - high.astype(F32)).astype(BF16)


def names_list(probe_rows, lists):
    found = probe_rows[0:1, :] == lists
    for p in range(1, PROBES):
        found = found | (probe_rows[p : p + 1, :] == lists)
    return found


def dispatch_body(probes_t, queries, sending):
    rows, count = sending.shape[0], queries.shape[0]
    slot = iota((rows, count), 0) + pl.program_id(0) * rows
    found = names_list(probes_t[...], slot >> 1)
    before = ones_where(iota((count, count), 0) < iota((count, count), 1))
    rank = dot(ones_where(found), before)
    chosen = ones_where(found & (rank == (slot & 1).astype(F32)))
    sending[...] = dot(chosen, queries[...]).astype(BF16)


def home_body(probes_t, probes, targets_wide, chosen_out, masks_out, notes_out):
    count = probes.shape[0]
    slots = chosen_out.shape[1]
    devices = notes_out.shape[0]
    per_device = masks_out.shape[0]
    block = 512
    after = ones_where(iota((count, count), 0) > iota((count, count), 1))
    for b in range(slots // block):
        slot = iota((count, block), 1) + b * block
        found = probes[:, 0:1] == (slot >> 1)
        for p in range(1, PROBES):
            found = found | (probes[:, p : p + 1] == (slot >> 1))
        rank = dot(after, ones_where(found))
        chosen_out[:, b * block : (b + 1) * block] = ones_where(
            found & (rank == (slot & 1).astype(F32))
        )
    wide = targets_wide[...]
    spot = wide & (PASSAGES - 1)
    column = wide // PASSAGES
    in_list = jnp.broadcast_to(probes[:, 0:1], wide.shape)
    for p in range(1, PROBES):
        in_list = jnp.where(column == p, probes[:, p : p + 1], in_list)
    parts = jnp.concatenate(
        [in_list >> 5, in_list & 31, spot >> 5, spot & 31], axis=1
    ).astype(F32).astype(BF16)
    before = ones_where(iota((count, count), 0) < iota((count, count), 1))
    lane = iota((devices, 128), 1)
    gathered = jnp.zeros((devices, 4 * 128), F32)
    lane_wide = iota((devices, 4 * 128), 1) & 127
    for i in range(per_device // 2):
        lists = iota((devices, count), 0) * (per_device // 2) + i
        found = names_list(probes_t[...], lists)
        rank = dot(ones_where(found), before)
        for r in range(2):
            mask = ones_where(found & (rank == float(r)))
            masks_out[2 * i + r] = mask
            here = dot(mask, parts)
            gathered = jnp.where(lane_wide // TARGETS == 2 * i + r, here, gathered)
    got_list = gathered[:, 0:128] * 32.0 + gathered[:, 128:256]
    got_spot = gathered[:, 256:384] * 32.0 + gathered[:, 384:512]
    own_list = iota((devices, 128), 0) * (per_device // 2) + lane // (2 * TARGETS)
    notes_out[...] = jnp.where(got_list == own_list.astype(F32), got_spot + 1.0, 0.0)


def fill_one_hot(codes, one_hot):
    for c in range(CHUNKS):
        part = codes[c * 16 : (c + 1) * 16, :].astype(F32).astype(BF16)
        for k in range(CENTROIDS):
            at = c * ENTRIES + k * 16
            one_hot[at : at + 16, :] = jnp.where(
                part == jnp.asarray(k, BF16), jnp.asarray(1, BF16), jnp.asarray(0, BF16)
            )


def score_body(offset, got, high, low, codes, exps, stats, table, one_hot):
    i = pl.program_id(0)
    half = got.shape[0] // (2 * 8)

    @pl.when(i == 0)
    def _():
        stats[...] = jnp.zeros_like(stats)
        for c in range(CHUNKS):
            rows = got[:, c * FEATS : (c + 1) * FEATS]
            twice = jnp.concatenate([rows, rows], axis=1)
            weights = jnp.concatenate([high[c], low[c]], axis=1)
            looked = dot(twice, weights, ((1,), (1,)))
            table[2 * c] = looked[:, 0:128]
            table[2 * c + 1] = looked[:, 128:256]

    fill_one_hot(codes.at[0], one_hot)
    rows = jnp.concatenate(
        [
            jnp.concatenate(
                [
                    table[j, pl.ds(2 * i + r, half, stride=16), :].astype(BF16)
                    for j in range(WIDTH // 128)
                ],
                axis=1,
            )
            for r in range(2)
        ],
        axis=0,
    )
    scores = dot(rows, one_hot[...])
    top = jnp.max(scores, axis=1, keepdims=True)
    exp_scores = jnp.exp(scores - top)
    total = jnp.sum(exp_scores, axis=1, keepdims=True)
    exps[0] = exp_scores
    lane = iota(stats.shape, 1)
    held = stats[...]
    for r in range(2):
        held = jnp.where(lane == 2 * i + r, top[r * half : (r + 1) * half], held)
        held = jnp.where(lane == 16 + 2 * i + r, total[r * half : (r + 1) * half], held)
    stats[...] = held


def weight_body(stats, masks, notes, message):
    per_device, devices, count = masks.shape
    low = -3.0e38
    peak = jnp.full((devices, count), low, F32)
    for s in range(per_device):
        peak = jnp.where(masks[s] > 0, stats[:, s : s + 1], peak) if s == 0 else jnp.maximum(
            peak, jnp.where(masks[s] > 0, stats[:, s : s + 1], low)
        )
    peak = jnp.max(peak, axis=0, keepdims=True)
    denom = jnp.zeros((devices, count), F32)
    for s in range(per_device):
        part = jnp.exp(stats[:, s : s + 1] - peak) * stats[:, 16 + s : 17 + s]
        denom = denom + jnp.where(masks[s] > 0, part, 0.0)
    denom = jnp.sum(denom, axis=0, keepdims=True)
    lane = iota((devices, 128), 1)
    held = jnp.zeros((devices, 128), F32)
    for s in range(per_device):
        part = jnp.exp(stats[:, s : s + 1] - peak) / denom
        part = jnp.sum(jnp.where(masks[s] > 0, part, 0.0), axis=1, keepdims=True)
        held = jnp.where(lane == s, part, held)
    message[:, 0:128] = held
    message[:, 128:256] = notes[...]


def grad_body(offset, exps, message, codes, got, high, low, part_out, book_out, hist, one_hot):
    i = pl.program_id(0)
    half = got.shape[0] // (2 * 8)
    fill_one_hot(codes.at[0], one_hot)
    turned = pltpu.roll(message[:, 128:256], (128 - 2 * TARGETS * i) % 128, 1)
    lane = iota((half, 128), 1)
    place = iota((half, PASSAGES), 1).astype(F32)
    grads = []
    for r in range(2):
        scale = jnp.sum(
            jnp.where(lane == 2 * i + r, message[:, 0:128], 0.0), axis=1, keepdims=True
        )
        teacher = jnp.zeros((half, PASSAGES), F32)
        for t in range(TARGETS):
            at = r * TARGETS + t
            weight = 2.0 * (TARGETS - t) / (TARGETS * (TARGETS + 1.0))
            teacher = jnp.where(place == turned[:, at : at + 1] - 1.0, weight, teacher)
        student = exps[0, r * half : (r + 1) * half, :] * scale
        grads.append((student - teacher).astype(BF16))
    grads = jnp.concatenate(grads, axis=0)
    found = dot(grads, one_hot[...], ((1,), (1,)))
    for r in range(2):
        for j in range(WIDTH // 128):
            hist[j, pl.ds(2 * i + r, half, stride=16), :] = found[
                r * half : (r + 1) * half, j * 128 : (j + 1) * 128
            ]

    @pl.when(i == pl.num_programs(0) - 1)
    def _():
        keep = iota((ENTRIES, FEATS), 0) % 16 == iota((ENTRIES, FEATS), 1) // SUBDIM
        for c in range(CHUNKS):
            h_high, h_low = split_two(jnp.concatenate([hist[2 * c], hist[2 * c + 1]], axis=1))
            both = jnp.concatenate([high[c], low[c]], axis=1)
            wide = dot(h_high, both)
            part = wide[:, 0:FEATS] + wide[:, FEATS:] + dot(h_low, high[c])
            part_out[:, c * FEATS : (c + 1) * FEATS] = part.astype(BF16)
            rows = got[:, c * FEATS : (c + 1) * FEATS]
            book = dot(rows, h_high, ((0,), (0,))) + dot(rows, h_low, ((0,), (0,)))
            book = jnp.where(keep, book.T, 0.0)
            book_out[:, c * FEATS : (c + 1) * FEATS] = jnp.sum(
                book.reshape(CENTROIDS, 16, FEATS), axis=1
            )


def combine_body(chosen, returned, out):
    out[...] = dot(chosen[...], returned[...]).astype(BF16)


def whole(shape):
    return pl.BlockSpec(shape, lambda *_: (0,) * len(shape))


def exchange(value):
    return lax.all_to_all(value, BOTH, 0, 0, tiled=True)


def spread_codebook(codebook):
    book = codebook.reshape(CENTROIDS, CHUNKS, FEATS).transpose(1, 0, 2)
    own = jnp.arange(16)[:, None] == jnp.arange(FEATS)[None, :] // SUBDIM
    spread = jnp.where(own[None, None], book[:, :, None, :], 0.0)
    spread = spread.reshape(CHUNKS, ENTRIES, FEATS)
    high = lax.reduce_precision(spread, 8, 7)
    return high.astype(BF16), (spread - high).astype(BF16)


def shards(queries, probes, targets, passage_codes, codebook):
    devices = lax.axis_size("corpus") * lax.axis_size("query")
    count = queries.shape[0]
    own_lists = passage_codes.shape[0] // lax.axis_size("query")
    per_device = own_lists * CAP
    slots = devices * per_device
    list_rows = devices * CAP
    probes_t = probes.T
    big = pltpu.CompilerParams(
        dimension_semantics=("arbitrary",), vmem_limit_bytes=58 * 1024 * 1024
    )

    sending = pl.pallas_call(
        dispatch_body,
        out_shape=jax.ShapeDtypeStruct((slots, D), BF16),
        grid=(8,),
        in_specs=[whole((PROBES, count)), whole((count, D))],
        out_specs=pl.BlockSpec((slots // 8, D), lambda b: (b, 0)),
        name="dispatch",
    )(probes_t, queries)
    got = exchange(sending)

    chosen, masks, notes = pl.pallas_call(
        home_body,
        out_shape=(
            jax.ShapeDtypeStruct((count, slots), BF16),
            jax.ShapeDtypeStruct((per_device, devices, count), BF16),
            jax.ShapeDtypeStruct((devices, 128), F32),
        ),
        name="home",
    )(probes_t, probes, jnp.tile(targets, (1, 128 // TARGETS)))
    high, low = spread_codebook(codebook)
    offset = (lax.axis_index("query") * own_lists).astype(jnp.int32).reshape(1)
    codes_spec = pl.BlockSpec((1, SUBSPACES, PASSAGES), lambda i, off: (off[0] + i, 0, 0))
    exps_spec = pl.BlockSpec((1, list_rows, PASSAGES), lambda i, off: (i, 0, 0))
    table_spec = whole((CHUNKS, ENTRIES, FEATS))

    exps, stats = pl.pallas_call(
        score_body,
        out_shape=(
            jax.ShapeDtypeStruct((own_lists, list_rows, PASSAGES), F32),
            jax.ShapeDtypeStruct((devices, 128), F32),
        ),
        grid_spec=pltpu.PrefetchScalarGridSpec(
            num_scalar_prefetch=1,
            grid=(own_lists,),
            in_specs=[whole((slots, D)), table_spec, table_spec, codes_spec],
            out_specs=[exps_spec, whole((devices, 128))],
            scratch_shapes=[
                pltpu.VMEM((WIDTH // 128, slots, 128), F32),
                pltpu.VMEM((WIDTH, PASSAGES), BF16),
            ],
        ),
        compiler_params=big,
        name="score",
    )(offset, got, high, low, passage_codes)

    message = pl.pallas_call(
        weight_body,
        out_shape=jax.ShapeDtypeStruct((devices, 256), F32),
        name="weigh",
    )(exchange(stats), masks, notes)

    partial_value, book = pl.pallas_call(
        grad_body,
        out_shape=(
            jax.ShapeDtypeStruct((slots, D), BF16),
            jax.ShapeDtypeStruct((CENTROIDS, D), F32),
        ),
        grid_spec=pltpu.PrefetchScalarGridSpec(
            num_scalar_prefetch=1,
            grid=(own_lists,),
            in_specs=[
                exps_spec,
                whole((devices, 256)),
                codes_spec,
                whole((slots, D)),
                table_spec,
                table_spec,
            ],
            out_specs=[whole((slots, D)), whole((CENTROIDS, D))],
            scratch_shapes=[
                pltpu.VMEM((WIDTH // 128, slots, 128), F32),
                pltpu.VMEM((WIDTH, PASSAGES), BF16),
            ],
        ),
        compiler_params=big,
        name="grad",
    )(offset, exps, exchange(message), passage_codes, got, high, low)

    book_parts = exchange(book.reshape(devices, -1))
    own_sum = jnp.sum(book_parts, axis=0, keepdims=True)
    book_sum = exchange(jnp.broadcast_to(own_sum, book_parts.shape)).reshape(CENTROIDS, D)
    normed = book_sum * lax.rsqrt(jnp.mean(book_sum * book_sum) + EPSILON)

    grad_queries = pl.pallas_call(
        combine_body,
        out_shape=jax.ShapeDtypeStruct((count, D), BF16),
        grid=(3,),
        in_specs=[whole((count, slots)), pl.BlockSpec((slots, D // 3), lambda b: (0, b))],
        out_specs=pl.BlockSpec((count, D // 3), lambda b: (0, b)),
        name="combine",
    )(chosen, exchange(partial_value))
    return grad_queries, normed


def solution(mesh):
    placed = (
        P(BOTH, None),
        P(BOTH, None),
        P(BOTH, None),
        P("corpus", None, None),
        P(),
    )
    return jax.shard_map(
        shards,
        mesh=mesh,
        in_specs=placed,
        out_specs=(P(BOTH, None), P()),
        check_vma=False,
    )
```

time: 708 us -> 230 us (0.32); the launches traced: 697 us -> 229 us
  matrix products: 170 us -> 0 us
  local copies, waits for them, and re-layouts: 168 us -> 8.89 us
  other arithmetic: 125 us -> 2.12 us
  blocking collectives: 153 us -> 44.3 us
  Pallas kernels: 0 us -> 69.2 us
  waiting for transfers between devices: 38.7 us -> 84.1 us
  starting transfers between devices: 40.1 us -> 19.1 us
    dot_general x20 -> x0, matrix products: 170 us -> none  [the longest x4 51.3 us: grad_piece(): jnp.einsum('grl,gkl->grk', grad_scores, one_hot, preferred_element_type=j...]
    psum x1 -> x0, blocking collectives: 142 us -> none  [shards(): book_sum = lax.psum(book_part, ('corpus', 'query'))]
    eq x8 -> x1, other arithmetic: 74.8 us -> 0.01 us  [spread_codebook(): own = jnp.arange(16)[:, None] == jnp.arange(FEATS)[None, :] // SUBDIM]
    pallas_call x0 -> x6, Pallas kernels: none -> 69.2 us  [the longest x1 31.7 us: shards(): pl.pallas_call(grad_body, out_shape=(jax.ShapeDtypeStruct((slots, D), BF1...]
    all_to_all x6 -> x3, waiting for transfers between devices: 38.7 us -> 84.1 us  [exchange(): return lax.all_to_all(value, BOTH, 0, 0, tiled=True)]
    reduce_sum x12 -> x1, other arithmetic: 34.4 us -> 0.15 us  [shards(): own_sum = jnp.sum(book_parts, axis=0, keepdims=True)]
    all_to_all x1 -> x3, blocking collectives: 11.5 us -> 44.3 us  [exchange(): return lax.all_to_all(value, BOTH, 0, 0, tiled=True)]
    eq x30 -> x0, local copies, waits for them, and re-layouts: 29.4 us -> none  [the longest x24 28.9 us: code_one_hot(): marked = code_block[:, :, None, :] == levels[None, None, :, None]]
  transfers between devices with their start and end apart: 6 -> 3, of which waited for: 3 -> 3; matrix products, arithmetic and copies ran while one was open for 6% -> 2% of each run, Pallas kernels for 0% -> 2%
where the time goes in v1:
time: 230 us; the launch traced here: 229 us
  waiting for transfers between devices  84.1 us (37%)
  Pallas kernels  69.2 us (30%)
  blocking collectives  44.3 us (19%)
  starting transfers between devices  19.1 us (8%)
  local copies, waits for them, and re-layouts  8.89 us (4%)
    all_to_all x3, waiting for transfers between devices, exchange(): return lax.all_to_all(value, BOTH, 0, 0, tiled=True)  84.1 us
    all_to_all x3, blocking collectives, exchange(): return lax.all_to_all(value, BOTH, 0, 0, tiled=True)  44.3 us
    pallas_call x1, Pallas kernels, shards(): pl.pallas_call(grad_body, out_shape=(jax.ShapeDtypeStruct((slots, D), BF1...  31.7 us
    all_to_all x3, starting transfers between devices, exchange(): return lax.all_to_all(value, BOTH, 0, 0, tiled=True)  19.1 us
    pallas_call x1, Pallas kernels, shards(): pl.pallas_call(score_body, out_shape=(jax.ShapeDtypeStruct((own_lists, li...  18 us
    pallas_call x1, Pallas kernels, shards(): pl.pallas_call(dispatch_body, out_shape=jax.ShapeDtypeStruct((slots, D),...  6.33 us
    unnamed x14, local copies, waits for them, and re-layouts  5.44 us
    pallas_call x1, Pallas kernels, shards(): pl.pallas_call(home_body, out_shape=(jax.ShapeDtypeStruct((count, slots),...  5.3 us
  transfers between devices with their start and end apart: 3, of which 3 were waited for; matrix products, arithmetic and copies ran while one was open for 2% of the time, Pallas kernels for 2%

profile of v1, /device:TPU:1, one launch (start us, length us, event | category | flops | bytes accessed | tf_op | source)
XLA Modules:
  0.0 229.1 jit_solution(2140457937107989717)
XLA Ops:
  0.6 0.0 copy-start
  0.6 6.3 %dispatch.1 = bf16[2048,768]{1,0:T(8,128)(2,1)} custom-call(s32[4,256]{1,0:T(4,128)} %bitcast.37, bf16[256,768]{1,0:T(8,128)(2,1)} %queries.1), custom_call_target="tpu_custom_call" | custom-call | tf_op jit(solution)/shard_map/dispatch/pallas_call | solution.py:260
  7.0 0.0 copy-start.4
  7.0 11.5 %all-to-all-start = ((bf16[128,16,768]{2,1,0:T(8,128)(2,1)}), bf16[128,16,768]{2,1,0:T(8,128)(2,1)S(1)}, u32[]{:S(2)}, u32[]{:S(2)}) async-start(bf16[128,16,768]{2,1,0:T(8,128)(2,1)} %bitcast.27), calls=%async_computation | async-start | bytes 6291456 | tf_op jit(solution)/shard_map/all_to_all | solution.py:236
  18.5 0.0 copy-done.4
  18.6 1.0 fusion
  19.6 41.1 %all-to-all-done = bf16[128,16,768]{2,1,0:T(8,128)(2,1)S(1)} async-done(((bf16[128,16,768]{2,1,0:T(8,128)(2,1)}), bf16[128,16,768]{2,1,0:T(8,128)(2,1)S(1)}, u32[]{:S(2)}, u32[]{:S(2)}) %all-to-all-start) | async-done | bytes 3145760 | tf_op jit(solution)/shard_map/all_to_all | solution.py:236
  60.7 0.0 copy-start.1
  60.7 1.7 copy-done.1
  62.4 0.0 copy-start.5
  62.4 18.0 %score.1 = (f32[8,256,1024]{2,1,0:T(8,128)}, f32[128,128]{1,0:T(8,128)}) custom-call(s32[1]{0:T(128)} %bitcast.2.offset, bf16[2048,768]{1,0:T(8,128)(2,1)} %bitcast.25, bf16[6,256,128]{2,1,0:T(8,128)(2,1)} %get-tuple-element.17.high, bf16[6,256,128]{2,1,0:T(8,128)(2,1)} %get-tuple-element.16.low, s32[32,96,1024]{2,1,0:T(8,128)} %codes.3), custom_call_target="tpu_custom_call" | custom-call | tf_op jit(solution)/shard_map/score/pallas_call | solution.py:285
  80.4 3.5 %all-to-all-start.1 = ((f32[128,1,128]{2,1,0:T(1,128)}), f32[128,1,128]{2,1,0:T(1,128)S(1)}, u32[]{:S(2)}, u32[]{:S(2)}) async-start(f32[128,1,128]{2,1,0:T(1,128)} %bitcast.36), calls=%async_computation.1 | async-start | bytes 131072 | tf_op jit(solution)/shard_map/all_to_all | solution.py:236
  83.9 0.0 copy-done
  84.0 0.0 copy-done.5
  84.0 0.8 copy.13.probes
  84.8 0.7 copy.14.targets_wide
  85.5 5.3 %home.1 = (bf16[256,2048]{1,0:T(8,128)(2,1)}, bf16[16,128,256]{2,1,0:T(8,128)(2,1)}, f32[128,128]{1,0:T(8,128)}) custom-call(s32[4,256]{1,0:T(4,128)} %bitcast.38, s32[256,4]{1,0:T(8,128)} %copy.13.probes, s32[256,128]{1,0:T(8,128)} %copy.14.targets_wide), custom_call_target="tpu_custom_call" | custom-call | tf_op jit(solution)/shard_map/home/pallas_call | solution.py:270
  90.8 3.2 %all-to-all-done.1 = f32[128,1,128]{2,1,0:T(1,128)S(1)} async-done(((f32[128,1,128]{2,1,0:T(1,128)}), f32[128,1,128]{2,1,0:T(1,128)S(1)}, u32[]{:S(2)}, u32[]{:S(2)}) %all-to-all-start.1) | async-done | bytes 65568 | tf_op jit(solution)/shard_map/all_to_all | solution.py:236
  94.0 0.0 copy-start.3
  94.0 0.6 copy-done.3
  94.6 3.5 %weigh.1 = f32[128,256]{1,0:T(8,128)} custom-call(f32[128,128]{1,0:T(8,128)} %bitcast.32, bf16[16,128,256]{2,1,0:T(8,128)(2,1)} %get-tuple-element.12.masks, f32[128,128]{1,0:T(8,128)} %get-tuple-element.13.notes), custom_call_target="tpu_custom_call" | custom-call | tf_op jit(solution)/shard_map/weigh/pallas_call | solution.py:305
  98.1 1.0 copy.17
  99.1 16.8 %all_to_all.59 = f32[128,1,256]{2,1,0:T(1,128)S(1)} all-to-all(f32[128,1,256]{2,1,0:T(1,128)S(1)} %copy.17), channel_id=1, replica_groups=mesh['corpus'=32,'query'=4] {'corpus','query'}, dimensions={0} | all-to-all | bytes 262144 | tf_op jit(solution)/shard_map/all_to_all | solution.py:236
  115.9 0.6 copy.21
  116.6 31.7 %grad.1 = (bf16[2048,768]{1,0:T(8,128)(2,1)}, f32[16,768]{1,0:T(8,128)}) custom-call(s32[1]{0:T(128)} %bitcast.2.offset, f32[8,256,1024]{2,1,0:T(8,128)} %get-tuple-element.10.exps, f32[128,256]{1,0:T(8,128)} %bitcast.30, s32[32,96,1024]{2,1,0:T(8,128)} %codes.3, bf16[2048,768]{1,0:T(8,128)(2,1)} %bitcast.26, bf16[6,256,128]{2,1,0:T(8,128)(2,1)} %get-tuple-element.17.high, ...), custom_call_target="tpu_custom_call" | custom-call | tf_op jit(solution)/shard_map/grad/pallas_call | solution.py:311
  148.3 0.9 all_to_all.50
  149.2 13.7 %all_to_all.60 = f32[128,1,96]{2,1,0:T(1,128)S(1)} all-to-all(f32[128,1,96]{2,1,0:T(1,128)S(1)} %bitcast.34), channel_id=1, replica_groups=mesh['corpus'=32,'query'=4] {'corpus','query'}, dimensions={0} | all-to-all | bytes 98304 | tf_op jit(solution)/shard_map/all_to_all | solution.py:236
  162.9 0.2 reduce_sum.18
  163.1 13.8 %all_to_all.61 = f32[128,1,96]{2,1,0:T(1,128)S(1)} all-to-all(f32[128,1,96]{2,1,0:T(1,128)S(1)} %broadcast_in_dim.42), channel_id=1, replica_groups=mesh['corpus'=32,'query'=4] {'corpus','query'}, dimensions={0} | all-to-all | bytes 98304 | tf_op jit(solution)/shard_map/all_to_all | solution.py:236
  176.8 4.1 %all-to-all-start.3 = ((bf16[128,16,768]{2,1,0:T(8,128)(2,1)}), bf16[128,16,768]{2,1,0:T(8,128)(2,1)S(1)}, u32[]{:S(2)}, u32[]{:S(2)}) async-start(bf16[128,16,768]{2,1,0:T(8,128)(2,1)} %bitcast.29), calls=%async_computation.3 | async-start | bytes 6291456 | tf_op jit(solution)/shard_map/all_to_all | solution.py:236
  180.9 0.7 multiply_reduce_fusion.1
  182.3 0.2 multiply_reduce_fusion
  182.5 0.7 mul.21
  183.2 39.9 %all-to-all-done.3 = bf16[128,16,768]{2,1,0:T(8,128)(2,1)S(1)} async-done(((bf16[128,16,768]{2,1,0:T(8,128)(2,1)}), bf16[128,16,768]{2,1,0:T(8,128)(2,1)S(1)}, u32[]{:S(2)}, u32[]{:S(2)}) %all-to-all-start.3) | async-done | bytes 3145760 | tf_op jit(solution)/shard_map/all_to_all | solution.py:236
  223.1 0.0 copy-start.2
  223.1 1.6 copy-done.2
  224.7 4.4 %combine.1 = bf16[256,768]{1,0:T(8,128)(2,1)} custom-call(bf16[256,2048]{1,0:T(8,128)(2,1)} %get-tuple-element.9.chosen, bf16[2048,768]{1,0:T(8,128)(2,1)} %bitcast.28), custom_call_target="tpu_custom_call" | custom-call | tf_op jit(solution)/shard_map/combine/pallas_call | solution.py:343
  (7 shorter events, 0.1 us)
Async XLA Ops:
  0.6 83.3 %copy-start = (s32[256,8]{0,1:T(8,128)S(1)}, s32[256,8]{0,1:T(8,128)}, u32[]{:S(2)}) copy-start(s32[256,8]{0,1:T(8,128)} %param.7) | copy-start | bytes 24580
  7.0 11.5 %copy-start.4 = (f32[16,768]{1,0:T(8,128)S(1)}, f32[16,768]{1,0:T(8,128)}, u32[]{:S(2)}) copy-start(f32[16,768]{1,0:T(8,128)} %param.9) | copy-start | bytes 147460
  7.0 53.7 %all-to-all-start = ((bf16[128,16,768]{2,1,0:T(8,128)(2,1)}), bf16[128,16,768]{2,1,0:T(8,128)(2,1)S(1)}, u32[]{:S(2)}, u32[]{:S(2)}) async-start(bf16[128,16,768]{2,1,0:T(8,128)(2,1)} %bitcast.27), calls=%async_computation | async-start | bytes 6291456 | tf_op jit(solution)/shard_map/all_to_all | solution.py:236
  60.7 1.7 copy-start.1
  62.4 21.6 %copy-start.5 = (s32[256,4]{0,1:T(4,128)S(1)}, s32[256,4]{0,1:T(4,128)}, u32[]{:S(2)}) copy-start(s32[256,4]{0,1:T(4,128)} %param.6) | copy-start | bytes 12292
  80.4 13.6 %all-to-all-start.1 = ((f32[128,1,128]{2,1,0:T(1,128)}), f32[128,1,128]{2,1,0:T(1,128)S(1)}, u32[]{:S(2)}, u32[]{:S(2)}) async-start(f32[128,1,128]{2,1,0:T(1,128)} %bitcast.36), calls=%async_computation.1 | async-start | bytes 131072 | tf_op jit(solution)/shard_map/all_to_all | solution.py:236
  94.0 0.6 copy-start.3
  176.8 46.3 %all-to-all-start.3 = ((bf16[128,16,768]{2,1,0:T(8,128)(2,1)}), bf16[128,16,768]{2,1,0:T(8,128)(2,1)S(1)}, u32[]{:S(2)}, u32[]{:S(2)}) async-start(bf16[128,16,768]{2,1,0:T(8,128)(2,1)} %bitcast.29), calls=%async_computation.3 | async-start | bytes 6291456 | tf_op jit(solution)/shard_map/all_to_all | solution.py:236
  223.1 1.6 copy-start.2

commit v2 on v1

v2 whole, which is shorter than its diff:
```python
import jax
import jax.numpy as jnp
from jax import lax
from jax.experimental import pallas as pl
from jax.experimental.pallas import tpu as pltpu
from jax.sharding import PartitionSpec as P


D = 768
SUBSPACES = 96
CENTROIDS = 16
SUBDIM = 8
PASSAGES = 1024
PROBES = 4
TARGETS = 8
CAP = 2
EPSILON = 1e-06

BOTH = ("corpus", "query")
CHUNKS = 6
FEATS = 128
ENTRIES = 256
WIDTH = SUBSPACES * CENTROIDS
OWN = 8
SLOTS = OWN * CAP
F32 = jnp.float32
BF16 = jnp.bfloat16


def dot(a, b, dims=((1,), (0,))):
    return lax.dot_general(a, b, (dims, ((), ())), preferred_element_type=F32)


def iota(shape, axis):
    return lax.broadcasted_iota(jnp.int32, shape, axis)


def ones_where(mask):
    return jnp.where(mask, 1.0, 0.0).astype(BF16)


def split_two(value):
    high = value.astype(BF16)
    return high, (value - high.astype(F32)).astype(BF16)


def names_list(probe_rows, lists):
    found = probe_rows[0:1, :] == lists
    for p in range(1, PROBES):
        found = found | (probe_rows[p : p + 1, :] == lists)
    return found


def dispatch_body(probes_t, queries, sending):
    count = queries.shape[0]
    rows = sending.shape[0] // CAP
    lists = iota((rows, count), 0) + pl.program_id(0) * rows
    found = names_list(probes_t[...], lists)
    before = ones_where(iota((count, count), 0) < iota((count, count), 1))
    rank = dot(ones_where(found), before)
    chosen = [
        jnp.where(found & (rank == float(r)), 1.0, 0.0).reshape(rows // OWN, 1, OWN, count)
        for r in range(CAP)
    ]
    chosen = jnp.concatenate(chosen, axis=1).reshape(rows * CAP, count).astype(BF16)
    sending[...] = dot(chosen, queries[...]).astype(BF16)


def home_body(probes_t, probes, targets_wide, chosen_out, masks_out, notes_out):
    count = probes.shape[0]
    slots = chosen_out.shape[1]
    devices = notes_out.shape[0]
    block = 512
    after = ones_where(iota((count, count), 0) > iota((count, count), 1))
    for b in range(slots // block):
        slot = iota((count, block), 1) + b * block
        lists = (slot // SLOTS) * OWN + (slot & (OWN - 1))
        found = probes[:, 0:1] == lists
        for p in range(1, PROBES):
            found = found | (probes[:, p : p + 1] == lists)
        rank = dot(after, ones_where(found))
        wanted = ((slot // OWN) & 1).astype(F32)
        chosen_out[:, b * block : (b + 1) * block] = ones_where(found & (rank == wanted))
    wide = targets_wide[...]
    spot = wide & (PASSAGES - 1)
    column = wide // PASSAGES
    in_list = jnp.broadcast_to(probes[:, 0:1], wide.shape)
    for p in range(1, PROBES):
        in_list = jnp.where(column == p, probes[:, p : p + 1], in_list)
    parts = jnp.concatenate(
        [in_list >> 5, in_list & 31, spot >> 5, spot & 31], axis=1
    ).astype(F32).astype(BF16)
    before = ones_where(iota((count, count), 0) < iota((count, count), 1))
    lane = iota((devices, 128), 1)
    gathered = jnp.zeros((devices, 4 * 128), F32)
    lane_wide = iota((devices, 4 * 128), 1) & 127
    for i in range(OWN):
        found = names_list(probes_t[...], iota((devices, count), 0) * OWN + i)
        rank = dot(ones_where(found), before)
        for r in range(CAP):
            mask = ones_where(found & (rank == float(r)))
            masks_out[r * OWN + i] = mask
            here = dot(mask, parts)
            gathered = jnp.where(lane_wide // TARGETS == r * OWN + i, here, gathered)
    got_list = gathered[:, 0:128] * 32.0 + gathered[:, 128:256]
    got_spot = gathered[:, 256:384] * 32.0 + gathered[:, 384:512]
    own_list = iota((devices, 128), 0) * OWN + ((lane // TARGETS) & (OWN - 1))
    notes_out[...] = jnp.where(got_list == own_list.astype(F32), got_spot + 1.0, 0.0)


def one_hot_body(offset, codes, one_hot):
    for c in range(CHUNKS):
        part = codes[0, c * 16 : (c + 1) * 16, :].astype(F32).astype(BF16)
        for k in range(CENTROIDS):
            at = c * ENTRIES + k * 16
            one_hot[0, at : at + 16, :] = jnp.where(
                part == jnp.asarray(k, BF16), jnp.asarray(1, BF16), jnp.asarray(0, BF16)
            )


def score_body(got, high, low, one_hot, masks, exps, stats, table):
    i = pl.program_id(0)
    half = stats.shape[0]

    @pl.when(i == 0)
    def _():
        stats[...] = jnp.zeros_like(stats)
        for c in range(CHUNKS):
            rows = got[:, c * FEATS : (c + 1) * FEATS]
            twice = jnp.concatenate([rows, rows], axis=1)
            weights = jnp.concatenate([high[c], low[c]], axis=1)
            looked = dot(twice, weights, ((1,), (1,)))
            table[2 * c] = looked[:, 0:128]
            table[2 * c + 1] = looked[:, 128:256]

    rows = jnp.concatenate(
        [
            jnp.concatenate(
                [
                    table[j, pl.ds(r * OWN + i, half, stride=SLOTS), :].astype(BF16)
                    for j in range(WIDTH // 128)
                ],
                axis=1,
            )
            for r in range(CAP)
        ],
        axis=0,
    )
    scores = dot(rows, one_hot[0])
    top = jnp.max(scores, axis=1, keepdims=True)
    exp_scores = jnp.exp(scores - top)
    total = jnp.sum(exp_scores, axis=1, keepdims=True)
    exps[0] = exp_scores
    lane = iota(stats.shape, 1)
    held = stats[...]
    for r in range(CAP):
        at = r * OWN + i
        held = jnp.where(lane == at, top[r * half : (r + 1) * half], held)
        held = jnp.where(lane == SLOTS + at, total[r * half : (r + 1) * half], held)
    stats[...] = held


def weight_body(stats, masks, notes, message):
    devices, count = masks.shape[1:]
    low = -3.0e38
    peak = jnp.full((devices, count), low, F32)
    for s in range(SLOTS):
        peak = jnp.maximum(peak, jnp.where(masks[s] > 0, stats[:, s : s + 1], low))
    peak = jnp.max(peak, axis=0, keepdims=True)
    denom = jnp.zeros((devices, count), F32)
    for s in range(SLOTS):
        part = jnp.exp(stats[:, s : s + 1] - peak) * stats[:, SLOTS + s : SLOTS + 1 + s]
        denom = denom + jnp.where(masks[s] > 0, part, 0.0)
    denom = jnp.sum(denom, axis=0, keepdims=True)
    lane = iota((devices, 128), 1)
    held = jnp.zeros((devices, 128), F32)
    for s in range(SLOTS):
        part = jnp.exp(stats[:, s : s + 1] - peak) / denom
        part = jnp.sum(jnp.where(masks[s] > 0, part, 0.0), axis=1, keepdims=True)
        held = jnp.where(lane == s, part, held)
    message[...] = jnp.stack([held, notes[...]], axis=1).reshape(message.shape)


def grad_body(exps, message, one_hot, got, high, low, part_out, book_out, hist):
    i = pl.program_id(0)
    half = message.shape[0] // 2
    lane = iota((half, 128), 1)
    weights = message[pl.ds(0, half, stride=2), :]
    turned = pltpu.roll(message[pl.ds(1, half, stride=2), :], (128 - TARGETS * i) % 128, 1)
    place = iota((half, PASSAGES), 1).astype(F32)
    grads = []
    for r in range(CAP):
        scale = jnp.sum(jnp.where(lane == r * OWN + i, weights, 0.0), axis=1, keepdims=True)
        teacher = jnp.zeros((half, PASSAGES), F32)
        for t in range(TARGETS):
            at = r * OWN * TARGETS + t
            weight = 2.0 * (TARGETS - t) / (TARGETS * (TARGETS + 1.0))
            teacher = jnp.where(place == turned[:, at : at + 1] - 1.0, weight, teacher)
        student = exps[0, r * half : (r + 1) * half, :] * scale
        grads.append((student - teacher).astype(BF16))
    grads = jnp.concatenate(grads, axis=0)
    found = dot(grads, one_hot[0], ((1,), (1,)))
    for r in range(CAP):
        for j in range(WIDTH // 128):
            hist[j, pl.ds(r * OWN + i, half, stride=SLOTS), :] = found[
                r * half : (r + 1) * half, j * 128 : (j + 1) * 128
            ]

    @pl.when(i == pl.num_programs(0) - 1)
    def _():
        keep = iota((ENTRIES, FEATS), 0) % 16 == iota((ENTRIES, FEATS), 1) // SUBDIM
        for c in range(CHUNKS):
            h_high, h_low = split_two(jnp.concatenate([hist[2 * c], hist[2 * c + 1]], axis=1))
            both = jnp.concatenate([high[c], low[c]], axis=1)
            wide = dot(h_high, both)
            part = wide[:, 0:FEATS] + wide[:, FEATS:] + dot(h_low, high[c])
            part_out[:, c * FEATS : (c + 1) * FEATS] = part.astype(BF16)
            book = dot(got[:, c * FEATS : (c + 1) * FEATS], h_high, ((0,), (0,)))
            book = jnp.where(keep, book.T, 0.0)
            book_out[:, c * FEATS : (c + 1) * FEATS] = jnp.sum(
                book.reshape(CENTROIDS, 16, FEATS), axis=1
            )


def norm_body(raw, normed):
    value = raw[...]
    mean = jnp.sum(value * value, keepdims=True) / (CENTROIDS * D)
    normed[...] = value * lax.rsqrt(mean + EPSILON)


def combine_body(chosen, returned, out):
    out[...] = dot(chosen[...], returned[...]).astype(BF16)


def whole(shape):
    return pl.BlockSpec(shape, lambda *_: (0,) * len(shape))


def exchange(value):
    return lax.all_to_all(value, BOTH, 0, 0, tiled=True)


def sum_everywhere(value, devices):
    step = 1
    while step < devices:
        other = lax.ppermute(value, BOTH, [(d, d ^ step) for d in range(devices)])
        value = value + other
        step *= 2
    return value


def spread_codebook(codebook):
    book = codebook.reshape(CENTROIDS, CHUNKS, FEATS).transpose(1, 0, 2)
    own = jnp.arange(16)[:, None] == jnp.arange(FEATS)[None, :] // SUBDIM
    spread = jnp.where(own[None, None], book[:, :, None, :], 0.0)
    spread = spread.reshape(CHUNKS, ENTRIES, FEATS)
    high = lax.reduce_precision(spread, 8, 7)
    return high.astype(BF16), (spread - high).astype(BF16)


def shards(queries, probes, targets, passage_codes, codebook):
    devices = lax.axis_size("corpus") * lax.axis_size("query")
    count = queries.shape[0]
    slots = devices * SLOTS
    list_rows = devices * CAP
    probes_t = probes.T
    big = pltpu.CompilerParams(
        dimension_semantics=("arbitrary",), vmem_limit_bytes=58 * 1024 * 1024
    )
    square = jax.ShapeDtypeStruct((devices, 128), F32)

    sending = pl.pallas_call(
        dispatch_body,
        out_shape=jax.ShapeDtypeStruct((slots, D), BF16),
        grid=(4,),
        in_specs=[whole((PROBES, count)), whole((count, D))],
        out_specs=pl.BlockSpec((slots // 4, D), lambda b: (b, 0)),
        name="dispatch",
    )(probes_t, queries)
    got = exchange(sending)

    chosen, masks, notes = pl.pallas_call(
        home_body,
        out_shape=(
            jax.ShapeDtypeStruct((count, slots), BF16),
            jax.ShapeDtypeStruct((SLOTS, devices, count), BF16),
            square,
        ),
        name="home",
    )(probes_t, probes, jnp.tile(targets, (1, 128 // TARGETS)))
    high, low = spread_codebook(codebook)
    offset = (lax.axis_index("query") * OWN).astype(jnp.int32).reshape(1)
    one_hot = pl.pallas_call(
        one_hot_body,
        out_shape=jax.ShapeDtypeStruct((OWN, WIDTH, PASSAGES), BF16),
        grid_spec=pltpu.PrefetchScalarGridSpec(
            num_scalar_prefetch=1,
            grid=(OWN,),
            in_specs=[
                pl.BlockSpec((1, SUBSPACES, PASSAGES), lambda i, off: (off[0] + i, 0, 0))
            ],
            out_specs=pl.BlockSpec((1, WIDTH, PASSAGES), lambda i, off: (i, 0, 0)),
        ),
        name="one_hot",
    )(offset, passage_codes)

    by_list = lambda *shape: pl.BlockSpec((1,) + shape, lambda i: (i, 0, 0))
    exps_spec = by_list(list_rows, PASSAGES)
    one_hot_spec = by_list(WIDTH, PASSAGES)
    table_spec = whole((CHUNKS, ENTRIES, FEATS))
    per_list = jax.ShapeDtypeStruct((OWN, list_rows, PASSAGES), F32)
    scratch = [pltpu.VMEM((WIDTH // 128, slots, 128), F32)]

    exps, stats = pl.pallas_call(
        score_body,
        out_shape=(per_list, square),
        grid=(OWN,),
        in_specs=[
            whole((slots, D)),
            table_spec,
            table_spec,
            one_hot_spec,
            pl.BlockSpec(memory_space=pl.ANY),
        ],
        out_specs=[exps_spec, whole(square.shape)],
        scratch_shapes=scratch,
        compiler_params=big,
        name="score",
    )(got, high, low, one_hot, masks)

    message = pl.pallas_call(
        weight_body, out_shape=jax.ShapeDtypeStruct((2 * devices, 128), F32), name="weigh"
    )(exchange(stats), masks, notes)

    partial_value, book = pl.pallas_call(
        grad_body,
        out_shape=(
            jax.ShapeDtypeStruct((slots, D), BF16),
            jax.ShapeDtypeStruct((CENTROIDS, D), F32),
        ),
        grid=(OWN,),
        in_specs=[
            exps_spec,
            whole((2 * devices, 128)),
            one_hot_spec,
            whole((slots, D)),
            table_spec,
            table_spec,
        ],
        out_specs=[whole((slots, D)), whole((CENTROIDS, D))],
        scratch_shapes=scratch,
        compiler_params=big,
        name="grad",
    )(exps, exchange(message), one_hot, got, high, low)

    normed = pl.pallas_call(
        norm_body, out_shape=jax.ShapeDtypeStruct((CENTROIDS, D), F32), name="book_norm"
    )(sum_everywhere(book, devices))

    grad_queries = pl.pallas_call(
        combine_body,
        out_shape=jax.ShapeDtypeStruct((count, D), BF16),
        grid=(3,),
        in_specs=[whole((count, slots)), pl.BlockSpec((slots, D // 3), lambda b: (0, b))],
        out_specs=pl.BlockSpec((count, D // 3), lambda b: (0, b)),
        name="combine",
    )(chosen, exchange(partial_value))
    return grad_queries, normed


def solution(mesh):
    placed = (
        P(BOTH, None),
        P(BOTH, None),
        P(BOTH, None),
        P("corpus", None, None),
        P(),
    )

    return jax.shard_map(
        shards,
        mesh=mesh,
        in_specs=placed,
        out_specs=(P(BOTH, None), P()),
        check_vma=False,
    )
```

time: 230 us -> 223 us (0.970)
  the two profiles are of different devices: /device:TPU:1 before, /device:TPU:0 now
where the time goes in v2:
time: 223 us; the launch traced here: 222 us
  Pallas kernels  83.2 us (37%)
  waiting for transfers between devices  71.6 us (32%)
  blocking collectives  29.9 us (13%)
  starting transfers between devices  29.6 us (13%)
  local copies, waits for them, and re-layouts  4.91 us (2%)
    ppermute x7, waiting for transfers between devices, sum_everywhere(): other = lax.ppermute(value, BOTH, [(d, d ^ step) for d in range(devices)])  49 us
    pallas_call x1, Pallas kernels, shards(): pl.pallas_call(grad_body, out_shape=(jax.ShapeDtypeStruct((slots, D), BF1...  31.7 us
    all_to_all x2, blocking collectives, exchange(): return lax.all_to_all(value, BOTH, 0, 0, tiled=True)  29.9 us
    all_to_all x2, waiting for transfers between devices, exchange(): return lax.all_to_all(value, BOTH, 0, 0, tiled=True)  22.6 us
    pallas_call x1, Pallas kernels, shards(): pl.pallas_call(score_body, out_shape=(per_list, square), grid=(OWN,), in_...  21.6 us
    all_to_all x2, starting transfers between devices, exchange(): return lax.all_to_all(value, BOTH, 0, 0, tiled=True)  16 us
    ppermute x7, starting transfers between devices, sum_everywhere(): other = lax.ppermute(value, BOTH, [(d, d ^ step) for d in range(devices)])  13.6 us
    pallas_call x1, Pallas kernels, shards(): pl.pallas_call(one_hot_body, out_shape=jax.ShapeDtypeStruct((OWN, WIDTH,...  10.7 us
  transfers between devices with their start and end apart: 9, of which 8 were waited for; matrix products, arithmetic and copies ran while one was open for 1% of the time, Pallas kernels for 8%

profile of v2, /device:TPU:0, one launch (start us, length us, event | category | flops | bytes accessed | tf_op | source)
XLA Modules:
  0.0 221.7 jit_solution(10264827488179960132)
XLA Ops:
  0.6 0.0 copy-start
  0.6 4.5 %dispatch.1 = bf16[2048,768]{1,0:T(8,128)(2,1)} custom-call(s32[4,256]{1,0:T(4,128)} %bitcast.33, bf16[256,768]{1,0:T(8,128)(2,1)} %queries.1), custom_call_target="tpu_custom_call" | custom-call | tf_op jit(solution)/shard_map/dispatch/pallas_call | solution.py:272
  5.1 0.0 copy-start.5
  5.1 0.0 copy-start.3
  5.1 11.2 %all-to-all-start = ((bf16[128,16,768]{2,1,0:T(8,128)(2,1)}), bf16[128,16,768]{2,1,0:T(8,128)(2,1)S(1)}, u32[]{:S(2)}, u32[]{:S(2)}) async-start(bf16[128,16,768]{2,1,0:T(8,128)(2,1)} %bitcast.25), calls=%async_computation | async-start | bytes 6291456 | tf_op jit(solution)/shard_map/all_to_all | solution.py:240
  16.3 0.0 copy-done.5
  16.3 0.8 copy.13.probes
  17.1 0.0 copy-done.3
  17.2 0.0 copy-done
  17.2 0.7 copy.14.targets_wide
  18.0 1.0 fusion
  19.0 5.3 %home.1 = (bf16[256,2048]{1,0:T(8,128)(2,1)}, bf16[16,128,256]{2,1,0:T(8,128)(2,1)}, f32[128,128]{1,0:T(8,128)}) custom-call(s32[4,256]{1,0:T(4,128)} %bitcast.34, s32[256,4]{1,0:T(8,128)} %copy.13.probes, s32[256,128]{1,0:T(8,128)} %copy.14.targets_wide), custom_call_target="tpu_custom_call" | custom-call | tf_op jit(solution)/shard_map/home/pallas_call | solution.py:282
  24.3 10.7 %one_hot.1 = bf16[8,1536,1024]{2,1,0:T(8,128)(2,1)} custom-call(s32[1]{0:T(128)} %bitcast.7.offset, s32[32,96,1024]{2,1,0:T(8,128)} %codes.1), custom_call_target="tpu_custom_call" | custom-call | tf_op jit(solution)/shard_map/one_hot/pallas_call | solution.py:293
  35.0 22.6 %all-to-all-done = bf16[128,16,768]{2,1,0:T(8,128)(2,1)S(1)} async-done(((bf16[128,16,768]{2,1,0:T(8,128)(2,1)}), bf16[128,16,768]{2,1,0:T(8,128)(2,1)S(1)}, u32[]{:S(2)}, u32[]{:S(2)}) %all-to-all-start) | async-done | bytes 3145760 | tf_op jit(solution)/shard_map/all_to_all | solution.py:240
  57.6 0.0 copy-start.1
  57.6 1.6 copy-done.1
  59.2 21.6 %score.1 = (f32[8,256,1024]{2,1,0:T(8,128)}, f32[128,128]{1,0:T(8,128)}) custom-call(bf16[2048,768]{1,0:T(8,128)(2,1)} %bitcast.22, bf16[6,256,128]{2,1,0:T(8,128)(2,1)} %get-tuple-element.17.high, bf16[6,256,128]{2,1,0:T(8,128)(2,1)} %get-tuple-element.16.low, bf16[8,1536,1024]{2,1,0:T(8,128)(2,1)} %one_hot.1, bf16[16,128,256]{2,1,0:T(8,128)(2,1)} %get-tuple-element.10.masks), custom_call_target="tpu_custom_call" | custom-call | tf_op jit(solution)/shard_map/score/pallas_call | solution.py:314
  80.9 14.9 %all_to_all.44 = f32[128,1,128]{2,1,0:T(1,128)} all-to-all(f32[128,1,128]{2,1,0:T(1,128)} %bitcast.32), channel_id=1, replica_groups=mesh['corpus'=32,'query'=4] {'corpus','query'}, dimensions={0} | all-to-all | bytes 131072 | tf_op jit(solution)/shard_map/all_to_all | solution.py:240
  95.7 3.6 %weigh.1 = f32[256,128]{1,0:T(8,128)} custom-call(f32[128,128]{1,0:T(8,128)} %bitcast.29, bf16[16,128,256]{2,1,0:T(8,128)(2,1)} %get-tuple-element.10.masks, f32[128,128]{1,0:T(8,128)} %get-tuple-element.13.notes), custom_call_target="tpu_custom_call" | custom-call | tf_op jit(solution)/shard_map/weigh/pallas_call | solution.py:331
  99.3 15.0 %all_to_all.45 = f32[128,2,128]{2,1,0:T(2,128)} all-to-all(f32[128,2,128]{2,1,0:T(2,128)} %bitcast.28), channel_id=1, replica_groups=mesh['corpus'=32,'query'=4] {'corpus','query'}, dimensions={0} | all-to-all | bytes 262144 | tf_op jit(solution)/shard_map/all_to_all | solution.py:240
  114.3 31.7 %grad.1 = (bf16[2048,768]{1,0:T(8,128)(2,1)}, f32[16,768]{1,0:T(8,128)}) custom-call(f32[8,256,1024]{2,1,0:T(8,128)} %get-tuple-element.11.exps, f32[256,128]{1,0:T(8,128)} %bitcast.27, bf16[8,1536,1024]{2,1,0:T(8,128)(2,1)} %one_hot.1, bf16[2048,768]{1,0:T(8,128)(2,1)} %bitcast.23, bf16[6,256,128]{2,1,0:T(8,128)(2,1)} %get-tuple-element.17.high, ...), custom_call_target="tpu_custom_call" | custom-call | tf_op jit(solution)/shard_map/grad/pallas_call | solution.py:335
  146.0 0.0 copy-start.4
  146.0 4.8 %all-to-all-start.3 = ((bf16[128,16,768]{2,1,0:T(8,128)(2,1)}), bf16[128,16,768]{2,1,0:T(8,128)(2,1)S(1)}, u32[]{:S(2)}, u32[]{:S(2)}) async-start(bf16[128,16,768]{2,1,0:T(8,128)(2,1)} %bitcast.26), calls=%async_computation.3 | async-start | bytes 6291456 | tf_op jit(solution)/shard_map/all_to_all | solution.py:240
  150.8 0.0 copy-done.4
  150.8 1.0 collective-permute-start
  151.8 35.0 %collective-permute-done = f32[16,768]{1,0:T(8,128)S(1)} collective-permute-done((f32[16,768]{1,0:T(8,128)S(1)}, f32[16,768]{1,0:T(8,128)S(1)}, u32[]{:S(2)}, u32[]{:S(2)}) %collective-permute-start) | collective-permute-done | bytes 49184 | tf_op jit(solution)/shard_map/ppermute | solution.py:246
  186.8 2.7 %collective-permute-start.1 = (f32[16,768]{1,0:T(8,128)S(1)}, f32[16,768]{1,0:T(8,128)S(1)}, u32[]{:S(2)}, u32[]{:S(2)}) collective-permute-start(f32[16,768]{1,0:T(8,128)S(1)} %add.27), channel_id=1, source_target_pairs={{0,2},{1,3},{2,0},{3,1},{4,6},{5,7},{6,4},{7,5},{8,10},{9,11},{10,... | collective-permute-start | bytes 147464 | tf_op jit(solution)/shard_map/ppermute | solution.py:246
  189.6 2.9 %collective-permute-done.1 = f32[16,768]{1,0:T(8,128)S(1)} collective-permute-done((f32[16,768]{1,0:T(8,128)S(1)}, f32[16,768]{1,0:T(8,128)S(1)}, u32[]{:S(2)}, u32[]{:S(2)}) %collective-permute-start.1) | collective-permute-done | bytes 49184 | tf_op jit(solution)/shard_map/ppermute | solution.py:246
  192.5 0.1 collective-permute-start.2
  192.6 1.2 collective-permute-done.2
  193.8 1.7 collective-permute-start.3
  195.5 2.5 %collective-permute-done.3 = f32[16,768]{1,0:T(8,128)S(1)} collective-permute-done((f32[16,768]{1,0:T(8,128)S(1)}, f32[16,768]{1,0:T(8,128)S(1)}, u32[]{:S(2)}, u32[]{:S(2)}) %collective-permute-start.3) | collective-permute-done | bytes 49184 | tf_op jit(solution)/shard_map/ppermute | solution.py:246
  198.0 3.5 %collective-permute-start.4 = (f32[16,768]{1,0:T(8,128)S(1)}, f32[16,768]{1,0:T(8,128)S(1)}, u32[]{:S(2)}, u32[]{:S(2)}) collective-permute-start(f32[16,768]{1,0:T(8,128)S(1)} %add.30), channel_id=1, source_target_pairs={{0,16},{1,17},{2,18},{3,19},{4,20},{5,21},{6,22},{7,23},{8,24},{9,... | collective-permute-start | bytes 147464 | tf_op jit(solution)/shard_map/ppermute | solution.py:246
  201.4 2.2 collective-permute-done.4
  203.6 1.5 collective-permute-start.5
  205.2 2.6 %collective-permute-done.5 = f32[16,768]{1,0:T(8,128)S(1)} collective-permute-done((f32[16,768]{1,0:T(8,128)S(1)}, f32[16,768]{1,0:T(8,128)S(1)}, u32[]{:S(2)}, u32[]{:S(2)}) %collective-permute-start.5) | collective-permute-done | bytes 49184 | tf_op jit(solution)/shard_map/ppermute | solution.py:246
  207.8 3.1 %collective-permute-start.6 = (f32[16,768]{1,0:T(8,128)S(1)}, f32[16,768]{1,0:T(8,128)S(1)}, u32[]{:S(2)}, u32[]{:S(2)}) collective-permute-start(f32[16,768]{1,0:T(8,128)S(1)} %add.32), channel_id=1, source_target_pairs={{0,64},{1,65},{2,66},{3,67},{4,68},{5,69},{6,70},{7,71},{8,72},{9,... | collective-permute-start | bytes 147464 | tf_op jit(solution)/shard_map/ppermute | solution.py:246
  210.9 2.6 %collective-permute-done.6 = f32[16,768]{1,0:T(8,128)S(1)} collective-permute-done((f32[16,768]{1,0:T(8,128)S(1)}, f32[16,768]{1,0:T(8,128)S(1)}, u32[]{:S(2)}, u32[]{:S(2)}) %collective-permute-start.6) | collective-permute-done | bytes 49184 | tf_op jit(solution)/shard_map/ppermute | solution.py:246
  213.5 0.6 add.33.raw
  214.1 1.6 book_norm.1
  215.7 0.0 all-to-all-done.3
  215.7 0.0 copy-start.2
  215.7 1.7 copy-done.2
  217.3 4.4 %combine.1 = bf16[256,768]{1,0:T(8,128)(2,1)} custom-call(bf16[256,2048]{1,0:T(8,128)(2,1)} %get-tuple-element.9.chosen, bf16[2048,768]{1,0:T(8,128)(2,1)} %bitcast.24), custom_call_target="tpu_custom_call" | custom-call | tf_op jit(solution)/shard_map/combine/pallas_call | solution.py:360
  (12 shorter events, 0.1 us)
Async XLA Ops:
  0.6 16.5 %copy-start = (s32[256,8]{0,1:T(8,128)S(1)}, s32[256,8]{0,1:T(8,128)}, u32[]{:S(2)}) copy-start(s32[256,8]{0,1:T(8,128)} %param.7) | copy-start | bytes 24580
  5.1 11.2 %copy-start.5 = (s32[256,4]{0,1:T(4,128)S(1)}, s32[256,4]{0,1:T(4,128)}, u32[]{:S(2)}) copy-start(s32[256,4]{0,1:T(4,128)} %param.6) | copy-start | bytes 12292
  5.1 12.0 %copy-start.3 = (f32[16,768]{1,0:T(8,128)S(1)}, f32[16,768]{1,0:T(8,128)}, u32[]{:S(2)}) copy-start(f32[16,768]{1,0:T(8,128)} %param.9) | copy-start | bytes 147460
  5.1 52.5 %all-to-all-start = ((bf16[128,16,768]{2,1,0:T(8,128)(2,1)}), bf16[128,16,768]{2,1,0:T(8,128)(2,1)S(1)}, u32[]{:S(2)}, u32[]{:S(2)}) async-start(bf16[128,16,768]{2,1,0:T(8,128)(2,1)} %bitcast.25), calls=%async_computation | async-start | bytes 6291456 | tf_op jit(solution)/shard_map/all_to_all | solution.py:240
  57.6 1.6 copy-start.1
  146.0 4.8 %copy-start.4 = (f32[16,768]{1,0:T(8,128)S(1)}, f32[16,768]{1,0:T(8,128)}, u32[]{:S(2)}) copy-start(f32[16,768]{1,0:T(8,128)} %get-tuple-element.15) | copy-start | bytes 147460
  146.0 69.7 %all-to-all-start.3 = ((bf16[128,16,768]{2,1,0:T(8,128)(2,1)}), bf16[128,16,768]{2,1,0:T(8,128)(2,1)S(1)}, u32[]{:S(2)}, u32[]{:S(2)}) async-start(bf16[128,16,768]{2,1,0:T(8,128)(2,1)} %bitcast.26), calls=%async_computation.3 | async-start | bytes 6291456 | tf_op jit(solution)/shard_map/all_to_all | solution.py:240
  150.8 36.0 %collective-permute-start = (f32[16,768]{1,0:T(8,128)S(1)}, f32[16,768]{1,0:T(8,128)S(1)}, u32[]{:S(2)}, u32[]{:S(2)}) collective-permute-start(f32[16,768]{1,0:T(8,128)S(1)} %copy-done.4), channel_id=1, source_target_pairs={{0,1},{1,0},{2,3},{3,2},{4,5},{5,4},{6,7},{7,6},{8,9},{9,8},{10,11... | collective-permute-start | bytes 147464 | tf_op jit(solution)/shard_map/ppermute | solution.py:246
  186.8 5.7 %collective-permute-start.1 = (f32[16,768]{1,0:T(8,128)S(1)}, f32[16,768]{1,0:T(8,128)S(1)}, u32[]{:S(2)}, u32[]{:S(2)}) collective-permute-start(f32[16,768]{1,0:T(8,128)S(1)} %add.27), channel_id=1, source_target_pairs={{0,2},{1,3},{2,0},{3,1},{4,6},{5,7},{6,4},{7,5},{8,10},{9,11},{10,... | collective-permute-start | bytes 147464 | tf_op jit(solution)/shard_map/ppermute | solution.py:246
  192.5 1.3 collective-permute-start.2
  193.8 4.2 %collective-permute-start.3 = (f32[16,768]{1,0:T(8,128)S(1)}, f32[16,768]{1,0:T(8,128)S(1)}, u32[]{:S(2)}, u32[]{:S(2)}) collective-permute-start(f32[16,768]{1,0:T(8,128)S(1)} %add.29), channel_id=1, source_target_pairs={{0,8},{1,9},{2,10},{3,11},{4,12},{5,13},{6,14},{7,15},{8,0},{9,1},... | collective-permute-start | bytes 147464 | tf_op jit(solution)/shard_map/ppermute | solution.py:246
  198.0 5.7 %collective-permute-start.4 = (f32[16,768]{1,0:T(8,128)S(1)}, f32[16,768]{1,0:T(8,128)S(1)}, u32[]{:S(2)}, u32[]{:S(2)}) collective-permute-start(f32[16,768]{1,0:T(8,128)S(1)} %add.30), channel_id=1, source_target_pairs={{0,16},{1,17},{2,18},{3,19},{4,20},{5,21},{6,22},{7,23},{8,24},{9,... | collective-permute-start | bytes 147464 | tf_op jit(solution)/shard_map/ppermute | solution.py:246
  203.6 4.2 %collective-permute-start.5 = (f32[16,768]{1,0:T(8,128)S(1)}, f32[16,768]{1,0:T(8,128)S(1)}, u32[]{:S(2)}, u32[]{:S(2)}) collective-permute-start(f32[16,768]{1,0:T(8,128)S(1)} %add.31), channel_id=1, source_target_pairs={{0,32},{1,33},{2,34},{3,35},{4,36},{5,37},{6,38},{7,39},{8,40},{9,... | collective-permute-start | bytes 147464 | tf_op jit(solution)/shard_map/ppermute | solution.py:246
  207.8 5.7 %collective-permute-start.6 = (f32[16,768]{1,0:T(8,128)S(1)}, f32[16,768]{1,0:T(8,128)S(1)}, u32[]{:S(2)}, u32[]{:S(2)}) collective-permute-start(f32[16,768]{1,0:T(8,128)S(1)} %add.32), channel_id=1, source_target_pairs={{0,64},{1,65},{2,66},{3,67},{4,68},{5,69},{6,70},{7,71},{8,72},{9,... | collective-permute-start | bytes 147464 | tf_op jit(solution)/shard_map/ppermute | solution.py:246
  215.7 1.7 copy-start.2

commit v3 on v2

--- a/solution.py
+++ b/solution.py
@@ -23,6 +23,7 @@
 WIDTH = SUBSPACES * CENTROIDS
 OWN = 8
 SLOTS = OWN * CAP
+BOOK_ROWS = 8
 F32 = jnp.float32
 BF16 = jnp.bfloat16
 
@@ -108,23 +109,59 @@
     notes_out[...] = jnp.where(got_list == own_list.astype(F32), got_spot + 1.0, 0.0)
 
 
-def one_hot_body(offset, codes, one_hot):
+def fill_one_hot(codes, one_hot):
     for c in range(CHUNKS):
         part = codes[0, c * 16 : (c + 1) * 16, :].astype(F32).astype(BF16)
         for k in range(CENTROIDS):
             at = c * ENTRIES + k * 16
-            one_hot[0, at : at + 16, :] = jnp.where(
+            one_hot[at : at + 16, :] = jnp.where(
                 part == jnp.asarray(k, BF16), jnp.asarray(1, BF16), jnp.asarray(0, BF16)
             )
 
 
-def score_body(got, high, low, one_hot, masks, exps, stats, table):
-    i = pl.program_id(0)
+def score_body(
+    offset, got, high, low, first, odd, even, exps, stats, table, hot_a, hot_b, held_a, held_b
+):
+    s = pl.program_id(0)
     half = stats.shape[0]
 
-    @pl.when(i == 0)
+    def score(i, hot, held):
+        rows = jnp.concatenate(
+            [
+                jnp.concatenate(
+                    [
+                        table[j, pl.ds(r * OWN + i, half, stride=SLOTS), :].astype(BF16)
+                        for j in range(WIDTH // 128)
+                    ],
+                    axis=1,
+                )
+                for r in range(CAP)
+            ],
+            axis=0,
+        )
+        held[...] = dot(rows, hot[...])
+
+    def soften(i, held, place):
+        scores = held[...]
+        top = jnp.max(scores, axis=1, keepdims=True)
+        exp_scores = jnp.exp(scores - top)
+        total = jnp.sum(exp_scores, axis=1, keepdims=True)
+        exps[place] = exp_scores
+        lane = iota(stats.shape, 1)
+        kept = stats[...]
+        for r in range(CAP):
+            at = r * OWN + i
+            kept = jnp.where(lane == at, top[r * half : (r + 1) * half], kept)
+            kept = jnp.where(lane == SLOTS + at, total[r * half : (r + 1) * half], kept)
+        stats[...] = kept
+
+    last = pl.num_programs(0) - 1
+
+    @pl.when(s == 0)
     def _():
         stats[...] = jnp.zeros_like(stats)
+        held_b[...] = jnp.zeros_like(held_b)
+        fill_one_hot(first, hot_a)
         for c in range(CHUNKS):
             rows = got[:, c * FEATS : (c + 1) * FEATS]
             twice = jnp.concatenate([rows, rows], axis=1)
@@ -133,31 +170,19 @@
             table[2 * c] = looked[:, 0:128]
             table[2 * c + 1] = looked[:, 128:256]
 
-    rows = jnp.concatenate(
-        [
-            jnp.concatenate(
-                [
-                    table[j, pl.ds(r * OWN + i, half, stride=SLOTS), :].astype(BF16)
-                    for j in range(WIDTH // 128)
-                ],
-                axis=1,
-            )
-            for r in range(CAP)
-        ],
-        axis=0,
-    )
-    scores = dot(rows, one_hot[0])
-    top = jnp.max(scores, axis=1, keepdims=True)
-    exp_scores = jnp.exp(scores - top)
-    total = jnp.sum(exp_scores, axis=1, keepdims=True)
-    exps[0] = exp_scores
-    lane = iota(stats.shape, 1)
-    held = stats[...]
-    for r in range(CAP):
-        at = r * OWN + i
-        held = jnp.where(lane == at, top[r * half : (r + 1) * half], held)
-        held = jnp.where(lane == SLOTS + at, total[r * half : (r + 1) * half], held)
-    stats[...] = held
+    @pl.when(s < last)
+    def _():
+        score(2 * s, hot_a, held_a)
+        fill_one_hot(odd, hot_b)
+        soften(2 * s - 1, held_b, 0)
+        score(2 * s + 1, hot_b, held_b)
+        fill_one_hot(even, hot_a)
+        soften(2 * s, held_a, 1)
+
+    @pl.when(s == last)
+    def _():
+        soften(2 * s - 1, held_b, 0)
+        exps[1] = jnp.zeros(exps.shape[1:], F32)
 
 
 def weight_body(stats, masks, notes, message):
@@ -181,55 +206,97 @@
     message[...] = jnp.stack([held, notes[...]], axis=1).reshape(message.shape)
 
 
-def grad_body(exps, message, one_hot, got, high, low, part_out, book_out, hist):
-    i = pl.program_id(0)
+def grad_body(
+    offset, message, got, high, low, exps_first, exps_odd, exps_even, first, odd, even,
+    out, hist, hot_a, hot_b, grads_a, grads_b,
+):
+    s = pl.program_id(0)
     half = message.shape[0] // 2
-    lane = iota((half, 128), 1)
-    weights = message[pl.ds(0, half, stride=2), :]
-    turned = pltpu.roll(message[pl.ds(1, half, stride=2), :], (128 - TARGETS * i) % 128, 1)
     place = iota((half, PASSAGES), 1).astype(F32)
-    grads = []
-    for r in range(CAP):
-        scale = jnp.sum(jnp.where(lane == r * OWN + i, weights, 0.0), axis=1, keepdims=True)
-        teacher = jnp.zeros((half, PASSAGES), F32)
-        for t in range(TARGETS):
-            at = r * OWN * TARGETS + t
-            weight = 2.0 * (TARGETS - t) / (TARGETS * (TARGETS + 1.0))
-            teacher = jnp.where(place == turned[:, at : at + 1] - 1.0, weight, teacher)
-        student = exps[0, r * half : (r + 1) * half, :] * scale
-        grads.append((student - teacher).astype(BF16))
-    grads = jnp.concatenate(grads, axis=0)
-    found = dot(grads, one_hot[0], ((1,), (1,)))
-    for r in range(CAP):
-        for j in range(WIDTH // 128):
-            hist[j, pl.ds(r * OWN + i, half, stride=SLOTS), :] = found[
-                r * half : (r + 1) * half, j * 128 : (j + 1) * 128
-            ]
-
-    @pl.when(i == pl.num_programs(0) - 1)
+
+    def prepare(i, exps, codes, hot, grads):
+        lane = iota((half, 128), 1)
+        weights = message[pl.ds(0, half, stride=2), :]
+        notes = message[pl.ds(1, half, stride=2), :]
+        turned = pltpu.roll(notes, (128 - TARGETS * i) % 128, 1)
+        for r in range(CAP):
+            scale = jnp.sum(jnp.where(lane == r * OWN + i, weights, 0.0), axis=1, keepdims=True)
+            teacher = jnp.zeros((half, PASSAGES), F32)
+            for t in range(TARGETS):
+                at = r * OWN * TARGETS + t
+                weight = 2.0 * (TARGETS - t) / (TARGETS * (TARGETS + 1.0))
+                teacher = jnp.where(place == turned[:, at : at + 1] - 1.0, weight, teacher)
+            student = exps[0, r * half : (r + 1) * half, :] * scale
+            grads[r * half : (r + 1) * half, :] = (student - teacher).astype(BF16)
+        fill_one_hot(codes, hot)
+
+    def count(i, hot, grads):
+        found = dot(grads[...], hot[...], ((1,), (1,)))
+        for r in range(CAP):
+            for j in range(WIDTH // 128):
+                hist[j, pl.ds(r * OWN + i, half, stride=SLOTS), :] = found[
+                    r * half : (r + 1) * half, j * 128 : (j + 1) * 128
+                ]
+
+    @pl.when(s == 0)
     def _():
+        prepare(0, exps_first, first, hot_a, grads_a)
+
+    count(2 * s, hot_a, grads_a)
+    prepare(2 * s + 1, exps_odd, odd, hot_b, grads_b)
+    count(2 * s + 1, hot_b, grads_b)
+    prepare(jnp.minimum(2 * s + 2, OWN - 1), exps_even, even, hot_a, grads_a)
+
+    @pl.when(s == pl.num_programs(0) - 1)
+    def _():
+        devices = out.shape[0]
         keep = iota((ENTRIES, FEATS), 0) % 16 == iota((ENTRIES, FEATS), 1) // SUBDIM
+        top = CHUNKS * SLOTS
+        out[CHUNKS * CENTROIDS :, top:, :] = jnp.zeros(
+            (devices - CHUNKS * CENTROIDS, BOOK_ROWS, 128), BF16
+        )
         for c in range(CHUNKS):
             h_high, h_low = split_two(jnp.concatenate([hist[2 * c], hist[2 * c + 1]], axis=1))
             both = jnp.concatenate([high[c], low[c]], axis=1)
             wide = dot(h_high, both)
             part = wide[:, 0:FEATS] + wide[:, FEATS:] + dot(h_low, high[c])
-            part_out[:, c * FEATS : (c + 1) * FEATS] = part.astype(BF16)
+            out[:, c * SLOTS : (c + 1) * SLOTS, :] = part.reshape(devices, SLOTS, FEATS).astype(
+                BF16
+            )
             book = dot(got[:, c * FEATS : (c + 1) * FEATS], h_high, ((0,), (0,)))
             book = jnp.where(keep, book.T, 0.0)
-            book_out[:, c * FEATS : (c + 1) * FEATS] = jnp.sum(
-                book.reshape(CENTROIDS, 16, FEATS), axis=1
-            )
-
-
-def norm_body(raw, normed):
-    value = raw[...]
+            book = jnp.sum(book.reshape(CENTROIDS, 16, FEATS), axis=1)
+            b_high = book.astype(BF16)
+            b_rest = book - b_high.astype(F32)
+            b_mid = b_rest.astype(BF16)
+            b_low = b_rest - b_mid.astype(F32)
+            row = iota((CENTROIDS, BOOK_ROWS, FEATS), 1)
+            parts = jnp.where(row == 0, b_high.astype(F32)[:, None, :], 0.0)
+            parts = jnp.where(row == 1, b_mid.astype(F32)[:, None, :], parts)
+            parts = jnp.where(row == 2, b_low[:, None, :], parts)
+            out[c * CENTROIDS : (c + 1) * CENTROIDS, top:, :] = parts.astype(BF16)
+
+
+def book_body(returned, total):
+    parts = returned[...].astype(F32)
+    total[...] = jnp.broadcast_to(
+        jnp.sum(jnp.sum(parts, axis=0), axis=0, keepdims=True), total.shape
+    )
+
+
+def norm_body(rows, normed):
+    value = rows[0 : CHUNKS * CENTROIDS, :]
     mean = jnp.sum(value * value, keepdims=True) / (CENTROIDS * D)
-    normed[...] = value * lax.rsqrt(mean + EPSILON)
+    value = value * lax.rsqrt(mean + EPSILON)
+    for c in range(CHUNKS):
+        normed[:, c * FEATS : (c + 1) * FEATS] = value[c * CENTROIDS : (c + 1) * CENTROIDS]
 
 
 def combine_body(chosen, returned, out):
-    out[...] = dot(chosen[...], returned[...]).astype(BF16)
+    devices = returned.shape[0]
+    for c in range(CHUNKS):
+        rows = returned[:, c * SLOTS : (c + 1) * SLOTS, :].reshape(devices * SLOTS, FEATS)
+        out[:, c * FEATS : (c + 1) * FEATS] = dot(chosen[...], rows).astype(BF16)
 
 
 def whole(shape):
@@ -238,15 +305,6 @@
 
 def exchange(value):
     return lax.all_to_all(value, BOTH, 0, 0, tiled=True)
-
-
-def sum_everywhere(value, devices):
-    step = 1
-    while step < devices:
-        other = lax.ppermute(value, BOTH, [(d, d ^ step) for d in range(devices)])
-        value = value + other
-        step *= 2
-    return value
 
 
 def spread_codebook(codebook):
@@ -290,81 +348,95 @@
     )(probes_t, probes, jnp.tile(targets, (1, 128 // TARGETS)))
     high, low = spread_codebook(codebook)
     offset = (lax.axis_index("query") * OWN).astype(jnp.int32).reshape(1)
-    one_hot = pl.pallas_call(
-        one_hot_body,
-        out_shape=jax.ShapeDtypeStruct((OWN, WIDTH, PASSAGES), BF16),
+
+    def code_of(index):
+        return pl.BlockSpec(
+            (1, SUBSPACES, PASSAGES), lambda s, off: (off[0] + index(s), 0, 0)
+        )
+
+    code_specs = [
+        code_of(lambda s: 0),
+        code_of(lambda s: jnp.minimum(2 * s + 1, OWN - 1)),
+        code_of(lambda s: jnp.minimum(2 * s + 2, OWN - 1)),
+    ]
+    table_spec = whole((CHUNKS, ENTRIES, FEATS))
+    table = pltpu.VMEM((WIDTH // 128, slots, 128), F32)
+    hot = pltpu.VMEM((WIDTH, PASSAGES), BF16)
+    codes = (passage_codes,) * 3
+
+    exps, stats = pl.pallas_call(
+        score_body,
+        out_shape=(jax.ShapeDtypeStruct((OWN + 2, list_rows, PASSAGES), F32), square),
         grid_spec=pltpu.PrefetchScalarGridSpec(
             num_scalar_prefetch=1,
-            grid=(OWN,),
-            in_specs=[
-                pl.BlockSpec((1, SUBSPACES, PASSAGES), lambda i, off: (off[0] + i, 0, 0))
+            grid=(OWN // 2 + 1,),
+            in_specs=[whole((slots, D)), table_spec, table_spec] + code_specs,
+            out_specs=[
+                pl.BlockSpec((2, list_rows, PASSAGES), lambda s, off: (s, 0, 0)),
+                whole(square.shape),
             ],
-            out_specs=pl.BlockSpec((1, WIDTH, PASSAGES), lambda i, off: (i, 0, 0)),
+            scratch_shapes=[table, hot, hot] + [pltpu.VMEM((list_rows, PASSAGES), F32)] * 2,
         ),
-        name="one_hot",
-    )(offset, passage_codes)
-
-    by_list = lambda *shape: pl.BlockSpec((1,) + shape, lambda i: (i, 0, 0))
-    exps_spec = by_list(list_rows, PASSAGES)
-    one_hot_spec = by_list(WIDTH, PASSAGES)
-    table_spec = whole((CHUNKS, ENTRIES, FEATS))
-    per_list = jax.ShapeDtypeStruct((OWN, list_rows, PASSAGES), F32)
-    scratch = [pltpu.VMEM((WIDTH // 128, slots, 128), F32)]
-
-    exps, stats = pl.pallas_call(
-        score_body,
-        out_shape=(per_list, square),
-        grid=(OWN,),
-        in_specs=[
-            whole((slots, D)),
-            table_spec,
-            table_spec,
-            one_hot_spec,
-            pl.BlockSpec(memory_space=pl.ANY),
-        ],
-        out_specs=[exps_spec, whole(square.shape)],
-        scratch_shapes=scratch,
         compiler_params=big,
         name="score",
-    )(got, high, low, one_hot, masks)
+    )(offset, got, high, low, *codes)
 
     message = pl.pallas_call(
         weight_body, out_shape=jax.ShapeDtypeStruct((2 * devices, 128), F32), name="weigh"
     )(exchange(stats), masks, notes)
 
-    partial_value, book = pl.pallas_call(
+    def exps_of(index):
+        return pl.BlockSpec((1, list_rows, PASSAGES), lambda s, off: (index(s), 0, 0))
+
+    result = pl.pallas_call(
         grad_body,
-        out_shape=(
-            jax.ShapeDtypeStruct((slots, D), BF16),
-            jax.ShapeDtypeStruct((CENTROIDS, D), F32),
+        out_shape=jax.ShapeDtypeStruct((devices, CHUNKS * SLOTS + BOOK_ROWS, FEATS), BF16),
+        grid_spec=pltpu.PrefetchScalarGridSpec(
+            num_scalar_prefetch=1,
+            grid=(OWN // 2,),
+            in_specs=[
+                whole((2 * devices, 128)),
+                whole((slots, D)),
+                table_spec,
+                table_spec,
+                exps_of(lambda s: 1),
+                exps_of(lambda s: 2 * s + 2),
+                exps_of(lambda s: jnp.minimum(2 * s + 3, OWN)),
+            ]
+            + code_specs,
+            out_specs=whole((devices, CHUNKS * SLOTS + BOOK_ROWS, FEATS)),
+            scratch_shapes=[table, hot, hot] + [pltpu.VMEM((list_rows, PASSAGES), BF16)] * 2,
         ),
-        grid=(OWN,),
-        in_specs=[
-            exps_spec,
-            whole((2 * devices, 128)),
-            one_hot_spec,
-            whole((slots, D)),
-            table_spec,
-            table_spec,
-        ],
-        out_specs=[whole((slots, D)), whole((CENTROIDS, D))],
-        scratch_shapes=scratch,
         compiler_params=big,
         name="grad",
-    )(exps, exchange(message), one_hot, got, high, low)
-
+    )(offset, exchange(message), got, high, low, exps, exps, exps, *codes)
+
+    returned = exchange(result)
+    book_spec = pl.BlockSpec(
+        (devices, BOOK_ROWS, FEATS), lambda b: (0, CHUNKS * SLOTS // BOOK_ROWS, 0)
+    )
+    book_sum = pl.pallas_call(
+        book_body,
+        out_shape=square,
+        grid=(1,),
+        in_specs=[book_spec],
+        out_specs=whole(square.shape),
+        name="book_sum",
+    )(returned)
     normed = pl.pallas_call(
         norm_body, out_shape=jax.ShapeDtypeStruct((CENTROIDS, D), F32), name="book_norm"
-    )(sum_everywhere(book, devices))
-
+    )(exchange(book_sum))
     grad_queries = pl.pallas_call(
         combine_body,
         out_shape=jax.ShapeDtypeStruct((count, D), BF16),
-        grid=(3,),
-        in_specs=[whole((count, slots)), pl.BlockSpec((slots, D // 3), lambda b: (0, b))],
-        out_specs=pl.BlockSpec((count, D // 3), lambda b: (0, b)),
+        grid=(1,),
+        in_specs=[
+            whole((count, slots)),
+            pl.BlockSpec((devices, CHUNKS * SLOTS, FEATS), lambda b: (0, 0, 0)),
+        ],
+        out_specs=whole((count, D)),
         name="combine",
-    )(chosen, exchange(partial_value))
+    )(chosen, returned)
     return grad_queries, normed
 
 

time: 223 us -> 211 us (0.946)
  the two profiles are of different devices: /device:TPU:0 before, /device:TPU:1 now
where the time goes in v3:
time: 211 us; the launch traced here: 210 us
  Pallas kernels  68.9 us (33%)
  blocking collectives  67 us (32%)
  waiting for transfers between devices  49.5 us (23%)
  starting transfers between devices  18.6 us (9%)
  local copies, waits for them, and re-layouts  4.5 us (2%)
    all_to_all x2, blocking collectives, exchange(): return lax.all_to_all(value, BOTH, 0, 0, tiled=True)  67 us
    all_to_all x3, waiting for transfers between devices, exchange(): return lax.all_to_all(value, BOTH, 0, 0, tiled=True)  49.5 us
    pallas_call x1, Pallas kernels, shards(): pl.pallas_call(grad_body, out_shape=jax.ShapeDtypeStruct((devices, CHUNKS...  29.1 us
    all_to_all x3, starting transfers between devices, exchange(): return lax.all_to_all(value, BOTH, 0, 0, tiled=True)  18.6 us
    pallas_call x1, Pallas kernels, shards(): pl.pallas_call(score_body, out_shape=(jax.ShapeDtypeStruct((OWN + 2, list...  18.4 us
    pallas_call x1, Pallas kernels, shards(): pl.pallas_call(home_body, out_shape=(jax.ShapeDtypeStruct((count, slots),...  5.26 us
    pallas_call x1, Pallas kernels, shards(): pl.pallas_call(combine_body, out_shape=jax.ShapeDtypeStruct((count, D), B...  4.75 us
    pallas_call x1, Pallas kernels, shards(): pl.pallas_call(dispatch_body, out_shape=jax.ShapeDtypeStruct((slots, D),...  4.46 us
  transfers between devices with their start and end apart: 3, of which 3 were waited for; matrix products, arithmetic and copies ran while one was open for 1% of the time, Pallas kernels for 5%

profile of v3, /device:TPU:1, one launch (start us, length us, event | category | flops | bytes accessed | tf_op | source)
XLA Modules:
  0.0 210.2 jit_solution(5728152348602652942)
XLA Ops:
  0.6 0.0 copy-start
  0.6 4.5 %dispatch.1 = bf16[2048,768]{1,0:T(8,128)(2,1)} custom-call(s32[4,256]{1,0:T(4,128)} %bitcast.35, bf16[256,768]{1,0:T(8,128)(2,1)} %queries.1), custom_call_target="tpu_custom_call" | custom-call | tf_op jit(solution)/shard_map/dispatch/pallas_call | solution.py:330
  5.1 0.0 copy-start.4
  5.1 11.5 %all-to-all-start = ((bf16[128,16,768]{2,1,0:T(8,128)(2,1)}), bf16[128,16,768]{2,1,0:T(8,128)(2,1)S(1)}, u32[]{:S(2)}, u32[]{:S(2)}) async-start(bf16[128,16,768]{2,1,0:T(8,128)(2,1)} %bitcast.26), calls=%async_computation | async-start | bytes 6291456 | tf_op jit(solution)/shard_map/all_to_all | solution.py:307
  16.6 0.0 copy-done.4
  16.7 1.0 fusion
  17.7 41.1 %all-to-all-done = bf16[128,16,768]{2,1,0:T(8,128)(2,1)S(1)} async-done(((bf16[128,16,768]{2,1,0:T(8,128)(2,1)}), bf16[128,16,768]{2,1,0:T(8,128)(2,1)S(1)}, u32[]{:S(2)}, u32[]{:S(2)}) %all-to-all-start) | async-done | bytes 3145760 | tf_op jit(solution)/shard_map/all_to_all | solution.py:307
  58.8 0.0 copy-start.1
  58.8 1.6 copy-done.1
  60.4 0.0 copy-start.5
  60.4 18.4 %score.1 = (f32[10,256,1024]{2,1,0:T(8,128)}, f32[128,128]{1,0:T(8,128)}) custom-call(s32[1]{0:T(128)} %bitcast.2.offset, bf16[2048,768]{1,0:T(8,128)(2,1)} %bitcast.24, bf16[6,256,128]{2,1,0:T(8,128)(2,1)} %get-tuple-element.13.high, bf16[6,256,128]{2,1,0:T(8,128)(2,1)} %get-tuple-element.12.low, s32[32,96,1024]{2,1,0:T(8,128)} %even.3, ...), custom_call_target="tpu_custom_call" | custom-call | tf_op jit(solution)/shard_map/score/pallas_call | solution.py:367
  78.9 3.5 %all-to-all-start.1 = ((f32[128,1,128]{2,1,0:T(1,128)}), f32[128,1,128]{2,1,0:T(1,128)S(1)}, u32[]{:S(2)}, u32[]{:S(2)}) async-start(f32[128,1,128]{2,1,0:T(1,128)} %bitcast.34), calls=%async_computation.1 | async-start | bytes 131072 | tf_op jit(solution)/shard_map/all_to_all | solution.py:307
  82.4 0.0 copy-done
  82.4 0.0 copy-done.5
  82.5 0.8 copy.13.probes
  83.3 0.8 copy.14.targets_wide
  84.0 5.3 %home.1 = (bf16[256,2048]{1,0:T(8,128)(2,1)}, bf16[16,128,256]{2,1,0:T(8,128)(2,1)}, f32[128,128]{1,0:T(8,128)}) custom-call(s32[4,256]{1,0:T(4,128)} %bitcast.36, s32[256,4]{1,0:T(8,128)} %copy.13.probes, s32[256,128]{1,0:T(8,128)} %copy.14.targets_wide), custom_call_target="tpu_custom_call" | custom-call | tf_op jit(solution)/shard_map/home/pallas_call | solution.py:340
  89.3 3.2 %all-to-all-done.1 = f32[128,1,128]{2,1,0:T(1,128)S(1)} async-done(((f32[128,1,128]{2,1,0:T(1,128)}), f32[128,1,128]{2,1,0:T(1,128)S(1)}, u32[]{:S(2)}, u32[]{:S(2)}) %all-to-all-start.1) | async-done | bytes 65568 | tf_op jit(solution)/shard_map/all_to_all | solution.py:307
  92.5 0.0 copy-start.2
  92.5 0.6 copy-done.2
  93.1 3.6 %weigh.1 = f32[256,128]{1,0:T(8,128)} custom-call(f32[128,128]{1,0:T(8,128)} %bitcast.29, bf16[16,128,256]{2,1,0:T(8,128)(2,1)} %get-tuple-element.9.masks, f32[128,128]{1,0:T(8,128)} %get-tuple-element.10.notes), custom_call_target="tpu_custom_call" | custom-call | tf_op jit(solution)/shard_map/weigh/pallas_call | solution.py:384
  96.7 17.2 %all_to_all.49 = f32[128,2,128]{2,1,0:T(2,128)} all-to-all(f32[128,2,128]{2,1,0:T(2,128)} %bitcast.28), channel_id=1, replica_groups=mesh['corpus'=32,'query'=4] {'corpus','query'}, dimensions={0} | all-to-all | bytes 262144 | tf_op jit(solution)/shard_map/all_to_all | solution.py:307
  113.9 29.1 %grad.1 = bf16[128,104,128]{2,1,0:T(8,128)(2,1)} custom-call(s32[1]{0:T(128)} %bitcast.2.offset, f32[256,128]{1,0:T(8,128)} %bitcast.27, bf16[2048,768]{1,0:T(8,128)(2,1)} %bitcast.25, bf16[6,256,128]{2,1,0:T(8,128)(2,1)} %get-tuple-element.13.high, bf16[6,256,128]{2,1,0:T(8,128)(2,1)} %get-tuple-element.12.low, ...), custom_call_target="tpu_custom_call" | custom-call | tf_op jit(solution)/shard_map/grad/pallas_call | solution.py:391
  142.9 49.8 %all_to_all.50.returned = bf16[128,104,128]{2,1,0:T(8,128)(2,1)} all-to-all(bf16[128,104,128]{2,1,0:T(8,128)(2,1)} %grad.1), channel_id=1, replica_groups=mesh['corpus'=32,'query'=4] {'corpus','query'}, dimensions={0} | all-to-all | bytes 6815744 | tf_op jit(solution)/shard_map/all_to_all | solution.py:307
  192.7 1.7 book_sum.1
  194.4 3.6 %all-to-all-start.4 = ((f32[128,1,128]{2,1,0:T(1,128)}), f32[128,1,128]{2,1,0:T(1,128)S(1)}, u32[]{:S(2)}, u32[]{:S(2)}) async-start(f32[128,1,128]{2,1,0:T(1,128)} %bitcast.30), calls=%async_computation.4 | async-start | bytes 131072 | tf_op jit(solution)/shard_map/all_to_all | solution.py:307
  198.0 4.8 %combine.1 = bf16[256,768]{1,0:T(8,128)(2,1)} custom-call(bf16[256,2048]{1,0:T(8,128)(2,1)} %get-tuple-element.7.chosen, bf16[128,104,128]{2,1,0:T(8,128)(2,1)} %all_to_all.50.returned), custom_call_target="tpu_custom_call" | custom-call | tf_op jit(solution)/shard_map/combine/pallas_call | solution.py:429
  202.8 5.2 %all-to-all-done.4 = f32[128,1,128]{2,1,0:T(1,128)S(1)} async-done(((f32[128,1,128]{2,1,0:T(1,128)}), f32[128,1,128]{2,1,0:T(1,128)S(1)}, u32[]{:S(2)}, u32[]{:S(2)}) %all-to-all-start.4) | async-done | bytes 65568 | tf_op jit(solution)/shard_map/all_to_all | solution.py:307
  208.0 0.0 copy-start.3
  208.0 0.6 copy-done.3
  208.6 1.6 book_norm.1
  (6 shorter events, 0.1 us)
Async XLA Ops:
  0.6 81.8 %copy-start = (s32[256,8]{0,1:T(8,128)S(1)}, s32[256,8]{0,1:T(8,128)}, u32[]{:S(2)}) copy-start(s32[256,8]{0,1:T(8,128)} %param.7) | copy-start | bytes 24580
  5.1 11.5 %copy-start.4 = (f32[16,768]{1,0:T(8,128)S(1)}, f32[16,768]{1,0:T(8,128)}, u32[]{:S(2)}) copy-start(f32[16,768]{1,0:T(8,128)} %param.9) | copy-start | bytes 147460
  5.1 53.7 %all-to-all-start = ((bf16[128,16,768]{2,1,0:T(8,128)(2,1)}), bf16[128,16,768]{2,1,0:T(8,128)(2,1)S(1)}, u32[]{:S(2)}, u32[]{:S(2)}) async-start(bf16[128,16,768]{2,1,0:T(8,128)(2,1)} %bitcast.26), calls=%async_computation | async-start | bytes 6291456 | tf_op jit(solution)/shard_map/all_to_all | solution.py:307
  58.8 1.6 copy-start.1
  60.4 22.0 %copy-start.5 = (s32[256,4]{0,1:T(4,128)S(1)}, s32[256,4]{0,1:T(4,128)}, u32[]{:S(2)}) copy-start(s32[256,4]{0,1:T(4,128)} %param.6) | copy-start | bytes 12292
  78.9 13.6 %all-to-all-start.1 = ((f32[128,1,128]{2,1,0:T(1,128)}), f32[128,1,128]{2,1,0:T(1,128)S(1)}, u32[]{:S(2)}, u32[]{:S(2)}) async-start(f32[128,1,128]{2,1,0:T(1,128)} %bitcast.34), calls=%async_computation.1 | async-start | bytes 131072 | tf_op jit(solution)/shard_map/all_to_all | solution.py:307
  92.5 0.6 copy-start.2
  194.4 13.6 %all-to-all-start.4 = ((f32[128,1,128]{2,1,0:T(1,128)}), f32[128,1,128]{2,1,0:T(1,128)S(1)}, u32[]{:S(2)}, u32[]{:S(2)}) async-start(f32[128,1,128]{2,1,0:T(1,128)} %bitcast.30), calls=%async_computation.4 | async-start | bytes 131072 | tf_op jit(solution)/shard_map/all_to_all | solution.py:307
  208.0 0.6 copy-start.3

commit v4 on v3

--- a/solution.py
+++ b/solution.py
@@ -120,7 +120,8 @@
 
 
 def score_body(
-    offset, got, high, low, first, odd, even, exps, stats, table, hot_a, hot_b, held_a, held_b
+    offset, got, high, low, notes, first, odd, even,
+    exps, message, table, hot_a, hot_b, held_a, held_b, stats,
 ):
     s = pl.program_id(0)
     half = stats.shape[0]
@@ -183,51 +184,60 @@
     def _():
         soften(2 * s - 1, held_b, 0)
         exps[1] = jnp.zeros(exps.shape[1:], F32)
-
-
-def weight_body(stats, masks, notes, message):
+        message[...] = jnp.stack([stats[...], notes[...]], axis=1).reshape(message.shape)
+
+
+def weight_body(stats, masks, weights, ratios):
     devices, count = masks.shape[1:]
+    tops = stats[pl.ds(0, devices, stride=2), :]
     low = -3.0e38
     peak = jnp.full((devices, count), low, F32)
     for s in range(SLOTS):
-        peak = jnp.maximum(peak, jnp.where(masks[s] > 0, stats[:, s : s + 1], low))
+        peak = jnp.maximum(peak, jnp.where(masks[s] > 0, tops[:, s : s + 1], low))
     peak = jnp.max(peak, axis=0, keepdims=True)
     denom = jnp.zeros((devices, count), F32)
     for s in range(SLOTS):
-        part = jnp.exp(stats[:, s : s + 1] - peak) * stats[:, SLOTS + s : SLOTS + 1 + s]
-        denom = denom + jnp.where(masks[s] > 0, part, 0.0)
+        ratio = jnp.where(masks[s] > 0, jnp.exp(tops[:, s : s + 1] - peak), 0.0)
+        ratios[s] = ratio
+        denom = denom + ratio * tops[:, SLOTS + s : SLOTS + 1 + s]
     denom = jnp.sum(denom, axis=0, keepdims=True)
     lane = iota((devices, 128), 1)
     held = jnp.zeros((devices, 128), F32)
     for s in range(SLOTS):
-        part = jnp.exp(stats[:, s : s + 1] - peak) / denom
-        part = jnp.sum(jnp.where(masks[s] > 0, part, 0.0), axis=1, keepdims=True)
+        part = jnp.sum(ratios[s] / denom, axis=1, keepdims=True)
         held = jnp.where(lane == s, part, held)
-    message[...] = jnp.stack([held, notes[...]], axis=1).reshape(message.shape)
+    weights[...] = held
+
+
+def teacher_body(message, teacher):
+    i = pl.program_id(0)
+    half = message.shape[0] // 2
+    turned = pltpu.roll(message[pl.ds(1, half, stride=2), :], (128 - TARGETS * i) % 128, 1)
+    place = iota((half, PASSAGES), 1).astype(F32)
+    for r in range(CAP):
+        held = jnp.zeros((half, PASSAGES), F32)
+        for t in range(TARGETS):
+            at = r * OWN * TARGETS + t
+            weight = 2.0 * (TARGETS - t) / (TARGETS * (TARGETS + 1.0))
+            held = jnp.where(place == turned[:, at : at + 1] - 1.0, weight, held)
+        teacher[0, r * half : (r + 1) * half, :] = held
 
 
 def grad_body(
-    offset, message, got, high, low, exps_first, exps_odd, exps_even, first, odd, even,
+    offset, weights, got, high, low, exps_first, exps_odd, exps_even,
+    teacher_first, teacher_odd, teacher_even, first, odd, even,
     out, hist, hot_a, hot_b, grads_a, grads_b,
 ):
     s = pl.program_id(0)
-    half = message.shape[0] // 2
-    place = iota((half, PASSAGES), 1).astype(F32)
-
-    def prepare(i, exps, codes, hot, grads):
+    half = weights.shape[0]
+
+    def prepare(i, exps, teacher, codes, hot, grads):
         lane = iota((half, 128), 1)
-        weights = message[pl.ds(0, half, stride=2), :]
-        notes = message[pl.ds(1, half, stride=2), :]
-        turned = pltpu.roll(notes, (128 - TARGETS * i) % 128, 1)
         for r in range(CAP):
-            scale = jnp.sum(jnp.where(lane == r * OWN + i, weights, 0.0), axis=1, keepdims=True)
-            teacher = jnp.zeros((half, PASSAGES), F32)
-            for t in range(TARGETS):
-                at = r * OWN * TARGETS + t
-                weight = 2.0 * (TARGETS - t) / (TARGETS * (TARGETS + 1.0))
-                teacher = jnp.where(place == turned[:, at : at + 1] - 1.0, weight, teacher)
-            student = exps[0, r * half : (r + 1) * half, :] * scale
-            grads[r * half : (r + 1) * half, :] = (student - teacher).astype(BF16)
+            own = jnp.where(lane == r * OWN + i, weights[...], 0.0)
+            scale = jnp.sum(own, axis=1, keepdims=True)
+            rows = slice(r * half, (r + 1) * half)
+            grads[rows, :] = (exps[0, rows, :] * scale - teacher[0, rows, :]).astype(BF16)
         fill_one_hot(codes, hot)
 
     def count(i, hot, grads):
@@ -240,12 +250,13 @@
 
     @pl.when(s == 0)
     def _():
-        prepare(0, exps_first, first, hot_a, grads_a)
+        prepare(0, exps_first, teacher_first, first, hot_a, grads_a)
 
     count(2 * s, hot_a, grads_a)
-    prepare(2 * s + 1, exps_odd, odd, hot_b, grads_b)
+    prepare(2 * s + 1, exps_odd, teacher_odd, odd, hot_b, grads_b)
     count(2 * s + 1, hot_b, grads_b)
-    prepare(jnp.minimum(2 * s + 2, OWN - 1), exps_even, even, hot_a, grads_a)
+    following = jnp.minimum(2 * s + 2, OWN - 1)
+    prepare(following, exps_even, teacher_even, even, hot_a, grads_a)
 
     @pl.when(s == pl.num_programs(0) - 1)
     def _():
@@ -336,6 +347,8 @@
         name="dispatch",
     )(probes_t, queries)
     got = exchange(sending)
+    got = pltpu.with_memory_space_constraint(got, pltpu.VMEM)
+    arrived = pl.BlockSpec(memory_space=pltpu.VMEM)
 
     chosen, masks, notes = pl.pallas_call(
         home_body,
@@ -364,26 +377,43 @@
     hot = pltpu.VMEM((WIDTH, PASSAGES), BF16)
     codes = (passage_codes,) * 3
 
-    exps, stats = pl.pallas_call(
+    exps, message = pl.pallas_call(
         score_body,
-        out_shape=(jax.ShapeDtypeStruct((OWN + 2, list_rows, PASSAGES), F32), square),
+        out_shape=(
+            jax.ShapeDtypeStruct((OWN + 2, list_rows, PASSAGES), F32),
+            jax.ShapeDtypeStruct((2 * devices, 128), F32),
+        ),
         grid_spec=pltpu.PrefetchScalarGridSpec(
             num_scalar_prefetch=1,
             grid=(OWN // 2 + 1,),
-            in_specs=[whole((slots, D)), table_spec, table_spec] + code_specs,
+            in_specs=[arrived, table_spec, table_spec, whole(square.shape)] + code_specs,
             out_specs=[
                 pl.BlockSpec((2, list_rows, PASSAGES), lambda s, off: (s, 0, 0)),
-                whole(square.shape),
+                whole((2 * devices, 128)),
             ],
-            scratch_shapes=[table, hot, hot] + [pltpu.VMEM((list_rows, PASSAGES), F32)] * 2,
+            scratch_shapes=[table, hot, hot]
+            + [pltpu.VMEM((list_rows, PASSAGES), F32)] * 2
+            + [pltpu.VMEM(square.shape, F32)],
         ),
         compiler_params=big,
         name="score",
-    )(offset, got, high, low, *codes)
-
-    message = pl.pallas_call(
-        weight_body, out_shape=jax.ShapeDtypeStruct((2 * devices, 128), F32), name="weigh"
-    )(exchange(stats), masks, notes)
+    )(offset, got, high, low, notes, *codes)
+
+    message = exchange(message)
+    weights = pl.pallas_call(
+        weight_body,
+        out_shape=square,
+        scratch_shapes=[pltpu.VMEM((SLOTS, devices, count), F32)],
+        name="weigh",
+    )(message, masks)
+    teacher = pl.pallas_call(
+        teacher_body,
+        out_shape=jax.ShapeDtypeStruct((OWN, list_rows, PASSAGES), F32),
+        grid=(OWN,),
+        in_specs=[whole((2 * devices, 128))],
+        out_specs=pl.BlockSpec((1, list_rows, PASSAGES), lambda i: (i, 0, 0)),
+        name="teacher",
+    )(message)
 
     def exps_of(index):
         return pl.BlockSpec((1, list_rows, PASSAGES), lambda s, off: (index(s), 0, 0))
@@ -395,13 +425,16 @@
             num_scalar_prefetch=1,
             grid=(OWN // 2,),
             in_specs=[
-                whole((2 * devices, 128)),
-                whole((slots, D)),
+                whole(square.shape),
+                arrived,
                 table_spec,
                 table_spec,
                 exps_of(lambda s: 1),
                 exps_of(lambda s: 2 * s + 2),
                 exps_of(lambda s: jnp.minimum(2 * s + 3, OWN)),
+                exps_of(lambda s: 0),
+                exps_of(lambda s: 2 * s + 1),
+                exps_of(lambda s: jnp.minimum(2 * s + 2, OWN - 1)),
             ]
             + code_specs,
             out_specs=whole((devices, CHUNKS * SLOTS + BOOK_ROWS, FEATS)),
@@ -409,7 +442,10 @@
         ),
         compiler_params=big,
         name="grad",
-    )(offset, exchange(message), got, high, low, exps, exps, exps, *codes)
+    )(
+        offset, exchange(weights), got, high, low,
+        exps, exps, exps, teacher, teacher, teacher, *codes,
+    )
 
     returned = exchange(result)
     book_spec = pl.BlockSpec(

time: 211 us -> 208 us (0.986)
  waiting for transfers between devices: 49.5 us -> 40.3 us
  Pallas kernels: 68.9 us -> 74.1 us
    all_to_all x3, waiting for transfers between devices: 49.5 us -> 40.3 us  [exchange(): return lax.all_to_all(value, BOTH, 0, 0, tiled=True)]
    pallas_call x1 -> x2, Pallas kernels: 3.55 us -> 12.2 us  [the longest x1 8.75 us: shards(): pl.pallas_call(teacher_body, out_shape=jax.ShapeDtypeStruct((OWN, list_ro...]
    pallas_call x1, Pallas kernels: 29.1 us -> 25.8 us  [shards(): pl.pallas_call(grad_body, out_shape=jax.ShapeDtypeStruct((devices, CHUNKS...]
  transfers between devices with their start and end apart: 3 -> 3, of which waited for: 3 -> 3; matrix products, arithmetic and copies ran while one was open for 1% -> 1% of each run, Pallas kernels for 5% -> 9%
where the time goes in v4:
time: 208 us; the launch traced here: 207 us
  Pallas kernels  74.1 us (36%)
  blocking collectives  68.7 us (33%)
  waiting for transfers between devices  40.3 us (19%)
  starting transfers between devices  19.4 us (9%)
  local copies, waits for them, and re-layouts  2.83 us (1%)
    all_to_all x2, blocking collectives, exchange(): return lax.all_to_all(value, BOTH, 0, 0, tiled=True)  68.7 us
    all_to_all x3, waiting for transfers between devices, exchange(): return lax.all_to_all(value, BOTH, 0, 0, tiled=True)  40.3 us
    pallas_call x1, Pallas kernels, shards(): pl.pallas_call(grad_body, out_shape=jax.ShapeDtypeStruct((devices, CHUNKS...  25.8 us
    all_to_all x3, starting transfers between devices, exchange(): return lax.all_to_all(value, BOTH, 0, 0, tiled=True)  19.4 us
    pallas_call x1, Pallas kernels, shards(): pl.pallas_call(score_body, out_shape=(jax.ShapeDtypeStruct((OWN + 2, list...  18.4 us
    pallas_call x1, Pallas kernels, shards(): pl.pallas_call(teacher_body, out_shape=jax.ShapeDtypeStruct((OWN, list_ro...  8.75 us
    pallas_call x1, Pallas kernels, shards(): pl.pallas_call(home_body, out_shape=(jax.ShapeDtypeStruct((count, slots),...  5.25 us
    pallas_call x1, Pallas kernels, shards(): pl.pallas_call(combine_body, out_shape=jax.ShapeDtypeStruct((count, D), B...  4.75 us
  transfers between devices with their start and end apart: 3, of which 3 were waited for; matrix products, arithmetic and copies ran while one was open for 1% of the time, Pallas kernels for 9%

profile of v4, /device:TPU:1, one launch (start us, length us, event | category | flops | bytes accessed | tf_op | source)
XLA Modules:
  0.0 207.1 jit_solution(12820261826851218640)
XLA Ops:
  0.6 0.0 copy-start
  0.6 4.4 %dispatch.1 = bf16[2048,768]{1,0:T(8,128)(2,1)} custom-call(s32[4,256]{1,0:T(4,128)} %bitcast.34, bf16[256,768]{1,0:T(8,128)(2,1)} %queries.1), custom_call_target="tpu_custom_call" | custom-call | tf_op jit(solution)/shard_map/dispatch/pallas_call | solution.py:341
  5.1 0.0 copy-start.4
  5.1 0.0 copy-start.3
  5.1 11.9 %all-to-all-start = ((bf16[128,16,768]{2,1,0:T(8,128)(2,1)}), bf16[128,16,768]{2,1,0:T(8,128)(2,1)}, u32[]{:S(2)}, u32[]{:S(2)}) async-start(bf16[128,16,768]{2,1,0:T(8,128)(2,1)} %bitcast.24), calls=%async_computation | async-start | bytes 6291456 | tf_op jit(solution)/shard_map/all_to_all | solution.py:318
  17.0 0.0 copy-done.4
  17.0 0.8 copy.13.probes
  17.8 0.0 copy-done.3
  17.8 0.0 copy-done
  17.9 0.7 copy.14.targets_wide
  18.6 1.0 fusion
  19.7 5.2 %home.1 = (bf16[256,2048]{1,0:T(8,128)(2,1)}, bf16[16,128,256]{2,1,0:T(8,128)(2,1)}, f32[128,128]{1,0:T(8,128)}) custom-call(s32[4,256]{1,0:T(4,128)} %bitcast.35, s32[256,4]{1,0:T(8,128)} %copy.13.probes, s32[256,128]{1,0:T(8,128)} %copy.14.targets_wide), custom_call_target="tpu_custom_call" | custom-call | tf_op jit(solution)/shard_map/home/pallas_call | solution.py:353
  24.9 34.0 %all-to-all-done = bf16[128,16,768]{2,1,0:T(8,128)(2,1)} async-done(((bf16[128,16,768]{2,1,0:T(8,128)(2,1)}), bf16[128,16,768]{2,1,0:T(8,128)(2,1)}, u32[]{:S(2)}, u32[]{:S(2)}) %all-to-all-start) | async-done | bytes 3145760 | tf_op jit(solution)/shard_map/all_to_all | solution.py:318
  58.9 18.4 %score.1 = (f32[10,256,1024]{2,1,0:T(8,128)}, f32[256,128]{1,0:T(8,128)}) custom-call(s32[1]{0:T(128)} %bitcast.2.offset, bf16[2048,768]{1,0:T(8,128)(2,1)} %bitcast.4.got, bf16[6,256,128]{2,1,0:T(8,128)(2,1)} %get-tuple-element.13.high, bf16[6,256,128]{2,1,0:T(8,128)(2,1)} %get-tuple-element.12.low, f32[128,128]{1,0:T(8,128)} %get-tuple-element.8.notes, ...), custom_call_target="tpu_custom_call" | custom-call | tf_op jit(solution)/shard_map/score/pallas_call | solution.py:380
  77.3 14.9 %all_to_all.49 = f32[128,2,128]{2,1,0:T(2,128)} all-to-all(f32[128,2,128]{2,1,0:T(2,128)} %bitcast.32), channel_id=1, replica_groups=mesh['corpus'=32,'query'=4] {'corpus','query'}, dimensions={0} | all-to-all | bytes 262144 | tf_op jit(solution)/shard_map/all_to_all | solution.py:318
  92.3 3.4 %weigh.1 = f32[128,128]{1,0:T(8,128)} custom-call(f32[256,128]{1,0:T(8,128)} %bitcast.25, bf16[16,128,256]{2,1,0:T(8,128)(2,1)} %get-tuple-element.10.masks), custom_call_target="tpu_custom_call" | custom-call | tf_op jit(solution)/shard_map/weigh/pallas_call | solution.py:403
  95.7 3.9 %all-to-all-start.2 = ((f32[128,1,128]{2,1,0:T(1,128)}), f32[128,1,128]{2,1,0:T(1,128)S(1)}, u32[]{:S(2)}, u32[]{:S(2)}) async-start(f32[128,1,128]{2,1,0:T(1,128)} %bitcast.29), calls=%async_computation.2 | async-start | bytes 131072 | tf_op jit(solution)/shard_map/all_to_all | solution.py:318
  99.6 8.7 %teacher.1.teacher_first.teacher_odd.teacher_even = f32[8,256,1024]{2,1,0:T(8,128)} custom-call(f32[256,128]{1,0:T(8,128)} %bitcast.26), custom_call_target="tpu_custom_call" | custom-call | tf_op jit(solution)/shard_map/teacher/pallas_call | solution.py:409
  108.4 1.2 all-to-all-done.2
  109.6 0.0 copy-start.1
  109.6 0.6 copy-done.1
  110.2 25.8 %grad.1 = bf16[128,104,128]{2,1,0:T(8,128)(2,1)} custom-call(s32[1]{0:T(128)} %bitcast.2.offset, f32[128,128]{1,0:T(8,128)} %bitcast.27, bf16[2048,768]{1,0:T(8,128)(2,1)} %bitcast.4.got, bf16[6,256,128]{2,1,0:T(8,128)(2,1)} %get-tuple-element.13.high, bf16[6,256,128]{2,1,0:T(8,128)(2,1)} %get-tuple-element.12.low, ...), custom_call_target="tpu_custom_call" | custom-call | tf_op jit(solution)/shard_map/grad/pallas_call | solution.py:421
  135.9 53.7 %all_to_all.50.returned = bf16[128,104,128]{2,1,0:T(8,128)(2,1)} all-to-all(bf16[128,104,128]{2,1,0:T(8,128)(2,1)} %grad.1), channel_id=1, replica_groups=mesh['corpus'=32,'query'=4] {'corpus','query'}, dimensions={0} | all-to-all | bytes 6815744 | tf_op jit(solution)/shard_map/all_to_all | solution.py:318
  189.7 1.7 book_sum.1
  191.4 3.6 %all-to-all-start.4 = ((f32[128,1,128]{2,1,0:T(1,128)}), f32[128,1,128]{2,1,0:T(1,128)S(1)}, u32[]{:S(2)}, u32[]{:S(2)}) async-start(f32[128,1,128]{2,1,0:T(1,128)} %bitcast.28), calls=%async_computation.4 | async-start | bytes 131072 | tf_op jit(solution)/shard_map/all_to_all | solution.py:318
  195.0 4.8 %combine.1 = bf16[256,768]{1,0:T(8,128)(2,1)} custom-call(bf16[256,2048]{1,0:T(8,128)(2,1)} %get-tuple-element.7.chosen, bf16[128,104,128]{2,1,0:T(8,128)(2,1)} %all_to_all.50.returned), custom_call_target="tpu_custom_call" | custom-call | tf_op jit(solution)/shard_map/combine/pallas_call | solution.py:465
  199.7 5.2 %all-to-all-done.4 = f32[128,1,128]{2,1,0:T(1,128)S(1)} async-done(((f32[128,1,128]{2,1,0:T(1,128)}), f32[128,1,128]{2,1,0:T(1,128)S(1)}, u32[]{:S(2)}, u32[]{:S(2)}) %all-to-all-start.4) | async-done | bytes 65568 | tf_op jit(solution)/shard_map/all_to_all | solution.py:318
  204.9 0.0 copy-start.2
  204.9 0.6 copy-done.2
  205.5 1.6 book_norm.1
  (6 shorter events, 0.1 us)
Async XLA Ops:
  0.6 17.2 %copy-start = (s32[256,8]{0,1:T(8,128)S(1)}, s32[256,8]{0,1:T(8,128)}, u32[]{:S(2)}) copy-start(s32[256,8]{0,1:T(8,128)} %param.7) | copy-start | bytes 24580
  5.1 11.9 %copy-start.4 = (s32[256,4]{0,1:T(4,128)S(1)}, s32[256,4]{0,1:T(4,128)}, u32[]{:S(2)}) copy-start(s32[256,4]{0,1:T(4,128)} %param.6) | copy-start | bytes 12292
  5.1 12.7 %copy-start.3 = (f32[16,768]{1,0:T(8,128)S(1)}, f32[16,768]{1,0:T(8,128)}, u32[]{:S(2)}) copy-start(f32[16,768]{1,0:T(8,128)} %param.9) | copy-start | bytes 147460
  5.1 53.8 %all-to-all-start = ((bf16[128,16,768]{2,1,0:T(8,128)(2,1)}), bf16[128,16,768]{2,1,0:T(8,128)(2,1)}, u32[]{:S(2)}, u32[]{:S(2)}) async-start(bf16[128,16,768]{2,1,0:T(8,128)(2,1)} %bitcast.24), calls=%async_computation | async-start | bytes 6291456 | tf_op jit(solution)/shard_map/all_to_all | solution.py:318
  95.7 13.9 %all-to-all-start.2 = ((f32[128,1,128]{2,1,0:T(1,128)}), f32[128,1,128]{2,1,0:T(1,128)S(1)}, u32[]{:S(2)}, u32[]{:S(2)}) async-start(f32[128,1,128]{2,1,0:T(1,128)} %bitcast.29), calls=%async_computation.2 | async-start | bytes 131072 | tf_op jit(solution)/shard_map/all_to_all | solution.py:318
  109.6 0.6 copy-start.1
  191.4 13.5 %all-to-all-start.4 = ((f32[128,1,128]{2,1,0:T(1,128)}), f32[128,1,128]{2,1,0:T(1,128)S(1)}, u32[]{:S(2)}, u32[]{:S(2)}) async-start(f32[128,1,128]{2,1,0:T(1,128)} %bitcast.28), calls=%async_computation.4 | async-start | bytes 131072 | tf_op jit(solution)/shard_map/all_to_all | solution.py:318
  204.9 0.6 copy-start.2

commit v5 on v4

--- a/solution.py
+++ b/solution.py
@@ -120,8 +120,8 @@
 
 
 def score_body(
-    offset, got, high, low, notes, first, odd, even,
-    exps, message, table, hot_a, hot_b, held_a, held_b, stats,
+    offset, got_far, high, low, notes, odd, even,
+    exps, message, table, hot_a, hot_b, held_a, held_b, stats, got, sems,
 ):
     s = pl.program_id(0)
     half = stats.shape[0]
@@ -160,29 +160,37 @@
 
     @pl.when(s == 0)
     def _():
+        copies = [
+            pltpu.make_async_copy(
+                got_far.at[:, c * FEATS : (c + 1) * FEATS], got.at[c], sems.at[c]
+            )
+            for c in range(CHUNKS)
+        ]
+        for copy in copies:
+            copy.start()
         stats[...] = jnp.zeros_like(stats)
         held_b[...] = jnp.zeros_like(held_b)
-        fill_one_hot(first, hot_a)
+        fill_one_hot(even, hot_a)
         for c in range(CHUNKS):
-            rows = got[:, c * FEATS : (c + 1) * FEATS]
-            twice = jnp.concatenate([rows, rows], axis=1)
+            copies[c].wait()
+            twice = jnp.concatenate([got[c], got[c]], axis=1)
             weights = jnp.concatenate([high[c], low[c]], axis=1)
             looked = dot(twice, weights, ((1,), (1,)))
             table[2 * c] = looked[:, 0:128]
             table[2 * c + 1] = looked[:, 128:256]
 
-    @pl.when(s < last)
+    @pl.when((s > 0) & (s < last))
     def _():
-        score(2 * s, hot_a, held_a)
+        score(2 * s - 2, hot_a, held_a)
         fill_one_hot(odd, hot_b)
-        soften(2 * s - 1, held_b, 0)
-        score(2 * s + 1, hot_b, held_b)
+        soften(2 * s - 3, held_b, 0)
+        score(2 * s - 1, hot_b, held_b)
         fill_one_hot(even, hot_a)
-        soften(2 * s, held_a, 1)
+        soften(2 * s - 2, held_a, 1)
 
     @pl.when(s == last)
     def _():
-        soften(2 * s - 1, held_b, 0)
+        soften(2 * s - 3, held_b, 0)
         exps[1] = jnp.zeros(exps.shape[1:], F32)
         message[...] = jnp.stack([stats[...], notes[...]], axis=1).reshape(message.shape)
 
@@ -224,9 +232,8 @@
 
 
 def grad_body(
-    offset, weights, got, high, low, exps_first, exps_odd, exps_even,
-    teacher_first, teacher_odd, teacher_even, first, odd, even,
-    out, hist, hot_a, hot_b, grads_a, grads_b,
+    offset, weights, got_far, high, low, exps_odd, exps_even, teacher_odd, teacher_even,
+    odd, even, out, hist, hot_a, hot_b, grads_a, grads_b, got, sems,
 ):
     s = pl.program_id(0)
     half = weights.shape[0]
@@ -248,18 +255,29 @@
                     r * half : (r + 1) * half, j * 128 : (j + 1) * 128
                 ]
 
+    copies = [
+        pltpu.make_async_copy(got_far.at[:, c * FEATS : (c + 1) * FEATS], got.at[c], sems.at[c])
+        for c in range(CHUNKS)
+    ]
+    following = jnp.minimum(2 * s, OWN - 1)
+
     @pl.when(s == 0)
     def _():
-        prepare(0, exps_first, teacher_first, first, hot_a, grads_a)
-
-    count(2 * s, hot_a, grads_a)
-    prepare(2 * s + 1, exps_odd, teacher_odd, odd, hot_b, grads_b)
-    count(2 * s + 1, hot_b, grads_b)
-    following = jnp.minimum(2 * s + 2, OWN - 1)
-    prepare(following, exps_even, teacher_even, even, hot_a, grads_a)
+        prepare(0, exps_even, teacher_even, even, hot_a, grads_a)
+        for copy in copies:
+            copy.start()
+
+    @pl.when(s > 0)
+    def _():
+        count(2 * s - 2, hot_a, grads_a)
+        prepare(2 * s - 1, exps_odd, teacher_odd, odd, hot_b, grads_b)
+        count(2 * s - 1, hot_b, grads_b)
+        prepare(following, exps_even, teacher_even, even, hot_a, grads_a)
 
     @pl.when(s == pl.num_programs(0) - 1)
     def _():
+        for copy in copies:
+            copy.wait()
         devices = out.shape[0]
         keep = iota((ENTRIES, FEATS), 0) % 16 == iota((ENTRIES, FEATS), 1) // SUBDIM
         top = CHUNKS * SLOTS
@@ -274,7 +292,7 @@
             out[:, c * SLOTS : (c + 1) * SLOTS, :] = part.reshape(devices, SLOTS, FEATS).astype(
                 BF16
             )
-            book = dot(got[:, c * FEATS : (c + 1) * FEATS], h_high, ((0,), (0,)))
+            book = dot(got[c], h_high, ((0,), (0,)))
             book = jnp.where(keep, book.T, 0.0)
             book = jnp.sum(book.reshape(CENTROIDS, 16, FEATS), axis=1)
             b_high = book.astype(BF16)
@@ -318,6 +336,10 @@
     return lax.all_to_all(value, BOTH, 0, 0, tiled=True)
 
 
+def uncopied(value):
+    return pltpu.with_memory_space_constraint(value, pltpu.VMEM)
+
+
 def spread_codebook(codebook):
     book = codebook.reshape(CENTROIDS, CHUNKS, FEATS).transpose(1, 0, 2)
     own = jnp.arange(16)[:, None] == jnp.arange(FEATS)[None, :] // SUBDIM
@@ -346,9 +368,9 @@
         out_specs=pl.BlockSpec((slots // 4, D), lambda b: (b, 0)),
         name="dispatch",
     )(probes_t, queries)
-    got = exchange(sending)
-    got = pltpu.with_memory_space_constraint(got, pltpu.VMEM)
-    arrived = pl.BlockSpec(memory_space=pltpu.VMEM)
+    got = uncopied(exchange(sending))
+    arrived = pl.BlockSpec(memory_space=pl.ANY)
+    arrived_here = pltpu.VMEM((CHUNKS, slots, FEATS), BF16)
 
     chosen, masks, notes = pl.pallas_call(
         home_body,
@@ -367,15 +389,17 @@
             (1, SUBSPACES, PASSAGES), lambda s, off: (off[0] + index(s), 0, 0)
         )
 
-    code_specs = [
-        code_of(lambda s: 0),
-        code_of(lambda s: jnp.minimum(2 * s + 1, OWN - 1)),
-        code_of(lambda s: jnp.minimum(2 * s + 2, OWN - 1)),
-    ]
+    def in_order(index_of):
+        return [
+            index_of(lambda s: jnp.clip(2 * s - 1, 1, OWN - 1)),
+            index_of(lambda s: jnp.minimum(2 * s, OWN - 1)),
+        ]
+
+    code_specs = in_order(code_of)
     table_spec = whole((CHUNKS, ENTRIES, FEATS))
     table = pltpu.VMEM((WIDTH // 128, slots, 128), F32)
     hot = pltpu.VMEM((WIDTH, PASSAGES), BF16)
-    codes = (passage_codes,) * 3
+    codes = (passage_codes,) * 2
 
     exps, message = pl.pallas_call(
         score_body,
@@ -385,15 +409,17 @@
         ),
         grid_spec=pltpu.PrefetchScalarGridSpec(
             num_scalar_prefetch=1,
-            grid=(OWN // 2 + 1,),
+            grid=(OWN // 2 + 2,),
             in_specs=[arrived, table_spec, table_spec, whole(square.shape)] + code_specs,
             out_specs=[
-                pl.BlockSpec((2, list_rows, PASSAGES), lambda s, off: (s, 0, 0)),
+                pl.BlockSpec(
+                    (2, list_rows, PASSAGES), lambda s, off: (jnp.maximum(s - 1, 0), 0, 0)
+                ),
                 whole((2 * devices, 128)),
             ],
             scratch_shapes=[table, hot, hot]
             + [pltpu.VMEM((list_rows, PASSAGES), F32)] * 2
-            + [pltpu.VMEM(square.shape, F32)],
+            + [pltpu.VMEM(square.shape, F32), arrived_here, pltpu.SemaphoreType.DMA((CHUNKS,))],
         ),
         compiler_params=big,
         name="score",
@@ -423,28 +449,26 @@
         out_shape=jax.ShapeDtypeStruct((devices, CHUNKS * SLOTS + BOOK_ROWS, FEATS), BF16),
         grid_spec=pltpu.PrefetchScalarGridSpec(
             num_scalar_prefetch=1,
-            grid=(OWN // 2,),
+            grid=(OWN // 2 + 1,),
             in_specs=[
                 whole(square.shape),
                 arrived,
                 table_spec,
                 table_spec,
-                exps_of(lambda s: 1),
-                exps_of(lambda s: 2 * s + 2),
-                exps_of(lambda s: jnp.minimum(2 * s + 3, OWN)),
-                exps_of(lambda s: 0),
-                exps_of(lambda s: 2 * s + 1),
-                exps_of(lambda s: jnp.minimum(2 * s + 2, OWN - 1)),
             ]
+            + in_order(lambda index: exps_of(lambda s: index(s) + 1))
+            + in_order(exps_of)
             + code_specs,
             out_specs=whole((devices, CHUNKS * SLOTS + BOOK_ROWS, FEATS)),
-            scratch_shapes=[table, hot, hot] + [pltpu.VMEM((list_rows, PASSAGES), BF16)] * 2,
+            scratch_shapes=[table, hot, hot]
+            + [pltpu.VMEM((list_rows, PASSAGES), BF16)] * 2
+            + [arrived_here, pltpu.SemaphoreType.DMA((CHUNKS,))],
         ),
         compiler_params=big,
         name="grad",
     )(
-        offset, exchange(weights), got, high, low,
-        exps, exps, exps, teacher, teacher, teacher, *codes,
+        offset, uncopied(exchange(weights)), got, high, low,
+        exps, exps, teacher, teacher, *codes,
     )
 
     returned = exchange(result)
@@ -461,7 +485,7 @@
     )(returned)
     normed = pl.pallas_call(
         norm_body, out_shape=jax.ShapeDtypeStruct((CENTROIDS, D), F32), name="book_norm"
-    )(exchange(book_sum))
+    )(uncopied(exchange(book_sum)))
     grad_queries = pl.pallas_call(
         combine_body,
         out_shape=jax.ShapeDtypeStruct((count, D), BF16),

time: 208 us -> 208 us (level)
    pallas_call x1, Pallas kernels: 18.4 us -> 21.9 us  [shards(): pl.pallas_call(score_body, out_shape=(jax.ShapeDtypeStruct((OWN + 2, list...]
where the time goes in v5:
time: 208 us; the launch traced here: 207 us
  Pallas kernels  75.3 us (36%)
  blocking collectives  68.9 us (33%)
  waiting for transfers between devices  40.3 us (19%)
  starting transfers between devices  19.4 us (9%)
    all_to_all x2, blocking collectives, exchange(): return lax.all_to_all(value, BOTH, 0, 0, tiled=True)  68.9 us
    all_to_all x3, waiting for transfers between devices, exchange(): return lax.all_to_all(value, BOTH, 0, 0, tiled=True)  40.3 us
    pallas_call x1, Pallas kernels, shards(): pl.pallas_call(grad_body, out_shape=jax.ShapeDtypeStruct((devices, CHUNKS...  24.3 us
    pallas_call x1, Pallas kernels, shards(): pl.pallas_call(score_body, out_shape=(jax.ShapeDtypeStruct((OWN + 2, list...  21.9 us
    all_to_all x3, starting transfers between devices, exchange(): return lax.all_to_all(value, BOTH, 0, 0, tiled=True)  19.4 us
    pallas_call x1, Pallas kernels, shards(): pl.pallas_call(teacher_body, out_shape=jax.ShapeDtypeStruct((OWN, list_ro...  8.73 us
    pallas_call x1, Pallas kernels, shards(): pl.pallas_call(home_body, out_shape=(jax.ShapeDtypeStruct((count, slots),...  5.26 us
    pallas_call x1, Pallas kernels, shards(): pl.pallas_call(combine_body, out_shape=jax.ShapeDtypeStruct((count, D), B...  4.75 us
  transfers between devices with their start and end apart: 3, of which 3 were waited for; matrix products, arithmetic and copies ran while one was open for 1% of the time, Pallas kernels for 9%

profile of v5, /device:TPU:1, one launch (start us, length us, event | category | flops | bytes accessed | tf_op | source)
XLA Modules:
  0.0 207.3 jit_solution(9495287314036792489)
XLA Ops:
  0.6 0.0 copy-start
  0.6 4.4 %dispatch.1 = bf16[2048,768]{1,0:T(8,128)(2,1)} custom-call(s32[4,256]{1,0:T(4,128)} %bitcast.34, bf16[256,768]{1,0:T(8,128)(2,1)} %queries.1), custom_call_target="tpu_custom_call" | custom-call | tf_op jit(solution)/shard_map/dispatch/pallas_call | solution.py:363
  5.1 0.0 copy-start.2
  5.1 0.0 copy-start.1
  5.1 11.9 %all-to-all-start = ((bf16[128,16,768]{2,1,0:T(8,128)(2,1)}), bf16[128,16,768]{2,1,0:T(8,128)(2,1)}, u32[]{:S(2)}, u32[]{:S(2)}) async-start(bf16[128,16,768]{2,1,0:T(8,128)(2,1)} %bitcast.26), calls=%async_computation | async-start | bytes 6291456 | tf_op jit(solution)/shard_map/all_to_all | solution.py:336
  17.0 0.0 copy-done.2
  17.0 0.8 copy.13.probes
  17.8 0.0 copy-done.1
  17.8 0.0 copy-done
  17.8 0.8 copy.14.targets_wide
  18.6 1.0 fusion
  19.7 5.3 %home.1 = (bf16[256,2048]{1,0:T(8,128)(2,1)}, bf16[16,128,256]{2,1,0:T(8,128)(2,1)}, f32[128,128]{1,0:T(8,128)}) custom-call(s32[4,256]{1,0:T(4,128)} %bitcast.35, s32[256,4]{1,0:T(8,128)} %copy.13.probes, s32[256,128]{1,0:T(8,128)} %copy.14.targets_wide), custom_call_target="tpu_custom_call" | custom-call | tf_op jit(solution)/shard_map/home/pallas_call | solution.py:375
  24.9 34.0 %all-to-all-done = bf16[128,16,768]{2,1,0:T(8,128)(2,1)} async-done(((bf16[128,16,768]{2,1,0:T(8,128)(2,1)}), bf16[128,16,768]{2,1,0:T(8,128)(2,1)}, u32[]{:S(2)}, u32[]{:S(2)}) %all-to-all-start) | async-done | bytes 3145760 | tf_op jit(solution)/shard_map/all_to_all | solution.py:336
  58.9 21.9 %score.1 = (f32[10,256,1024]{2,1,0:T(8,128)}, f32[256,128]{1,0:T(8,128)}) custom-call(s32[1]{0:T(128)} %bitcast.2.offset, bf16[2048,768]{1,0:T(8,128)(2,1)} %bitcast.4.got_far, bf16[6,256,128]{2,1,0:T(8,128)(2,1)} %get-tuple-element.13.high, bf16[6,256,128]{2,1,0:T(8,128)(2,1)} %get-tuple-element.12.low, f32[128,128]{1,0:T(8,128)} %get-tuple-element.8.notes, ...), custom_call_target="tpu_custom_call" | custom-call | tf_op jit(solution)/shard_map/score/pallas_call | solution.py:404
  80.8 15.2 %all_to_all.49 = f32[128,2,128]{2,1,0:T(2,128)} all-to-all(f32[128,2,128]{2,1,0:T(2,128)} %bitcast.32), channel_id=1, replica_groups=mesh['corpus'=32,'query'=4] {'corpus','query'}, dimensions={0} | all-to-all | bytes 262144 | tf_op jit(solution)/shard_map/all_to_all | solution.py:336
  95.9 3.4 %weigh.1 = f32[128,128]{1,0:T(8,128)} custom-call(f32[256,128]{1,0:T(8,128)} %bitcast.27, bf16[16,128,256]{2,1,0:T(8,128)(2,1)} %get-tuple-element.10.masks), custom_call_target="tpu_custom_call" | custom-call | tf_op jit(solution)/shard_map/weigh/pallas_call | solution.py:429
  99.4 4.0 %all-to-all-start.2 = ((f32[128,1,128]{2,1,0:T(1,128)}), f32[128,1,128]{2,1,0:T(1,128)S(1)}, u32[]{:S(2)}, u32[]{:S(2)}) async-start(f32[128,1,128]{2,1,0:T(1,128)} %bitcast.30), calls=%async_computation.2 | async-start | bytes 131072 | tf_op jit(solution)/shard_map/all_to_all | solution.py:336
  103.3 8.7 %teacher.1.teacher_odd.teacher_even = f32[8,256,1024]{2,1,0:T(8,128)} custom-call(f32[256,128]{1,0:T(8,128)} %bitcast.28), custom_call_target="tpu_custom_call" | custom-call | tf_op jit(solution)/shard_map/teacher/pallas_call | solution.py:435
  112.1 1.2 all-to-all-done.2
  113.2 24.3 %grad.1 = bf16[128,104,128]{2,1,0:T(8,128)(2,1)} custom-call(s32[1]{0:T(128)} %bitcast.2.offset, f32[128,128]{1,0:T(8,128)S(1)} %bitcast.24, bf16[2048,768]{1,0:T(8,128)(2,1)} %bitcast.4.got_far, bf16[6,256,128]{2,1,0:T(8,128)(2,1)} %get-tuple-element.13.high, bf16[6,256,128]{2,1,0:T(8,128)(2,1)} %get-tuple-element.12.low, ...), custom_call_target="tpu_custom_call" | custom-call | tf_op jit(solution)/shard_map/grad/pallas_call | solution.py:447
  137.6 53.7 %all_to_all.50.returned = bf16[128,104,128]{2,1,0:T(8,128)(2,1)} all-to-all(bf16[128,104,128]{2,1,0:T(8,128)(2,1)} %grad.1), channel_id=1, replica_groups=mesh['corpus'=32,'query'=4] {'corpus','query'}, dimensions={0} | all-to-all | bytes 6815744 | tf_op jit(solution)/shard_map/all_to_all | solution.py:336
  191.3 1.7 book_sum.1
  193.0 3.6 %all-to-all-start.4 = ((f32[128,1,128]{2,1,0:T(1,128)}), f32[128,1,128]{2,1,0:T(1,128)S(1)}, u32[]{:S(2)}, u32[]{:S(2)}) async-start(f32[128,1,128]{2,1,0:T(1,128)} %bitcast.29), calls=%async_computation.4 | async-start | bytes 131072 | tf_op jit(solution)/shard_map/all_to_all | solution.py:336
  196.6 4.8 %combine.1 = bf16[256,768]{1,0:T(8,128)(2,1)} custom-call(bf16[256,2048]{1,0:T(8,128)(2,1)} %get-tuple-element.7.chosen, bf16[128,104,128]{2,1,0:T(8,128)(2,1)} %all_to_all.50.returned), custom_call_target="tpu_custom_call" | custom-call | tf_op jit(solution)/shard_map/combine/pallas_call | solution.py:489
  201.4 5.2 %all-to-all-done.4 = f32[128,1,128]{2,1,0:T(1,128)S(1)} async-done(((f32[128,1,128]{2,1,0:T(1,128)}), f32[128,1,128]{2,1,0:T(1,128)S(1)}, u32[]{:S(2)}, u32[]{:S(2)}) %all-to-all-start.4) | async-done | bytes 65568 | tf_op jit(solution)/shard_map/all_to_all | solution.py:336
  206.5 0.8 book_norm.1
  (6 shorter events, 0.1 us)
Async XLA Ops:
  0.6 17.2 %copy-start = (s32[256,8]{0,1:T(8,128)S(1)}, s32[256,8]{0,1:T(8,128)}, u32[]{:S(2)}) copy-start(s32[256,8]{0,1:T(8,128)} %param.7) | copy-start | bytes 24580
  5.1 11.9 %copy-start.2 = (s32[256,4]{0,1:T(4,128)S(1)}, s32[256,4]{0,1:T(4,128)}, u32[]{:S(2)}) copy-start(s32[256,4]{0,1:T(4,128)} %param.6) | copy-start | bytes 12292
  5.1 12.7 %copy-start.1 = (f32[16,768]{1,0:T(8,128)S(1)}, f32[16,768]{1,0:T(8,128)}, u32[]{:S(2)}) copy-start(f32[16,768]{1,0:T(8,128)} %param.9) | copy-start | bytes 147460
  5.1 53.8 %all-to-all-start = ((bf16[128,16,768]{2,1,0:T(8,128)(2,1)}), bf16[128,16,768]{2,1,0:T(8,128)(2,1)}, u32[]{:S(2)}, u32[]{:S(2)}) async-start(bf16[128,16,768]{2,1,0:T(8,128)(2,1)} %bitcast.26), calls=%async_computation | async-start | bytes 6291456 | tf_op jit(solution)/shard_map/all_to_all | solution.py:336
  99.4 13.9 %all-to-all-start.2 = ((f32[128,1,128]{2,1,0:T(1,128)}), f32[128,1,128]{2,1,0:T(1,128)S(1)}, u32[]{:S(2)}, u32[]{:S(2)}) async-start(f32[128,1,128]{2,1,0:T(1,128)} %bitcast.30), calls=%async_computation.2 | async-start | bytes 131072 | tf_op jit(solution)/shard_map/all_to_all | solution.py:336
  193.0 13.6 %all-to-all-start.4 = ((f32[128,1,128]{2,1,0:T(1,128)}), f32[128,1,128]{2,1,0:T(1,128)S(1)}, u32[]{:S(2)}, u32[]{:S(2)}) async-start(f32[128,1,128]{2,1,0:T(1,128)} %bitcast.29), calls=%async_computation.4 | async-start | bytes 131072 | tf_op jit(solution)/shard_map/all_to_all | solution.py:336

commit v6 on v5

--- a/solution.py
+++ b/solution.py
@@ -121,26 +121,25 @@
 
 def score_body(
     offset, got_far, high, low, notes, odd, even,
-    exps, message, table, hot_a, hot_b, held_a, held_b, stats, got, sems,
+    exps, message, table, hot_a, hot_b, held_a, held_b, stats, got, second, sem,
 ):
     s = pl.program_id(0)
     half = stats.shape[0]
 
-    def score(i, hot, held):
-        rows = jnp.concatenate(
-            [
-                jnp.concatenate(
-                    [
-                        table[j, pl.ds(r * OWN + i, half, stride=SLOTS), :].astype(BF16)
-                        for j in range(WIDTH // 128)
-                    ],
-                    axis=1,
-                )
-                for r in range(CAP)
-            ],
-            axis=0,
-        )
-        held[...] = dot(rows, hot[...])
+    def score(i, hot, held, ranks):
+        rows = [
+            jnp.concatenate(
+                [
+                    table[j, pl.ds(r * OWN + i, half, stride=SLOTS), :].astype(BF16)
+                    for j in range(WIDTH // 128)
+                ],
+                axis=1,
+            )
+            for r in range(ranks)
+        ]
+        held[0 : ranks * half, :] = dot(jnp.concatenate(rows, axis=0), hot[...])
+        if ranks < CAP:
+            held[ranks * half :, :] = jnp.zeros((held.shape[0] - ranks * half, PASSAGES), F32)
 
     def soften(i, held, place):
         scores = held[...]
@@ -160,33 +159,49 @@
 
     @pl.when(s == 0)
     def _():
-        copies = [
-            pltpu.make_async_copy(
-                got_far.at[:, c * FEATS : (c + 1) * FEATS], got.at[c], sems.at[c]
-            )
-            for c in range(CHUNKS)
-        ]
-        for copy in copies:
-            copy.start()
+        copy = pltpu.make_async_copy(got_far, got, sem)
+        copy.start()
         stats[...] = jnp.zeros_like(stats)
         held_b[...] = jnp.zeros_like(held_b)
         fill_one_hot(even, hot_a)
+        copy.wait()
         for c in range(CHUNKS):
-            copies[c].wait()
-            twice = jnp.concatenate([got[c], got[c]], axis=1)
+            rows = got[:, c * FEATS : (c + 1) * FEATS]
+            twice = jnp.concatenate([rows, rows], axis=1)
             weights = jnp.concatenate([high[c], low[c]], axis=1)
             looked = dot(twice, weights, ((1,), (1,)))
             table[2 * c] = looked[:, 0:128]
             table[2 * c + 1] = looked[:, 128:256]
-
-    @pl.when((s > 0) & (s < last))
-    def _():
-        score(2 * s - 2, hot_a, held_a)
+        size = jnp.zeros((SLOTS, FEATS), F32)
+        for c in range(CHUNKS):
+            rows = jnp.abs(got[:, c * FEATS : (c + 1) * FEATS])
+            while rows.shape[0] > SLOTS:
+                middle = rows.shape[0] // 2
+                rows = jnp.maximum(rows[:middle], rows[middle:])
+            size = jnp.maximum(size, rows.astype(F32))
+        slot = iota(size.shape, 0)
+        for pair in range(OWN // 2):
+            at = OWN + 2 * pair
+            second[pair] = jnp.max(jnp.where((slot == at) | (slot == at + 1), size, 0.0))
+
+    def step(ranks):
+        score(2 * s - 2, hot_a, held_a, ranks)
         fill_one_hot(odd, hot_b)
         soften(2 * s - 3, held_b, 0)
-        score(2 * s - 1, hot_b, held_b)
+        score(2 * s - 1, hot_b, held_b, ranks)
         fill_one_hot(even, hot_a)
         soften(2 * s - 2, held_a, 1)
+
+    inside = (s > 0) & (s < last)
+    filled = second[jnp.clip(s - 1, 0, OWN // 2 - 1)] > 0.0
+
+    @pl.when(inside & filled)
+    def _():
+        step(CAP)
+
+    @pl.when(inside & jnp.logical_not(filled))
+    def _():
+        step(1)
 
     @pl.when(s == last)
     def _():
@@ -232,8 +247,8 @@
 
 
 def grad_body(
-    offset, weights, got_far, high, low, exps_odd, exps_even, teacher_odd, teacher_even,
-    odd, even, out, hist, hot_a, hot_b, grads_a, grads_b, got, sems,
+    offset, weights, message, got_far, high, low, exps_odd, exps_even, teacher_odd, teacher_even,
+    odd, even, out, hist, hot_a, hot_b, grads_a, grads_b, got, second, sems,
 ):
     s = pl.program_id(0)
     half = weights.shape[0]
@@ -247,9 +262,9 @@
             grads[rows, :] = (exps[0, rows, :] * scale - teacher[0, rows, :]).astype(BF16)
         fill_one_hot(codes, hot)
 
-    def count(i, hot, grads):
-        found = dot(grads[...], hot[...], ((1,), (1,)))
-        for r in range(CAP):
+    def count(i, hot, grads, ranks):
+        found = dot(grads[0 : ranks * half, :], hot[...], ((1,), (1,)))
+        for r in range(ranks):
             for j in range(WIDTH // 128):
                 hist[j, pl.ds(r * OWN + i, half, stride=SLOTS), :] = found[
                     r * half : (r + 1) * half, j * 128 : (j + 1) * 128
@@ -266,13 +281,33 @@
         prepare(0, exps_even, teacher_even, even, hot_a, grads_a)
         for copy in copies:
             copy.start()
-
-    @pl.when(s > 0)
-    def _():
-        count(2 * s - 2, hot_a, grads_a)
+        for row in range(half):
+            at = row * SLOTS + OWN
+            hist[:, at : at + OWN, :] = jnp.zeros((hist.shape[0], OWN, 128), F32)
+        weight = jnp.max(jnp.abs(weights[...]), axis=0, keepdims=True)
+        note = jnp.max(message[pl.ds(1, half, stride=2), :], axis=0, keepdims=True)
+        lane = iota(weight.shape, 1)
+        for pair in range(OWN // 2):
+            at = OWN + 2 * pair
+            held = jnp.where((lane == at) | (lane == at + 1), weight, 0.0)
+            noted = jnp.where(lane // (2 * TARGETS) == at // 2, note, 0.0)
+            second[pair] = jnp.maximum(jnp.max(held), jnp.max(noted))
+
+    def step(ranks):
+        count(2 * s - 2, hot_a, grads_a, ranks)
         prepare(2 * s - 1, exps_odd, teacher_odd, odd, hot_b, grads_b)
-        count(2 * s - 1, hot_b, grads_b)
+        count(2 * s - 1, hot_b, grads_b, ranks)
         prepare(following, exps_even, teacher_even, even, hot_a, grads_a)
+
+    filled = second[jnp.maximum(s - 1, 0)] > 0.0
+
+    @pl.when((s > 0) & filled)
+    def _():
+        step(CAP)
+
+    @pl.when((s > 0) & jnp.logical_not(filled))
+    def _():
+        step(1)
 
     @pl.when(s == pl.num_programs(0) - 1)
     def _():
@@ -419,7 +454,12 @@
             ],
             scratch_shapes=[table, hot, hot]
             + [pltpu.VMEM((list_rows, PASSAGES), F32)] * 2
-            + [pltpu.VMEM(square.shape, F32), arrived_here, pltpu.SemaphoreType.DMA((CHUNKS,))],
+            + [
+                pltpu.VMEM(square.shape, F32),
+                pltpu.VMEM((slots, D), BF16),
+                pltpu.SMEM((OWN // 2,), F32),
+                pltpu.SemaphoreType.DMA(()),
+            ],
         ),
         compiler_params=big,
         name="score",
@@ -452,6 +492,7 @@
             grid=(OWN // 2 + 1,),
             in_specs=[
                 whole(square.shape),
+                whole((2 * devices, 128)),
                 arrived,
                 table_spec,
                 table_spec,
@@ -462,12 +503,12 @@
             out_specs=whole((devices, CHUNKS * SLOTS + BOOK_ROWS, FEATS)),
             scratch_shapes=[table, hot, hot]
             + [pltpu.VMEM((list_rows, PASSAGES), BF16)] * 2
-            + [arrived_here, pltpu.SemaphoreType.DMA((CHUNKS,))],
+            + [arrived_here, pltpu.SMEM((OWN // 2,), F32), pltpu.SemaphoreType.DMA((CHUNKS,))],
         ),
         compiler_params=big,
         name="grad",
     )(
-        offset, uncopied(exchange(weights)), got, high, low,
+        offset, uncopied(exchange(weights)), message, got, high, low,
         exps, exps, teacher, teacher, *codes,
     )
 

time: 208 us -> 200 us (0.962)
  Pallas kernels: 75.3 us -> 67.7 us
    pallas_call x1, Pallas kernels: 21.9 us -> 16 us  [shards(): pl.pallas_call(score_body, out_shape=(jax.ShapeDtypeStruct((OWN + 2, list...]
where the time goes in v6:
time: 200 us
  blocking collectives  68.7 us (34%)
  Pallas kernels  67.7 us (34%)
  waiting for transfers between devices  40.4 us (20%)
  starting transfers between devices  19.7 us (10%)
    all_to_all x2, blocking collectives, exchange(): return lax.all_to_all(value, BOTH, 0, 0, tiled=True)  68.7 us
    all_to_all x3, waiting for transfers between devices, exchange(): return lax.all_to_all(value, BOTH, 0, 0, tiled=True)  40.4 us
    pallas_call x1, Pallas kernels, shards(): pl.pallas_call(grad_body, out_shape=jax.ShapeDtypeStruct((devices, CHUNKS...  22.6 us
    all_to_all x3, starting transfers between devices, exchange(): return lax.all_to_all(value, BOTH, 0, 0, tiled=True)  19.7 us
    pallas_call x1, Pallas kernels, shards(): pl.pallas_call(score_body, out_shape=(jax.ShapeDtypeStruct((OWN + 2, list...  16 us
    pallas_call x1, Pallas kernels, shards(): pl.pallas_call(teacher_body, out_shape=jax.ShapeDtypeStruct((OWN, list_ro...  8.73 us
    pallas_call x1, Pallas kernels, shards(): pl.pallas_call(home_body, out_shape=(jax.ShapeDtypeStruct((count, slots),...  5.27 us
    pallas_call x1, Pallas kernels, shards(): pl.pallas_call(combine_body, out_shape=jax.ShapeDtypeStruct((count, D), B...  4.75 us
  transfers between devices with their start and end apart: 3, of which 3 were waited for; matrix products, arithmetic and copies ran while one was open for 1% of the time, Pallas kernels for 9%

profile of v6, /device:TPU:1, one launch (start us, length us, event | category | flops | bytes accessed | tf_op | source)
XLA Modules:
  0.0 199.9 jit_solution(8025943521839361579)
XLA Ops:
  0.6 0.0 copy-start
  0.6 4.4 %dispatch.1 = bf16[2048,768]{1,0:T(8,128)(2,1)} custom-call(s32[4,256]{1,0:T(4,128)} %bitcast.35, bf16[256,768]{1,0:T(8,128)(2,1)} %queries.1), custom_call_target="tpu_custom_call" | custom-call | tf_op jit(solution)/shard_map/dispatch/pallas_call | solution.py:398
  5.1 0.0 copy-start.2
  5.1 0.0 copy-start.1
  5.1 11.9 %all-to-all-start = ((bf16[128,16,768]{2,1,0:T(8,128)(2,1)}), bf16[128,16,768]{2,1,0:T(8,128)(2,1)}, u32[]{:S(2)}, u32[]{:S(2)}) async-start(bf16[128,16,768]{2,1,0:T(8,128)(2,1)} %bitcast.26), calls=%async_computation | async-start | bytes 6291456 | tf_op jit(solution)/shard_map/all_to_all | solution.py:371
  17.0 0.0 copy-done.2
  17.0 0.8 copy.13.probes
  17.8 0.0 copy-done.1
  17.8 0.0 copy-done
  17.8 0.8 copy.14.targets_wide
  18.6 1.0 fusion
  19.7 5.3 %home.1 = (bf16[256,2048]{1,0:T(8,128)(2,1)}, bf16[16,128,256]{2,1,0:T(8,128)(2,1)}, f32[128,128]{1,0:T(8,128)}) custom-call(s32[4,256]{1,0:T(4,128)} %bitcast.36, s32[256,4]{1,0:T(8,128)} %copy.13.probes, s32[256,128]{1,0:T(8,128)} %copy.14.targets_wide), custom_call_target="tpu_custom_call" | custom-call | tf_op jit(solution)/shard_map/home/pallas_call | solution.py:410
  24.9 33.9 %all-to-all-done = bf16[128,16,768]{2,1,0:T(8,128)(2,1)} async-done(((bf16[128,16,768]{2,1,0:T(8,128)(2,1)}), bf16[128,16,768]{2,1,0:T(8,128)(2,1)}, u32[]{:S(2)}, u32[]{:S(2)}) %all-to-all-start) | async-done | bytes 3145760 | tf_op jit(solution)/shard_map/all_to_all | solution.py:371
  58.9 16.0 %score.1 = (f32[10,256,1024]{2,1,0:T(8,128)}, f32[256,128]{1,0:T(8,128)}) custom-call(s32[1]{0:T(128)} %bitcast.2.offset, bf16[2048,768]{1,0:T(8,128)(2,1)} %bitcast.4.got_far, bf16[6,256,128]{2,1,0:T(8,128)(2,1)} %get-tuple-element.13.high, bf16[6,256,128]{2,1,0:T(8,128)(2,1)} %get-tuple-element.12.low, f32[128,128]{1,0:T(8,128)} %get-tuple-element.8.notes, ...), custom_call_target="tpu_custom_call" | custom-call | tf_op jit(solution)/shard_map/score/pallas_call | solution.py:439
  74.9 15.0 %all_to_all.49 = f32[128,2,128]{2,1,0:T(2,128)} all-to-all(f32[128,2,128]{2,1,0:T(2,128)} %bitcast.33), channel_id=1, replica_groups=mesh['corpus'=32,'query'=4] {'corpus','query'}, dimensions={0} | all-to-all | bytes 262144 | tf_op jit(solution)/shard_map/all_to_all | solution.py:371
  89.8 3.4 %weigh.1 = f32[128,128]{1,0:T(8,128)} custom-call(f32[256,128]{1,0:T(8,128)} %bitcast.27, bf16[16,128,256]{2,1,0:T(8,128)(2,1)} %get-tuple-element.10.masks), custom_call_target="tpu_custom_call" | custom-call | tf_op jit(solution)/shard_map/weigh/pallas_call | solution.py:469
  93.3 4.1 %all-to-all-start.2 = ((f32[128,1,128]{2,1,0:T(1,128)}), f32[128,1,128]{2,1,0:T(1,128)S(1)}, u32[]{:S(2)}, u32[]{:S(2)}) async-start(f32[128,1,128]{2,1,0:T(1,128)} %bitcast.31), calls=%async_computation.2 | async-start | bytes 131072 | tf_op jit(solution)/shard_map/all_to_all | solution.py:371
  97.4 8.7 %teacher.1.teacher_odd.teacher_even = f32[8,256,1024]{2,1,0:T(8,128)} custom-call(f32[256,128]{1,0:T(8,128)} %bitcast.28), custom_call_target="tpu_custom_call" | custom-call | tf_op jit(solution)/shard_map/teacher/pallas_call | solution.py:475
  106.1 1.2 all-to-all-done.2
  107.3 22.6 %grad.1 = bf16[128,104,128]{2,1,0:T(8,128)(2,1)} custom-call(s32[1]{0:T(128)} %bitcast.2.offset, f32[128,128]{1,0:T(8,128)S(1)} %bitcast.24, f32[256,128]{1,0:T(8,128)} %bitcast.29, bf16[2048,768]{1,0:T(8,128)(2,1)} %bitcast.4.got_far, bf16[6,256,128]{2,1,0:T(8,128)(2,1)} %get-tuple-element.13.high, bf16[6,256,128]{2,1,0:T(8,128)(2,1)} %get-tuple-element.12.low, ...), custom_call_target="tpu_custom_call" | custom-call | tf_op jit(solution)/shard_map/grad/pallas_call | solution.py:487
  129.9 53.7 %all_to_all.50.returned = bf16[128,104,128]{2,1,0:T(8,128)(2,1)} all-to-all(bf16[128,104,128]{2,1,0:T(8,128)(2,1)} %grad.1), channel_id=1, replica_groups=mesh['corpus'=32,'query'=4] {'corpus','query'}, dimensions={0} | all-to-all | bytes 6815744 | tf_op jit(solution)/shard_map/all_to_all | solution.py:371
  183.7 1.7 book_sum.1
  185.4 3.7 %all-to-all-start.4 = ((f32[128,1,128]{2,1,0:T(1,128)}), f32[128,1,128]{2,1,0:T(1,128)S(1)}, u32[]{:S(2)}, u32[]{:S(2)}) async-start(f32[128,1,128]{2,1,0:T(1,128)} %bitcast.30), calls=%async_computation.4 | async-start | bytes 131072 | tf_op jit(solution)/shard_map/all_to_all | solution.py:371
  189.1 4.8 %combine.1 = bf16[256,768]{1,0:T(8,128)(2,1)} custom-call(bf16[256,2048]{1,0:T(8,128)(2,1)} %get-tuple-element.7.chosen, bf16[128,104,128]{2,1,0:T(8,128)(2,1)} %all_to_all.50.returned), custom_call_target="tpu_custom_call" | custom-call | tf_op jit(solution)/shard_map/combine/pallas_call | solution.py:530
  193.8 5.3 %all-to-all-done.4 = f32[128,1,128]{2,1,0:T(1,128)S(1)} async-done(((f32[128,1,128]{2,1,0:T(1,128)}), f32[128,1,128]{2,1,0:T(1,128)S(1)}, u32[]{:S(2)}, u32[]{:S(2)}) %all-to-all-start.4) | async-done | bytes 65568 | tf_op jit(solution)/shard_map/all_to_all | solution.py:371
  199.1 0.8 book_norm.1
  (6 shorter events, 0.1 us)
Async XLA Ops:
  0.6 17.2 %copy-start = (s32[256,8]{0,1:T(8,128)S(1)}, s32[256,8]{0,1:T(8,128)}, u32[]{:S(2)}) copy-start(s32[256,8]{0,1:T(8,128)} %param.7) | copy-start | bytes 24580
  5.1 11.9 %copy-start.2 = (s32[256,4]{0,1:T(4,128)S(1)}, s32[256,4]{0,1:T(4,128)}, u32[]{:S(2)}) copy-start(s32[256,4]{0,1:T(4,128)} %param.6) | copy-start | bytes 12292
  5.1 12.7 %copy-start.1 = (f32[16,768]{1,0:T(8,128)S(1)}, f32[16,768]{1,0:T(8,128)}, u32[]{:S(2)}) copy-start(f32[16,768]{1,0:T(8,128)} %param.9) | copy-start | bytes 147460
  5.1 53.8 %all-to-all-start = ((bf16[128,16,768]{2,1,0:T(8,128)(2,1)}), bf16[128,16,768]{2,1,0:T(8,128)(2,1)}, u32[]{:S(2)}, u32[]{:S(2)}) async-start(bf16[128,16,768]{2,1,0:T(8,128)(2,1)} %bitcast.26), calls=%async_computation | async-start | bytes 6291456 | tf_op jit(solution)/shard_map/all_to_all | solution.py:371
  93.3 14.0 %all-to-all-start.2 = ((f32[128,1,128]{2,1,0:T(1,128)}), f32[128,1,128]{2,1,0:T(1,128)S(1)}, u32[]{:S(2)}, u32[]{:S(2)}) async-start(f32[128,1,128]{2,1,0:T(1,128)} %bitcast.31), calls=%async_computation.2 | async-start | bytes 131072 | tf_op jit(solution)/shard_map/all_to_all | solution.py:371
  185.4 13.8 %all-to-all-start.4 = ((f32[128,1,128]{2,1,0:T(1,128)}), f32[128,1,128]{2,1,0:T(1,128)S(1)}, u32[]{:S(2)}, u32[]{:S(2)}) async-start(f32[128,1,128]{2,1,0:T(1,128)} %bitcast.30), calls=%async_computation.4 | async-start | bytes 131072 | tf_op jit(solution)/shard_map/all_to_all | solution.py:371

commit v7 on v6

--- a/solution.py
+++ b/solution.py
@@ -52,13 +52,17 @@
     return found
 
 
-def dispatch_body(probes_t, queries, sending):
+def dispatch_body(probes_t, queries, sending, before):
     count = queries.shape[0]
     rows = sending.shape[0] // CAP
     lists = iota((rows, count), 0) + pl.program_id(0) * rows
     found = names_list(probes_t[...], lists)
-    before = ones_where(iota((count, count), 0) < iota((count, count), 1))
-    rank = dot(ones_where(found), before)
+
+    @pl.when(pl.program_id(0) == 0)
+    def _():
+        before[...] = ones_where(iota((count, count), 0) < iota((count, count), 1))
+
+    rank = dot(ones_where(found), before[...])
     chosen = [
         jnp.where(found & (rank == float(r)), 1.0, 0.0).reshape(rows // OWN, 1, OWN, count)
         for r in range(CAP)
@@ -67,7 +71,7 @@
     sending[...] = dot(chosen, queries[...]).astype(BF16)
 
 
-def home_body(probes_t, probes, targets_wide, chosen_out, masks_out, notes_out):
+def home_body(probes_t, probes, targets_wide, chosen_out, masks_out, notes_out, used_out):
     count = probes.shape[0]
     slots = chosen_out.shape[1]
     devices = notes_out.shape[0]
@@ -101,6 +105,7 @@
         for r in range(CAP):
             mask = ones_where(found & (rank == float(r)))
             masks_out[r * OWN + i] = mask
+            used_out[r * OWN + i] = jnp.max(mask.astype(F32)).astype(jnp.int32)
             here = dot(mask, parts)
             gathered = jnp.where(lane_wide // TARGETS == r * OWN + i, here, gathered)
     got_list = gathered[:, 0:128] * 32.0 + gathered[:, 128:256]
@@ -210,26 +215,53 @@
         message[...] = jnp.stack([stats[...], notes[...]], axis=1).reshape(message.shape)
 
 
-def weight_body(stats, masks, weights, ratios):
-    devices, count = masks.shape[1:]
+def weight_body(used, stats, masks, weights, ratios, peaks, totals):
+    devices, _ = masks.shape[1:]
     tops = stats[pl.ds(0, devices, stride=2), :]
-    low = -3.0e38
-    peak = jnp.full((devices, count), low, F32)
-    for s in range(SLOTS):
-        peak = jnp.maximum(peak, jnp.where(masks[s] > 0, tops[:, s : s + 1], low))
-    peak = jnp.max(peak, axis=0, keepdims=True)
-    denom = jnp.zeros((devices, count), F32)
-    for s in range(SLOTS):
+    lane = iota((devices, 128), 1)
+
+    def each_second(body):
+        for s in range(OWN, SLOTS):
+            pl.when(used[s] > 0)(lambda s=s: body(s))
+
+    def top_of(s):
+        return jnp.where(masks[s] > 0, tops[:, s : s + 1], -3.0e38)
+
+    peak = top_of(0)
+    for s in range(1, OWN):
+        peak = jnp.maximum(peak, top_of(s))
+    peaks[...] = peak
+
+    @each_second
+    def _(s):
+        peaks[...] = jnp.maximum(peaks[...], top_of(s))
+
+    peak = jnp.max(peaks[...], axis=0, keepdims=True)
+
+    def total_of(s):
         ratio = jnp.where(masks[s] > 0, jnp.exp(tops[:, s : s + 1] - peak), 0.0)
         ratios[s] = ratio
-        denom = denom + ratio * tops[:, SLOTS + s : SLOTS + 1 + s]
-    denom = jnp.sum(denom, axis=0, keepdims=True)
-    lane = iota((devices, 128), 1)
+        return ratio * tops[:, SLOTS + s : SLOTS + 1 + s]
+
+    total = total_of(0)
+    for s in range(1, OWN):
+        total = total + total_of(s)
+    totals[...] = total
+
+    @each_second
+    def _(s):
+        totals[...] = totals[...] + total_of(s)
+
+    share = 1.0 / jnp.sum(totals[...], axis=0, keepdims=True)
     held = jnp.zeros((devices, 128), F32)
-    for s in range(SLOTS):
-        part = jnp.sum(ratios[s] / denom, axis=1, keepdims=True)
-        held = jnp.where(lane == s, part, held)
+    for s in range(OWN):
+        held = jnp.where(lane == s, jnp.sum(ratios[s] * share, axis=1, keepdims=True), held)
     weights[...] = held
+
+    @each_second
+    def _(s):
+        part = jnp.sum(ratios[s] * share, axis=1, keepdims=True)
+        weights[...] = jnp.where(lane == s, part, weights[...])
 
 
 def teacher_body(message, teacher):
@@ -237,13 +269,26 @@
     half = message.shape[0] // 2
     turned = pltpu.roll(message[pl.ds(1, half, stride=2), :], (128 - TARGETS * i) % 128, 1)
     place = iota((half, PASSAGES), 1).astype(F32)
-    for r in range(CAP):
+
+    def fill(r):
         held = jnp.zeros((half, PASSAGES), F32)
         for t in range(TARGETS):
             at = r * OWN * TARGETS + t
             weight = 2.0 * (TARGETS - t) / (TARGETS * (TARGETS + 1.0))
             held = jnp.where(place == turned[:, at : at + 1] - 1.0, weight, held)
         teacher[0, r * half : (r + 1) * half, :] = held
+
+    fill(0)
+    at = OWN * TARGETS
+    noted = jnp.max(turned[:, at : at + TARGETS]) > 0.0
+
+    @pl.when(noted)
+    def _():
+        fill(1)
+
+    @pl.when(jnp.logical_not(noted))
+    def _():
+        teacher[0, half:, :] = jnp.zeros((half, PASSAGES), F32)
 
 
 def grad_body(
@@ -401,19 +446,24 @@
         grid=(4,),
         in_specs=[whole((PROBES, count)), whole((count, D))],
         out_specs=pl.BlockSpec((slots // 4, D), lambda b: (b, 0)),
+        scratch_shapes=[pltpu.VMEM((count, count), BF16)],
         name="dispatch",
     )(probes_t, queries)
     got = uncopied(exchange(sending))
     arrived = pl.BlockSpec(memory_space=pl.ANY)
     arrived_here = pltpu.VMEM((CHUNKS, slots, FEATS), BF16)
 
-    chosen, masks, notes = pl.pallas_call(
+    here = pl.BlockSpec(memory_space=pltpu.VMEM)
+    scalars = pl.BlockSpec(memory_space=pltpu.SMEM)
+    chosen, masks, notes, used = pl.pallas_call(
         home_body,
         out_shape=(
             jax.ShapeDtypeStruct((count, slots), BF16),
             jax.ShapeDtypeStruct((SLOTS, devices, count), BF16),
             square,
+            jax.ShapeDtypeStruct((SLOTS,), jnp.int32),
         ),
+        out_specs=(here, here, here, scalars),
         name="home",
     )(probes_t, probes, jnp.tile(targets, (1, 128 // TARGETS)))
     high, low = spread_codebook(codebook)
@@ -469,9 +519,11 @@
     weights = pl.pallas_call(
         weight_body,
         out_shape=square,
-        scratch_shapes=[pltpu.VMEM((SLOTS, devices, count), F32)],
+        in_specs=[scalars, here, here],
+        scratch_shapes=[pltpu.VMEM((SLOTS, devices, count), F32)]
+        + [pltpu.VMEM((devices, count), F32)] * 2,
         name="weigh",
-    )(message, masks)
+    )(used, message, masks)
     teacher = pl.pallas_call(
         teacher_body,
         out_shape=jax.ShapeDtypeStruct((OWN, list_rows, PASSAGES), F32),

time: 200 us -> 199 us (level)
  no operation moved by 1% of the time
where the time goes in v7:
time: 199 us
  blocking collectives  67.3 us (34%)
  Pallas kernels  66.9 us (34%)
  waiting for transfers between devices  41.4 us (21%)
  starting transfers between devices  19.7 us (10%)
    all_to_all x2, blocking collectives, exchange(): return lax.all_to_all(value, BOTH, 0, 0, tiled=True)  67.3 us
    all_to_all x3, waiting for transfers between devices, exchange(): return lax.all_to_all(value, BOTH, 0, 0, tiled=True)  41.4 us
    pallas_call x1, Pallas kernels, shards(): pl.pallas_call(grad_body, out_shape=jax.ShapeDtypeStruct((devices, CHUNKS...  22.6 us
    all_to_all x3, starting transfers between devices, exchange(): return lax.all_to_all(value, BOTH, 0, 0, tiled=True)  19.7 us
    pallas_call x1, Pallas kernels, shards(): pl.pallas_call(score_body, out_shape=(jax.ShapeDtypeStruct((OWN + 2, list...  16 us
    pallas_call x1, Pallas kernels, shards(): pl.pallas_call(teacher_body, out_shape=jax.ShapeDtypeStruct((OWN, list_ro...  7.34 us
    pallas_call x1, Pallas kernels, shards(): pl.pallas_call(home_body, out_shape=(jax.ShapeDtypeStruct((count, slots),...  5.71 us
    pallas_call x1, Pallas kernels, shards(): pl.pallas_call(dispatch_body, out_shape=jax.ShapeDtypeStruct((slots, D),...  4.81 us
  transfers between devices with their start and end apart: 3, of which 3 were waited for; matrix products, arithmetic and copies ran while one was open for 1% of the time, Pallas kernels for 9%

profile of v7, /device:TPU:1, one launch (start us, length us, event | category | flops | bytes accessed | tf_op | source)
XLA Modules:
  0.0 198.7 jit_solution(8016097921517507980)
XLA Ops:
  0.6 0.0 copy-start
  0.6 4.8 %dispatch.1 = bf16[2048,768]{1,0:T(8,128)(2,1)} custom-call(s32[4,256]{1,0:T(4,128)} %bitcast.35, bf16[256,768]{1,0:T(8,128)(2,1)} %queries.1), custom_call_target="tpu_custom_call" | custom-call | tf_op jit(solution)/shard_map/dispatch/pallas_call | solution.py:443
  5.5 0.0 copy-start.2
  5.5 0.0 copy-start.1
  5.5 11.9 %all-to-all-start = ((bf16[128,16,768]{2,1,0:T(8,128)(2,1)}), bf16[128,16,768]{2,1,0:T(8,128)(2,1)}, u32[]{:S(2)}, u32[]{:S(2)}) async-start(bf16[128,16,768]{2,1,0:T(8,128)(2,1)} %bitcast.26), calls=%async_computation | async-start | bytes 6291456 | tf_op jit(solution)/shard_map/all_to_all | solution.py:416
  17.4 0.0 copy-done.2
  17.4 0.8 copy.13.probes
  18.2 0.0 copy-done.1
  18.2 0.0 copy-done
  18.2 0.8 copy.14.targets_wide
  19.0 1.0 fusion
  20.0 5.7 %home.1 = (bf16[256,2048]{1,0:T(8,128)(2,1)}, bf16[16,128,256]{2,1,0:T(8,128)(2,1)}, f32[128,128]{1,0:T(8,128)}, s32[16]{0:T(128)}) custom-call(s32[4,256]{1,0:T(4,128)} %bitcast.36, s32[256,4]{1,0:T(8,128)} %copy.13.probes, s32[256,128]{1,0:T(8,128)} %copy.14.targets_wide), custom_call_target="tpu_custom_call" | custom-call | tf_op jit(solution)/shard_map/home/pallas_call | solution.py:458
  25.8 33.5 %all-to-all-done = bf16[128,16,768]{2,1,0:T(8,128)(2,1)} async-done(((bf16[128,16,768]{2,1,0:T(8,128)(2,1)}), bf16[128,16,768]{2,1,0:T(8,128)(2,1)}, u32[]{:S(2)}, u32[]{:S(2)}) %all-to-all-start) | async-done | bytes 3145760 | tf_op jit(solution)/shard_map/all_to_all | solution.py:416
  59.3 16.0 %score.1 = (f32[10,256,1024]{2,1,0:T(8,128)}, f32[256,128]{1,0:T(8,128)}) custom-call(s32[1]{0:T(128)} %bitcast.2.offset, bf16[2048,768]{1,0:T(8,128)(2,1)} %bitcast.4.got_far, bf16[6,256,128]{2,1,0:T(8,128)(2,1)} %get-tuple-element.15.high, bf16[6,256,128]{2,1,0:T(8,128)(2,1)} %get-tuple-element.14.low, f32[128,128]{1,0:T(8,128)} %get-tuple-element.10.notes, ...), custom_call_target="tpu_custom_call" | custom-call | tf_op jit(solution)/shard_map/score/pallas_call | solution.py:489
  75.2 15.0 %all_to_all.49 = f32[128,2,128]{2,1,0:T(2,128)} all-to-all(f32[128,2,128]{2,1,0:T(2,128)} %bitcast.33), channel_id=1, replica_groups=mesh['corpus'=32,'query'=4] {'corpus','query'}, dimensions={0} | all-to-all | bytes 262144 | tf_op jit(solution)/shard_map/all_to_all | solution.py:416
  90.2 3.2 %weigh.1 = f32[128,128]{1,0:T(8,128)} custom-call(s32[16]{0:T(128)} %get-tuple-element.9.used, f32[256,128]{1,0:T(8,128)} %bitcast.27, bf16[16,128,256]{2,1,0:T(8,128)(2,1)} %get-tuple-element.12.masks), custom_call_target="tpu_custom_call" | custom-call | tf_op jit(solution)/shard_map/weigh/pallas_call | solution.py:519
  93.4 4.1 %all-to-all-start.2 = ((f32[128,1,128]{2,1,0:T(1,128)}), f32[128,1,128]{2,1,0:T(1,128)S(1)}, u32[]{:S(2)}, u32[]{:S(2)}) async-start(f32[128,1,128]{2,1,0:T(1,128)} %bitcast.31), calls=%async_computation.2 | async-start | bytes 131072 | tf_op jit(solution)/shard_map/all_to_all | solution.py:416
  97.5 7.3 %teacher.1.teacher_odd.teacher_even = f32[8,256,1024]{2,1,0:T(8,128)} custom-call(f32[256,128]{1,0:T(8,128)} %bitcast.28), custom_call_target="tpu_custom_call" | custom-call | tf_op jit(solution)/shard_map/teacher/pallas_call | solution.py:527
  104.8 2.6 %all-to-all-done.2 = f32[128,1,128]{2,1,0:T(1,128)S(1)} async-done(((f32[128,1,128]{2,1,0:T(1,128)}), f32[128,1,128]{2,1,0:T(1,128)S(1)}, u32[]{:S(2)}, u32[]{:S(2)}) %all-to-all-start.2) | async-done | bytes 65568 | tf_op jit(solution)/shard_map/all_to_all | solution.py:416
  107.4 22.6 %grad.1 = bf16[128,104,128]{2,1,0:T(8,128)(2,1)} custom-call(s32[1]{0:T(128)} %bitcast.2.offset, f32[128,128]{1,0:T(8,128)S(1)} %bitcast.24, f32[256,128]{1,0:T(8,128)} %bitcast.29, bf16[2048,768]{1,0:T(8,128)(2,1)} %bitcast.4.got_far, bf16[6,256,128]{2,1,0:T(8,128)(2,1)} %get-tuple-element.15.high, bf16[6,256,128]{2,1,0:T(8,128)(2,1)} %get-tuple-element.14.low, ...), custom_call_target="tpu_custom_call" | custom-call | tf_op jit(solution)/shard_map/grad/pallas_call | solution.py:539
  130.1 52.3 %all_to_all.50.returned = bf16[128,104,128]{2,1,0:T(8,128)(2,1)} all-to-all(bf16[128,104,128]{2,1,0:T(8,128)(2,1)} %grad.1), channel_id=1, replica_groups=mesh['corpus'=32,'query'=4] {'corpus','query'}, dimensions={0} | all-to-all | bytes 6815744 | tf_op jit(solution)/shard_map/all_to_all | solution.py:416
  182.4 1.7 book_sum.1
  184.1 3.7 %all-to-all-start.4 = ((f32[128,1,128]{2,1,0:T(1,128)}), f32[128,1,128]{2,1,0:T(1,128)S(1)}, u32[]{:S(2)}, u32[]{:S(2)}) async-start(f32[128,1,128]{2,1,0:T(1,128)} %bitcast.30), calls=%async_computation.4 | async-start | bytes 131072 | tf_op jit(solution)/shard_map/all_to_all | solution.py:416
  187.8 4.8 %combine.1 = bf16[256,768]{1,0:T(8,128)(2,1)} custom-call(bf16[256,2048]{1,0:T(8,128)(2,1)} %get-tuple-element.8.chosen, bf16[128,104,128]{2,1,0:T(8,128)(2,1)} %all_to_all.50.returned), custom_call_target="tpu_custom_call" | custom-call | tf_op jit(solution)/shard_map/combine/pallas_call | solution.py:582
  192.6 5.3 %all-to-all-done.4 = f32[128,1,128]{2,1,0:T(1,128)S(1)} async-done(((f32[128,1,128]{2,1,0:T(1,128)}), f32[128,1,128]{2,1,0:T(1,128)S(1)}, u32[]{:S(2)}, u32[]{:S(2)}) %all-to-all-start.4) | async-done | bytes 65568 | tf_op jit(solution)/shard_map/all_to_all | solution.py:416
  197.9 0.8 book_norm.1
  (6 shorter events, 0.1 us)
Async XLA Ops:
  0.6 17.6 %copy-start = (s32[256,8]{0,1:T(8,128)S(1)}, s32[256,8]{0,1:T(8,128)}, u32[]{:S(2)}) copy-start(s32[256,8]{0,1:T(8,128)} %param.7) | copy-start | bytes 24580
  5.5 11.9 %copy-start.2 = (s32[256,4]{0,1:T(4,128)S(1)}, s32[256,4]{0,1:T(4,128)}, u32[]{:S(2)}) copy-start(s32[256,4]{0,1:T(4,128)} %param.6) | copy-start | bytes 12292
  5.5 12.7 %copy-start.1 = (f32[16,768]{1,0:T(8,128)S(1)}, f32[16,768]{1,0:T(8,128)}, u32[]{:S(2)}) copy-start(f32[16,768]{1,0:T(8,128)} %param.9) | copy-start | bytes 147460
  5.5 53.8 %all-to-all-start = ((bf16[128,16,768]{2,1,0:T(8,128)(2,1)}), bf16[128,16,768]{2,1,0:T(8,128)(2,1)}, u32[]{:S(2)}, u32[]{:S(2)}) async-start(bf16[128,16,768]{2,1,0:T(8,128)(2,1)} %bitcast.26), calls=%async_computation | async-start | bytes 6291456 | tf_op jit(solution)/shard_map/all_to_all | solution.py:416
  93.4 14.0 %all-to-all-start.2 = ((f32[128,1,128]{2,1,0:T(1,128)}), f32[128,1,128]{2,1,0:T(1,128)S(1)}, u32[]{:S(2)}, u32[]{:S(2)}) async-start(f32[128,1,128]{2,1,0:T(1,128)} %bitcast.31), calls=%async_computation.2 | async-start | bytes 131072 | tf_op jit(solution)/shard_map/all_to_all | solution.py:416
  184.1 13.8 %all-to-all-start.4 = ((f32[128,1,128]{2,1,0:T(1,128)}), f32[128,1,128]{2,1,0:T(1,128)S(1)}, u32[]{:S(2)}, u32[]{:S(2)}) async-start(f32[128,1,128]{2,1,0:T(1,128)} %bitcast.30), calls=%async_computation.4 | async-start | bytes 131072 | tf_op jit(solution)/shard_map/all_to_all | solution.py:416

commit v8 on v7

--- a/solution.py
+++ b/solution.py
@@ -52,17 +52,13 @@
     return found
 
 
-def dispatch_body(probes_t, queries, sending, before):
+def dispatch_body(probes_t, queries, sending):
     count = queries.shape[0]
     rows = sending.shape[0] // CAP
     lists = iota((rows, count), 0) + pl.program_id(0) * rows
     found = names_list(probes_t[...], lists)
-
-    @pl.when(pl.program_id(0) == 0)
-    def _():
-        before[...] = ones_where(iota((count, count), 0) < iota((count, count), 1))
-
-    rank = dot(ones_where(found), before[...])
+    before = ones_where(iota((count, count), 0) < iota((count, count), 1))
+    rank = dot(ones_where(found), before)
     chosen = [
         jnp.where(found & (rank == float(r)), 1.0, 0.0).reshape(rows // OWN, 1, OWN, count)
         for r in range(CAP)
@@ -291,9 +287,19 @@
         teacher[0, half:, :] = jnp.zeros((half, PASSAGES), F32)
 
 
+def regroup_body(got, rows):
+    size = got.shape[0]
+    row, column = iota((size, size), 0), iota((size, size), 1)
+    turn = ones_where((row // SLOTS == column % SLOTS) & (row % SLOTS == column // SLOTS))
+    turned = dot(turn, got[...]).astype(BF16)
+    for slot in range(SLOTS):
+        rows[slot] = turned[slot * SLOTS : (slot + 1) * SLOTS, :]
+
+
 def grad_body(
     offset, weights, message, got_far, high, low, exps_odd, exps_even, teacher_odd, teacher_even,
-    odd, even, out, hist, hot_a, hot_b, grads_a, grads_b, got, second, sems,
+    odd, even, out, hist, hot_a, hot_b, grads_a, grads_b, got, second,
+    spread, books, sems,
 ):
     s = pl.program_id(0)
     half = weights.shape[0]
@@ -311,7 +317,8 @@
         found = dot(grads[0 : ranks * half, :], hot[...], ((1,), (1,)))
         for r in range(ranks):
             for j in range(WIDTH // 128):
-                hist[j, pl.ds(r * OWN + i, half, stride=SLOTS), :] = found[
+                at = pl.multiple_of((r * OWN + i) * half, half)
+                hist[j, pl.ds(at, half), :] = found[
                     r * half : (r + 1) * half, j * 128 : (j + 1) * 128
                 ]
 
@@ -328,7 +335,7 @@
             copy.start()
         for row in range(half):
             at = row * SLOTS + OWN
-            hist[:, at : at + OWN, :] = jnp.zeros((hist.shape[0], OWN, 128), F32)
+            spread[:, at : at + OWN, :] = jnp.zeros((CHUNKS, OWN, FEATS), F32)
         weight = jnp.max(jnp.abs(weights[...]), axis=0, keepdims=True)
         note = jnp.max(message[pl.ds(1, half, stride=2), :], axis=0, keepdims=True)
         lane = iota(weight.shape, 1)
@@ -354,10 +361,36 @@
     def _():
         step(1)
 
-    @pl.when(s == pl.num_programs(0) - 1)
+    last = s == pl.num_programs(0) - 1
+
+    def finish(slot, slots):
+        rows = slice(slot * half, (slot + slots) * half)
+        for c in range(CHUNKS):
+            h_high, h_low = split_two(
+                jnp.concatenate([hist[2 * c, rows, :], hist[2 * c + 1, rows, :]], axis=1)
+            )
+            both = jnp.concatenate([high[c], low[c]], axis=1)
+            wide = dot(h_high, both)
+            part = wide[:, 0:FEATS] + wide[:, FEATS:] + dot(h_low, high[c])
+            for j in range(slots):
+                spread[c, pl.ds(slot + j, half, stride=SLOTS), :] = part[j * half : (j + 1) * half]
+            book = dot(got[c, rows, :], h_high, ((0,), (0,)))
+            books[c] = book if slot == 0 else books[c] + book
+
+    @pl.when(last)
     def _():
         for copy in copies:
             copy.wait()
+        finish(0, OWN)
+
+    for pair in range(OWN // 2):
+
+        @pl.when(last & (second[pair] > 0.0))
+        def _(pair=pair):
+            finish(OWN + 2 * pair, 2)
+
+    @pl.when(last)
+    def _():
         devices = out.shape[0]
         keep = iota((ENTRIES, FEATS), 0) % 16 == iota((ENTRIES, FEATS), 1) // SUBDIM
         top = CHUNKS * SLOTS
@@ -365,15 +398,9 @@
             (devices - CHUNKS * CENTROIDS, BOOK_ROWS, 128), BF16
         )
         for c in range(CHUNKS):
-            h_high, h_low = split_two(jnp.concatenate([hist[2 * c], hist[2 * c + 1]], axis=1))
-            both = jnp.concatenate([high[c], low[c]], axis=1)
-            wide = dot(h_high, both)
-            part = wide[:, 0:FEATS] + wide[:, FEATS:] + dot(h_low, high[c])
-            out[:, c * SLOTS : (c + 1) * SLOTS, :] = part.reshape(devices, SLOTS, FEATS).astype(
-                BF16
-            )
-            book = dot(got[c], h_high, ((0,), (0,)))
-            book = jnp.where(keep, book.T, 0.0)
+            part = spread[c].reshape(devices, SLOTS, FEATS)
+            out[:, c * SLOTS : (c + 1) * SLOTS, :] = part.astype(BF16)
+            book = jnp.where(keep, books[c].T, 0.0)
             book = jnp.sum(book.reshape(CENTROIDS, 16, FEATS), axis=1)
             b_high = book.astype(BF16)
             b_rest = book - b_high.astype(F32)
@@ -446,7 +473,6 @@
         grid=(4,),
         in_specs=[whole((PROBES, count)), whole((count, D))],
         out_specs=pl.BlockSpec((slots // 4, D), lambda b: (b, 0)),
-        scratch_shapes=[pltpu.VMEM((count, count), BF16)],
         name="dispatch",
     )(probes_t, queries)
     got = uncopied(exchange(sending))
@@ -515,7 +541,15 @@
         name="score",
     )(offset, got, high, low, notes, *codes)
 
-    message = exchange(message)
+    message = uncopied(exchange(message))
+    regrouped = pl.pallas_call(
+        regroup_body,
+        out_shape=jax.ShapeDtypeStruct((SLOTS, devices, D), BF16),
+        grid=(devices // SLOTS,),
+        in_specs=[pl.BlockSpec((SLOTS * SLOTS, D), lambda b: (b, 0))],
+        out_specs=pl.BlockSpec((SLOTS, SLOTS, D), lambda b: (0, b, 0)),
+        name="regroup",
+    )(got).reshape(slots, D)
     weights = pl.pallas_call(
         weight_body,
         out_shape=square,
@@ -555,12 +589,18 @@
             out_specs=whole((devices, CHUNKS * SLOTS + BOOK_ROWS, FEATS)),
             scratch_shapes=[table, hot, hot]
             + [pltpu.VMEM((list_rows, PASSAGES), BF16)] * 2
-            + [arrived_here, pltpu.SMEM((OWN // 2,), F32), pltpu.SemaphoreType.DMA((CHUNKS,))],
+            + [
+                arrived_here,
+                pltpu.SMEM((OWN // 2,), F32),
+                pltpu.VMEM((CHUNKS, slots, FEATS), F32),
+                pltpu.VMEM((CHUNKS, FEATS, ENTRIES), F32),
+                pltpu.SemaphoreType.DMA((CHUNKS,)),
+            ],
         ),
         compiler_params=big,
         name="grad",
     )(
-        offset, uncopied(exchange(weights)), message, got, high, low,
+        offset, uncopied(exchange(weights)), message, regrouped, high, low,
         exps, exps, teacher, teacher, *codes,
     )
 

time: 199 us -> 200 us (level)
  waiting for transfers between devices: 41.4 us -> 39 us
    pallas_call x0 -> x1, Pallas kernels: none -> 4.56 us  [shards(): pl.pallas_call(regroup_body, out_shape=jax.ShapeDtypeStruct((SLOTS, devic...]
    pallas_call x1, Pallas kernels: 22.6 us -> 19.5 us  [shards(): pl.pallas_call(grad_body, out_shape=jax.ShapeDtypeStruct((devices, CHUNKS...]
    all_to_all x3, waiting for transfers between devices: 41.4 us -> 39 us  [exchange(): return lax.all_to_all(value, BOTH, 0, 0, tiled=True)]
  transfers between devices with their start and end apart: 3 -> 3, of which waited for: 3 -> 2; matrix products, arithmetic and copies ran while one was open for 1% -> 1% of each run, Pallas kernels for 9% -> 11%
where the time goes in v8:
time: 200 us; the launch traced here: 199 us
  blocking collectives  69 us (34%)
  Pallas kernels  66.8 us (33%)
  waiting for transfers between devices  39 us (20%)
  starting transfers between devices  19.3 us (10%)
  local copies, waits for them, and re-layouts  3.48 us (2%)
    all_to_all x2, blocking collectives, exchange(): return lax.all_to_all(value, BOTH, 0, 0, tiled=True)  69 us
    all_to_all x3, waiting for transfers between devices, exchange(): return lax.all_to_all(value, BOTH, 0, 0, tiled=True)  39 us
    pallas_call x1, Pallas kernels, shards(): pl.pallas_call(grad_body, out_shape=jax.ShapeDtypeStruct((devices, CHUNKS...  19.5 us
    all_to_all x3, starting transfers between devices, exchange(): return lax.all_to_all(value, BOTH, 0, 0, tiled=True)  19.3 us
    pallas_call x1, Pallas kernels, shards(): pl.pallas_call(score_body, out_shape=(jax.ShapeDtypeStruct((OWN + 2, list...  15.8 us
    pallas_call x1, Pallas kernels, shards(): pl.pallas_call(teacher_body, out_shape=jax.ShapeDtypeStruct((OWN, list_ro...  6.43 us
    pallas_call x1, Pallas kernels, shards(): pl.pallas_call(home_body, out_shape=(jax.ShapeDtypeStruct((count, slots),...  5.72 us
    pallas_call x1, Pallas kernels, shards(): pl.pallas_call(combine_body, out_shape=jax.ShapeDtypeStruct((count, D), B...  4.75 us
  transfers between devices with their start and end apart: 3, of which 2 were waited for; matrix products, arithmetic and copies ran while one was open for 1% of the time, Pallas kernels for 11%

profile of v8, /device:TPU:1, one launch (start us, length us, event | category | flops | bytes accessed | tf_op | source)
XLA Modules:
  0.0 199.4 jit_solution(5454978172882448869)
XLA Ops:
  0.6 0.0 copy-start
  0.6 4.4 %dispatch.1 = bf16[2048,768]{1,0:T(8,128)(2,1)} custom-call(s32[4,256]{1,0:T(4,128)} %bitcast.39, bf16[256,768]{1,0:T(8,128)(2,1)} %queries.1), custom_call_target="tpu_custom_call" | custom-call | tf_op jit(solution)/shard_map/dispatch/pallas_call | solution.py:470
  5.1 0.0 copy-start.4
  5.1 0.0 copy-start.3
  5.1 11.5 %all-to-all-start = ((bf16[128,16,768]{2,1,0:T(8,128)(2,1)}), bf16[128,16,768]{2,1,0:T(8,128)(2,1)S(1)}, u32[]{:S(2)}, u32[]{:S(2)}) async-start(bf16[128,16,768]{2,1,0:T(8,128)(2,1)} %bitcast.33), calls=%async_computation | async-start | bytes 6291456 | tf_op jit(solution)/shard_map/all_to_all | solution.py:443
  16.6 0.0 copy-done.4
  16.6 0.8 copy.13.probes
  17.4 0.0 copy-done.3
  17.4 0.0 copy-done
  17.4 0.7 copy.14.targets_wide
  18.2 1.0 fusion
  19.3 5.7 %home.1 = (bf16[256,2048]{1,0:T(8,128)(2,1)}, bf16[16,128,256]{2,1,0:T(8,128)(2,1)}, f32[128,128]{1,0:T(8,128)}, s32[16]{0:T(128)}) custom-call(s32[4,256]{1,0:T(4,128)} %bitcast.40, s32[256,4]{1,0:T(8,128)} %copy.13.probes, s32[256,128]{1,0:T(8,128)} %copy.14.targets_wide), custom_call_target="tpu_custom_call" | custom-call | tf_op jit(solution)/shard_map/home/pallas_call | solution.py:484
  25.0 33.8 %all-to-all-done = bf16[128,16,768]{2,1,0:T(8,128)(2,1)S(1)} async-done(((bf16[128,16,768]{2,1,0:T(8,128)(2,1)}), bf16[128,16,768]{2,1,0:T(8,128)(2,1)S(1)}, u32[]{:S(2)}, u32[]{:S(2)}) %all-to-all-start) | async-done | bytes 3145760 | tf_op jit(solution)/shard_map/all_to_all | solution.py:443
  58.8 0.0 copy-start.1
  58.8 15.8 %score.1 = (f32[10,256,1024]{2,1,0:T(8,128)}, f32[256,128]{1,0:T(8,128)}) custom-call(s32[1]{0:T(128)} %bitcast.2.offset, bf16[2048,768]{1,0:T(8,128)(2,1)S(1)} %bitcast.25, bf16[6,256,128]{2,1,0:T(8,128)(2,1)} %get-tuple-element.15.high, bf16[6,256,128]{2,1,0:T(8,128)(2,1)} %get-tuple-element.14.low, f32[128,128]{1,0:T(8,128)} %get-tuple-element.10.notes, ...), custom_call_target="tpu_custom_call" | custom-call | tf_op jit(solution)/shard_map/score/pallas_call | solution.py:515
  74.6 0.0 copy-done.1
  74.6 14.1 %all_to_all.49 = f32[128,2,128]{2,1,0:T(2,128)S(1)} all-to-all(f32[128,2,128]{2,1,0:T(2,128)} %bitcast.37), channel_id=1, replica_groups=mesh['corpus'=32,'query'=4] {'corpus','query'}, dimensions={0} | all-to-all | bytes 262144 | tf_op jit(solution)/shard_map/all_to_all | solution.py:443
  88.8 3.1 %weigh.1 = f32[128,128]{1,0:T(8,128)} custom-call(s32[16]{0:T(128)} %get-tuple-element.9.used, f32[256,128]{1,0:T(8,128)S(1)} %bitcast.27, bf16[16,128,256]{2,1,0:T(8,128)(2,1)} %get-tuple-element.12.masks), custom_call_target="tpu_custom_call" | custom-call | tf_op jit(solution)/shard_map/weigh/pallas_call | solution.py:553
  91.9 4.1 %all-to-all-start.2 = ((f32[128,1,128]{2,1,0:T(1,128)}), f32[128,1,128]{2,1,0:T(1,128)S(1)}, u32[]{:S(2)}, u32[]{:S(2)}) async-start(f32[128,1,128]{2,1,0:T(1,128)} %bitcast.34), calls=%async_computation.2 | async-start | bytes 131072 | tf_op jit(solution)/shard_map/all_to_all | solution.py:443
  95.9 0.0 copy-start.2
  96.0 1.9 copy-done.2
  97.8 4.6 %regroup.1 = bf16[16,128,768]{2,1,0:T(8,128)(2,1)} custom-call(bf16[2048,768]{1,0:T(8,128)(2,1)S(1)} %bitcast.26), custom_call_target="tpu_custom_call" | custom-call | tf_op jit(solution)/shard_map/regroup/pallas_call | solution.py:545
  102.4 6.4 %teacher.1.teacher_odd.teacher_even = f32[8,256,1024]{2,1,0:T(8,128)} custom-call(f32[256,128]{1,0:T(8,128)S(1)} %bitcast.28), custom_call_target="tpu_custom_call" | custom-call | tf_op jit(solution)/shard_map/teacher/pallas_call | solution.py:561
  108.8 0.0 all-to-all-done.2
  108.8 19.5 %grad.1 = bf16[128,104,128]{2,1,0:T(8,128)(2,1)} custom-call(s32[1]{0:T(128)} %bitcast.2.offset, f32[128,128]{1,0:T(8,128)S(1)} %bitcast.30, f32[256,128]{1,0:T(8,128)S(1)} %bitcast.29, bf16[2048,768]{1,0:T(8,128)(2,1)} %bitcast.32, bf16[6,256,128]{2,1,0:T(8,128)(2,1)} %get-tuple-element.15.high, bf16[6,256,128]{2,1,0:T(8,128)(2,1)} %get-tuple-element.14.low, ...), custom_call_target="tpu_custom_call" | custom-call | tf_op jit(solution)/shard_map/grad/pallas_call | solution.py:573
  128.4 54.9 %all_to_all.50.returned = bf16[128,104,128]{2,1,0:T(8,128)(2,1)} all-to-all(bf16[128,104,128]{2,1,0:T(8,128)(2,1)} %grad.1), channel_id=1, replica_groups=mesh['corpus'=32,'query'=4] {'corpus','query'}, dimensions={0} | all-to-all | bytes 6815744 | tf_op jit(solution)/shard_map/all_to_all | solution.py:443
  183.2 1.7 book_sum.1
  184.9 3.7 %all-to-all-start.4 = ((f32[128,1,128]{2,1,0:T(1,128)}), f32[128,1,128]{2,1,0:T(1,128)S(1)}, u32[]{:S(2)}, u32[]{:S(2)}) async-start(f32[128,1,128]{2,1,0:T(1,128)} %bitcast.35), calls=%async_computation.4 | async-start | bytes 131072 | tf_op jit(solution)/shard_map/all_to_all | solution.py:443
  188.7 4.8 %combine.1 = bf16[256,768]{1,0:T(8,128)(2,1)} custom-call(bf16[256,2048]{1,0:T(8,128)(2,1)} %get-tuple-element.8.chosen, bf16[128,104,128]{2,1,0:T(8,128)(2,1)} %all_to_all.50.returned), custom_call_target="tpu_custom_call" | custom-call | tf_op jit(solution)/shard_map/combine/pallas_call | solution.py:622
  193.5 5.2 %all-to-all-done.4 = f32[128,1,128]{2,1,0:T(1,128)S(1)} async-done(((f32[128,1,128]{2,1,0:T(1,128)}), f32[128,1,128]{2,1,0:T(1,128)S(1)}, u32[]{:S(2)}, u32[]{:S(2)}) %all-to-all-start.4) | async-done | bytes 65568 | tf_op jit(solution)/shard_map/all_to_all | solution.py:443
  198.7 0.8 book_norm.1
  (6 shorter events, 0.1 us)
Async XLA Ops:
  0.6 16.8 %copy-start = (s32[256,8]{0,1:T(8,128)S(1)}, s32[256,8]{0,1:T(8,128)}, u32[]{:S(2)}) copy-start(s32[256,8]{0,1:T(8,128)} %param.7) | copy-start | bytes 24580
  5.1 11.5 %copy-start.4 = (s32[256,4]{0,1:T(4,128)S(1)}, s32[256,4]{0,1:T(4,128)}, u32[]{:S(2)}) copy-start(s32[256,4]{0,1:T(4,128)} %param.6) | copy-start | bytes 12292
  5.1 12.3 %copy-start.3 = (f32[16,768]{1,0:T(8,128)S(1)}, f32[16,768]{1,0:T(8,128)}, u32[]{:S(2)}) copy-start(f32[16,768]{1,0:T(8,128)} %param.9) | copy-start | bytes 147460
  5.1 53.7 %all-to-all-start = ((bf16[128,16,768]{2,1,0:T(8,128)(2,1)}), bf16[128,16,768]{2,1,0:T(8,128)(2,1)S(1)}, u32[]{:S(2)}, u32[]{:S(2)}) async-start(bf16[128,16,768]{2,1,0:T(8,128)(2,1)} %bitcast.33), calls=%async_computation | async-start | bytes 6291456 | tf_op jit(solution)/shard_map/all_to_all | solution.py:443
  58.8 15.8 %copy-start.1 = (bf16[128,16,768]{2,1,0:T(8,128)(2,1)}, bf16[128,16,768]{2,1,0:T(8,128)(2,1)S(1)}, u32[]{:S(2)}) copy-start(bf16[128,16,768]{2,1,0:T(8,128)(2,1)S(1)} %all-to-all-done) | copy-start | bytes 9437188
  91.9 16.9 %all-to-all-start.2 = ((f32[128,1,128]{2,1,0:T(1,128)}), f32[128,1,128]{2,1,0:T(1,128)S(1)}, u32[]{:S(2)}, u32[]{:S(2)}) async-start(f32[128,1,128]{2,1,0:T(1,128)} %bitcast.34), calls=%async_computation.2 | async-start | bytes 131072 | tf_op jit(solution)/shard_map/all_to_all | solution.py:443
  95.9 1.9 copy-start.2
  184.9 13.7 %all-to-all-start.4 = ((f32[128,1,128]{2,1,0:T(1,128)}), f32[128,1,128]{2,1,0:T(1,128)S(1)}, u32[]{:S(2)}, u32[]{:S(2)}) async-start(f32[128,1,128]{2,1,0:T(1,128)} %bitcast.35), calls=%async_computation.4 | async-start | bytes 131072 | tf_op jit(solution)/shard_map/all_to_all | solution.py:443

commit v9 on v8

--- a/solution.py
+++ b/solution.py
@@ -470,9 +470,9 @@
     sending = pl.pallas_call(
         dispatch_body,
         out_shape=jax.ShapeDtypeStruct((slots, D), BF16),
-        grid=(4,),
+        grid=(2,),
         in_specs=[whole((PROBES, count)), whole((count, D))],
-        out_specs=pl.BlockSpec((slots // 4, D), lambda b: (b, 0)),
+        out_specs=pl.BlockSpec((slots // 2, D), lambda b: (b, 0)),
         name="dispatch",
     )(probes_t, queries)
     got = uncopied(exchange(sending))
@@ -557,7 +557,7 @@
         scratch_shapes=[pltpu.VMEM((SLOTS, devices, count), F32)]
         + [pltpu.VMEM((devices, count), F32)] * 2,
         name="weigh",
-    )(used, message, masks)
+    )(used, message, uncopied(masks))
     teacher = pl.pallas_call(
         teacher_body,
         out_shape=jax.ShapeDtypeStruct((OWN, list_rows, PASSAGES), F32),

time: 200 us -> 200 us (level)
  no operation moved by 1% of the time
where the time goes in v9:
time: 200 us
  blocking collectives  68.9 us (34%)
  Pallas kernels  66 us (33%)
  waiting for transfers between devices  39.1 us (20%)
  starting transfers between devices  19.3 us (10%)
  local copies, waits for them, and re-layouts  4.73 us (2%)
    all_to_all x2, blocking collectives, exchange(): return lax.all_to_all(value, BOTH, 0, 0, tiled=True)  68.9 us
    all_to_all x3, waiting for transfers between devices, exchange(): return lax.all_to_all(value, BOTH, 0, 0, tiled=True)  39.1 us
    pallas_call x1, Pallas kernels, shards(): pl.pallas_call(grad_body, out_shape=jax.ShapeDtypeStruct((devices, CHUNKS...  19.5 us
    all_to_all x3, starting transfers between devices, exchange(): return lax.all_to_all(value, BOTH, 0, 0, tiled=True)  19.3 us
    pallas_call x1, Pallas kernels, shards(): pl.pallas_call(score_body, out_shape=(jax.ShapeDtypeStruct((OWN + 2, list...  15.8 us
    pallas_call x1, Pallas kernels, shards(): pl.pallas_call(teacher_body, out_shape=jax.ShapeDtypeStruct((OWN, list_ro...  6.42 us
    pallas_call x1, Pallas kernels, shards(): pl.pallas_call(home_body, out_shape=(jax.ShapeDtypeStruct((count, slots),...  5.71 us
    pallas_call x1, Pallas kernels, shards(): pl.pallas_call(combine_body, out_shape=jax.ShapeDtypeStruct((count, D), B...  4.75 us
  transfers between devices with their start and end apart: 3, of which 2 were waited for; matrix products, arithmetic and copies ran while one was open for 1% of the time, Pallas kernels for 11%

profile of v9, /device:TPU:1, one launch (start us, length us, event | category | flops | bytes accessed | tf_op | source)
XLA Modules:
  0.0 199.8 jit_solution(11599762364150902846)
XLA Ops:
  0.6 0.0 copy-start
  0.6 3.9 %dispatch.1 = bf16[2048,768]{1,0:T(8,128)(2,1)} custom-call(s32[4,256]{1,0:T(4,128)} %bitcast.39, bf16[256,768]{1,0:T(8,128)(2,1)} %queries.1), custom_call_target="tpu_custom_call" | custom-call | tf_op jit(solution)/shard_map/dispatch/pallas_call | solution.py:470
  4.6 0.0 copy-start.5
  4.6 0.0 copy-start.4
  4.6 11.5 %all-to-all-start = ((bf16[128,16,768]{2,1,0:T(8,128)(2,1)}), bf16[128,16,768]{2,1,0:T(8,128)(2,1)S(1)}, u32[]{:S(2)}, u32[]{:S(2)}) async-start(bf16[128,16,768]{2,1,0:T(8,128)(2,1)} %bitcast.33), calls=%async_computation | async-start | bytes 6291456 | tf_op jit(solution)/shard_map/all_to_all | solution.py:443
  16.1 0.0 copy-done.5
  16.1 0.8 copy.13.probes
  16.9 0.0 copy-done.4
  16.9 0.0 copy-done
  17.0 0.7 copy.14.targets_wide
  17.7 1.0 fusion
  18.8 5.7 %home.1 = (bf16[256,2048]{1,0:T(8,128)(2,1)}, bf16[16,128,256]{2,1,0:T(8,128)(2,1)}, f32[128,128]{1,0:T(8,128)}, s32[16]{0:T(128)}) custom-call(s32[4,256]{1,0:T(4,128)} %bitcast.40, s32[256,4]{1,0:T(8,128)} %copy.13.probes, s32[256,128]{1,0:T(8,128)} %copy.14.targets_wide), custom_call_target="tpu_custom_call" | custom-call | tf_op jit(solution)/shard_map/home/pallas_call | solution.py:484
  24.5 33.8 %all-to-all-done = bf16[128,16,768]{2,1,0:T(8,128)(2,1)S(1)} async-done(((bf16[128,16,768]{2,1,0:T(8,128)(2,1)}), bf16[128,16,768]{2,1,0:T(8,128)(2,1)S(1)}, u32[]{:S(2)}, u32[]{:S(2)}) %all-to-all-start) | async-done | bytes 3145760 | tf_op jit(solution)/shard_map/all_to_all | solution.py:443
  58.3 0.0 copy-start.1
  58.3 15.8 %score.1 = (f32[10,256,1024]{2,1,0:T(8,128)}, f32[256,128]{1,0:T(8,128)}) custom-call(s32[1]{0:T(128)} %bitcast.2.offset, bf16[2048,768]{1,0:T(8,128)(2,1)S(1)} %bitcast.25, bf16[6,256,128]{2,1,0:T(8,128)(2,1)} %get-tuple-element.15.high, bf16[6,256,128]{2,1,0:T(8,128)(2,1)} %get-tuple-element.14.low, f32[128,128]{1,0:T(8,128)} %get-tuple-element.10.notes, ...), custom_call_target="tpu_custom_call" | custom-call | tf_op jit(solution)/shard_map/score/pallas_call | solution.py:515
  74.1 0.0 copy-done.1
  74.1 14.0 %all_to_all.49 = f32[128,2,128]{2,1,0:T(2,128)S(1)} all-to-all(f32[128,2,128]{2,1,0:T(2,128)} %bitcast.37), channel_id=1, replica_groups=mesh['corpus'=32,'query'=4] {'corpus','query'}, dimensions={0} | all-to-all | bytes 262144 | tf_op jit(solution)/shard_map/all_to_all | solution.py:443
  88.1 0.0 copy-start.3
  88.1 1.2 copy-done.3
  89.3 2.7 %weigh.1 = f32[128,128]{1,0:T(8,128)} custom-call(s32[16]{0:T(128)} %get-tuple-element.9.used, f32[256,128]{1,0:T(8,128)S(1)} %bitcast.27, bf16[16,128,256]{2,1,0:T(8,128)(2,1)S(1)} %copy-done.3), custom_call_target="tpu_custom_call" | custom-call | tf_op jit(solution)/shard_map/weigh/pallas_call | solution.py:553
  92.1 4.1 %all-to-all-start.2 = ((f32[128,1,128]{2,1,0:T(1,128)}), f32[128,1,128]{2,1,0:T(1,128)S(1)}, u32[]{:S(2)}, u32[]{:S(2)}) async-start(f32[128,1,128]{2,1,0:T(1,128)} %bitcast.34), calls=%async_computation.2 | async-start | bytes 131072 | tf_op jit(solution)/shard_map/all_to_all | solution.py:443
  96.1 0.0 copy-start.2
  96.2 1.9 copy-done.2
  98.0 4.6 %regroup.1 = bf16[16,128,768]{2,1,0:T(8,128)(2,1)} custom-call(bf16[2048,768]{1,0:T(8,128)(2,1)S(1)} %bitcast.26), custom_call_target="tpu_custom_call" | custom-call | tf_op jit(solution)/shard_map/regroup/pallas_call | solution.py:545
  102.7 6.4 %teacher.1.teacher_odd.teacher_even = f32[8,256,1024]{2,1,0:T(8,128)} custom-call(f32[256,128]{1,0:T(8,128)S(1)} %bitcast.28), custom_call_target="tpu_custom_call" | custom-call | tf_op jit(solution)/shard_map/teacher/pallas_call | solution.py:561
  109.1 0.0 all-to-all-done.2
  109.1 19.5 %grad.1 = bf16[128,104,128]{2,1,0:T(8,128)(2,1)} custom-call(s32[1]{0:T(128)} %bitcast.2.offset, f32[128,128]{1,0:T(8,128)S(1)} %bitcast.30, f32[256,128]{1,0:T(8,128)S(1)} %bitcast.29, bf16[2048,768]{1,0:T(8,128)(2,1)} %bitcast.32, bf16[6,256,128]{2,1,0:T(8,128)(2,1)} %get-tuple-element.15.high, bf16[6,256,128]{2,1,0:T(8,128)(2,1)} %get-tuple-element.14.low, ...), custom_call_target="tpu_custom_call" | custom-call | tf_op jit(solution)/shard_map/grad/pallas_call | solution.py:573
  128.6 54.9 %all_to_all.50.returned = bf16[128,104,128]{2,1,0:T(8,128)(2,1)} all-to-all(bf16[128,104,128]{2,1,0:T(8,128)(2,1)} %grad.1), channel_id=1, replica_groups=mesh['corpus'=32,'query'=4] {'corpus','query'}, dimensions={0} | all-to-all | bytes 6815744 | tf_op jit(solution)/shard_map/all_to_all | solution.py:443
  183.5 1.7 book_sum.1
  185.2 3.8 %all-to-all-start.4 = ((f32[128,1,128]{2,1,0:T(1,128)}), f32[128,1,128]{2,1,0:T(1,128)S(1)}, u32[]{:S(2)}, u32[]{:S(2)}) async-start(f32[128,1,128]{2,1,0:T(1,128)} %bitcast.35), calls=%async_computation.4 | async-start | bytes 131072 | tf_op jit(solution)/shard_map/all_to_all | solution.py:443
  189.0 4.8 %combine.1 = bf16[256,768]{1,0:T(8,128)(2,1)} custom-call(bf16[256,2048]{1,0:T(8,128)(2,1)} %get-tuple-element.8.chosen, bf16[128,104,128]{2,1,0:T(8,128)(2,1)} %all_to_all.50.returned), custom_call_target="tpu_custom_call" | custom-call | tf_op jit(solution)/shard_map/combine/pallas_call | solution.py:622
  193.8 5.3 %all-to-all-done.4 = f32[128,1,128]{2,1,0:T(1,128)S(1)} async-done(((f32[128,1,128]{2,1,0:T(1,128)}), f32[128,1,128]{2,1,0:T(1,128)S(1)}, u32[]{:S(2)}, u32[]{:S(2)}) %all-to-all-start.4) | async-done | bytes 65568 | tf_op jit(solution)/shard_map/all_to_all | solution.py:443
  199.1 0.8 book_norm.1
  (6 shorter events, 0.1 us)
Async XLA Ops:
  0.6 16.3 %copy-start = (s32[256,8]{0,1:T(8,128)S(1)}, s32[256,8]{0,1:T(8,128)}, u32[]{:S(2)}) copy-start(s32[256,8]{0,1:T(8,128)} %param.7) | copy-start | bytes 24580
  4.6 11.5 %copy-start.5 = (s32[256,4]{0,1:T(4,128)S(1)}, s32[256,4]{0,1:T(4,128)}, u32[]{:S(2)}) copy-start(s32[256,4]{0,1:T(4,128)} %param.6) | copy-start | bytes 12292
  4.6 12.3 %copy-start.4 = (f32[16,768]{1,0:T(8,128)S(1)}, f32[16,768]{1,0:T(8,128)}, u32[]{:S(2)}) copy-start(f32[16,768]{1,0:T(8,128)} %param.9) | copy-start | bytes 147460
  4.6 53.7 %all-to-all-start = ((bf16[128,16,768]{2,1,0:T(8,128)(2,1)}), bf16[128,16,768]{2,1,0:T(8,128)(2,1)S(1)}, u32[]{:S(2)}, u32[]{:S(2)}) async-start(bf16[128,16,768]{2,1,0:T(8,128)(2,1)} %bitcast.33), calls=%async_computation | async-start | bytes 6291456 | tf_op jit(solution)/shard_map/all_to_all | solution.py:443
  58.3 15.9 %copy-start.1 = (bf16[128,16,768]{2,1,0:T(8,128)(2,1)}, bf16[128,16,768]{2,1,0:T(8,128)(2,1)S(1)}, u32[]{:S(2)}) copy-start(bf16[128,16,768]{2,1,0:T(8,128)(2,1)S(1)} %all-to-all-done) | copy-start | bytes 9437188
  88.1 1.2 copy-start.3
  92.1 17.0 %all-to-all-start.2 = ((f32[128,1,128]{2,1,0:T(1,128)}), f32[128,1,128]{2,1,0:T(1,128)S(1)}, u32[]{:S(2)}, u32[]{:S(2)}) async-start(f32[128,1,128]{2,1,0:T(1,128)} %bitcast.34), calls=%async_computation.2 | async-start | bytes 131072 | tf_op jit(solution)/shard_map/all_to_all | solution.py:443
  96.1 1.9 copy-start.2
  185.2 13.8 %all-to-all-start.4 = ((f32[128,1,128]{2,1,0:T(1,128)}), f32[128,1,128]{2,1,0:T(1,128)S(1)}, u32[]{:S(2)}, u32[]{:S(2)}) async-start(f32[128,1,128]{2,1,0:T(1,128)} %bitcast.35), calls=%async_computation.4 | async-start | bytes 131072 | tf_op jit(solution)/shard_map/all_to_all | solution.py:443
